TPU v7x, 32 devices: a whole 2x2x4 slice. The times are simulated.
32 devices in a mesh: ctx: 4 (over y, x), vis: 8 (over z, core).
Axes of the slice: x: 2, y: 2, z: 4, core: 2. Of those that a mesh axis runs over, the one named last changes fastest.
Arguments:
- patches: bfloat16 [4096, 1280], P(('ctx', 'vis')), may hold values from -10 to 10
- vis_gain: float32 [1280], replicated, may hold values from 0.5 to 1.5
- w_qkv: bfloat16 [1280, 3840], P(None, 'vis'), may hold values from -2 to 2
- w_out: bfloat16 [1280, 1280], P('vis'), may hold values from -0.15625 to 0.15625
- merge_gain: float32 [1280], replicated, may hold values from 0.5 to 1.5
- w_merge: bfloat16 [5120, 8192], P(None, 'vis'), may hold values from -0.078125 to 0.078125
- token_dest: int32 [4, 256], replicated, may hold values from 0 to 3, as said below
- token_row: int32 [4, 256], replicated, may hold values from 0 to 1023, as said below
- prompt_text: bfloat16 [4096, 8192], P('ctx', 'vis'), may hold values from -6 to 6
- kv_gain: float32 [8192], P('vis'), may hold values from 0.5 to 1.5
- w_kv: bfloat16 [8192, 1024], P('vis'), may hold values from -1 to 1
- queries: bfloat16 [512, 4096], P('ctx'), may hold values from -12 to 12
- resp_kv: bfloat16 [512, 1024], P('ctx'), may hold values from -12 to 12
- resp_len: int32 [4], P('ctx'), may hold values from 64 to 128
Outputs:
- attended: bfloat16 [512, 4096], P('ctx')
Inputs may be any that keep to these rules, and one draw needn't show every extreme that they name: `token_dest`: the tokens of one image are in order of their prompt shard; at most 96 tokens of one image go to one shard, and from every image exactly 96 go to some shard. `token_row`: no two visual tokens take the same position of one shard.
All inputs are finite; a program needn't handle non-finite values.
Results may differ from a plain program's by a relative error of at most 0.014.
Values may be sent and summed in bfloat16 or wider, within the bound.
A program may use at most 128 MiB of HBM per device.

v0:
```python
import functools
import math

import jax
import jax.numpy as jnp
from jax import lax
from jax.experimental import pallas as pl
from jax.experimental.pallas import tpu as pltpu
from jax.sharding import Mesh, PartitionSpec as P

VD = 1280
VHEADS = 16
D = 8192
HD = 128
QH = 32
KVH = 4
VHD = 80
MD = 5120


EPS = 1e-06
VIS = ("vk", "vh", "core")
SUB = ("vh", "core")
MESH = pl.DeviceIdType.MESH
VMEM = pl.BlockSpec(memory_space=pltpu.VMEM)
F32 = jnp.float32
BF16 = jnp.bfloat16


def layer_norm(values, gain):
    center = values - jnp.mean(values, axis=-1, keepdims=True)
    spread = jnp.mean(center * center, axis=-1, keepdims=True)
    return center * lax.rsqrt(spread + EPS) * gain


def vision_attention(qkv, local_heads):
    scale = 1.0 / math.sqrt(VHD)
    outs = []
    for h in range(local_heads):
        base = h * 3 * VHD
        query = qkv[:, base : base + VHD]
        keys = qkv[:, base + VHD : base + 2 * VHD]
        values = qkv[:, base + 2 * VHD : base + 3 * VHD]
        scores = jnp.einsum("qd,kd->qk", query, keys, preferred_element_type=F32) * scale
        expo = jnp.exp(scores - jnp.max(scores, axis=1, keepdims=True))
        summed = jnp.sum(expo, axis=1, keepdims=True)
        mixed = jnp.einsum("qk,kd->dq", expo.astype(BF16), values, preferred_element_type=F32)
        outs.append((mixed / summed.reshape(1, -1)).astype(BF16))
    return jnp.concatenate(outs, axis=0)


def flat_index(names, sizes):
    index = 0
    for name, size in zip(names, sizes):
        index = index * size + lax.axis_index(name)
    return index


def coordinates(index, names, sizes):
    place = {}
    for name, size in reversed(list(zip(names, sizes))):
        place[name] = index % size
        index = index // size
    return place


def exchange_kernel(names, sizes, spread, count, *refs):
    xs, outs = refs[:count], refs[count : 2 * count]
    send_sem, recv_sem, local_sem = refs[2 * count :]
    total = math.prod(sizes)
    me = flat_index(names, sizes)
    barrier = pltpu.get_barrier_semaphore()
    for step in range(1, total):
        pl.semaphore_signal(
            barrier,
            inc=1,
            device_id=coordinates((me + step) % total, names, sizes),
            device_id_type=MESH,
        )
    pl.semaphore_wait(barrier, total - 1)
    copies = []
    for step in range(1, total):
        target = (me + step) % total
        for i in range(count):
            copy = pltpu.make_async_remote_copy(
                src_ref=xs[i] if spread else xs[i].at[target],
                dst_ref=outs[i].at[me],
                send_sem=send_sem.at[i, step],
                recv_sem=recv_sem.at[i, step],
                device_id=coordinates(target, names, sizes),
                device_id_type=MESH,
            )
            copy.start()
            copies.append(copy)
    for i in range(count):
        own = pltpu.make_async_copy(
            xs[i] if spread else xs[i].at[me], outs[i].at[me], local_sem.at[i]
        )
        own.start()
        copies.append(own)
    for copy in copies:
        copy.wait()


def exchange(xs, names, spread, collective_id):
    sizes = tuple(lax.axis_size(name) for name in names)
    total, count = math.prod(sizes), len(xs)
    shapes = [((total,) + x.shape) if spread else x.shape for x in xs]
    return pl.pallas_call(
        functools.partial(exchange_kernel, names, sizes, spread, count),
        out_shape=[jax.ShapeDtypeStruct(sh, x.dtype) for sh, x in zip(shapes, xs)],
        in_specs=[VMEM] * count,
        out_specs=[VMEM] * count,
        scratch_shapes=[
            pltpu.SemaphoreType.DMA((count, total)),
            pltpu.SemaphoreType.DMA((count, total)),
            pltpu.SemaphoreType.DMA((count,)),
        ],
        compiler_params=pltpu.CompilerParams(
            collective_id=collective_id, has_side_effects=True
        ),
        cost_estimate=pl.CostEstimate(flops=0, bytes_accessed=30_000_000, transcendentals=0),
    )(*xs)


def line_kernel(sizes, chunks, x_ref, out_ref, send_sem, recv_sem, share_send, share_recv, local_sem):
    chips = sizes[0] * sizes[1]
    core = lax.axis_index("core")
    chip = lax.axis_index("vk") * sizes[1] + lax.axis_index("vh")
    rows = x_ref.shape[0] // chunks

    def at(where, which):
        return {"vk": where // sizes[1], "vh": where % sizes[1], "core": which}

    def neighbour(direction):
        return chip + 1 if direction == 0 else chip - 1

    def has(direction):
        return chip < chips - 1 if direction == 0 else chip > 0

    barrier = pltpu.get_barrier_semaphore()
    pl.semaphore_signal(barrier, inc=1, device_id=at(chip, 1 - core), device_id_type=MESH)
    for direction in range(2):
        @pl.when(has(direction))
        def _():
            pl.semaphore_signal(
                barrier, inc=1, device_id=at(neighbour(direction), core), device_id_type=MESH
            )
    pl.semaphore_wait(barrier, 1 + jnp.where(has(0), 1, 0) + jnp.where(has(1), 1, 0))

    def slot(origin, which, piece):
        return out_ref.at[origin * 2 + which, pl.ds(piece * rows, rows)]

    def source(origin, piece, hop):
        return x_ref.at[pl.ds(piece * rows, rows)] if hop == 0 else slot(origin, core, piece)

    def origin_of(direction, hop):
        return chip - hop if direction == 0 else chip + hop

    def exists(direction, hop):
        return chip >= hop if direction == 0 else chip + hop < chips

    def pass_on(direction, hop, piece):
        origin = origin_of(direction, hop)
        return pltpu.make_async_remote_copy(
            src_ref=source(origin, piece, hop),
            dst_ref=slot(origin, core, piece),
            send_sem=send_sem.at[direction, hop, piece],
            recv_sem=recv_sem.at[direction, hop, piece],
            device_id=at(neighbour(direction), core),
            device_id_type=MESH,
        )

    def arrival(direction, hop, piece):
        origin = origin_of(direction, hop)
        return pltpu.make_async_remote_copy(
            src_ref=slot(origin, core, piece),
            dst_ref=slot(origin, core, piece),
            send_sem=send_sem.at[direction, hop - 1, piece],
            recv_sem=recv_sem.at[direction, hop - 1, piece],
            device_id=at(chip, 1 - core),
            device_id_type=MESH,
        )

    def share(origin, piece, hop):
        return pltpu.make_async_remote_copy(
            src_ref=source(origin, piece, hop),
            dst_ref=slot(origin, core, piece),
            send_sem=share_send.at[origin, piece],
            recv_sem=share_recv.at[origin, piece],
            device_id=at(chip, 1 - core),
            device_id_type=MESH,
        )

    for piece in range(chunks):
        for direction in range(2):
            @pl.when(has(direction))
            def _():
                pass_on(direction, 0, piece).start()
    own = pltpu.make_async_copy(x_ref, out_ref.at[chip * 2 + core], local_sem)
    own.start()
    for piece in range(chunks):
        share(chip, piece, 0).start()
    for hop in range(1, chips):
        for piece in range(chunks):
            for direction in range(2):
                @pl.when(exists(direction, hop))
                def _():
                    arrival(direction, hop, piece).wait_recv()
                    if hop < chips - 1:
                        @pl.when(has(direction))
                        def _():
                            pass_on(direction, hop, piece).start()
                    share(origin_of(direction, hop), piece, hop).start()
    own.wait()
    for piece in range(chunks):
        share(chip, piece, 0).wait_send()
        for direction in range(2):
            for hop in range(chips):
                if hop < chips - 1:
                    @pl.when(jnp.logical_and(exists(direction, hop), has(direction)))
                    def _():
                        pass_on(direction, hop, piece).wait_send()
                if hop > 0:
                    @pl.when(exists(direction, hop))
                    def _():
                        share(origin_of(direction, hop), piece, hop).wait_send()
        for origin in range(chips):
            pltpu.make_async_remote_copy(
                src_ref=slot(origin, 1 - core, piece),
                dst_ref=slot(origin, 1 - core, piece),
                send_sem=share_send.at[origin, piece],
                recv_sem=share_recv.at[origin, piece],
                device_id=at(chip, 1 - core),
                device_id_type=MESH,
            ).wait_recv()


def line_gather(x, chunks, collective_id):
    sizes = tuple(lax.axis_size(name) for name in VIS)
    chips = sizes[0] * sizes[1]
    return pl.pallas_call(
        functools.partial(line_kernel, sizes, chunks),
        out_shape=jax.ShapeDtypeStruct((2 * chips,) + x.shape, x.dtype),
        in_specs=[VMEM],
        out_specs=VMEM,
        scratch_shapes=[
            pltpu.SemaphoreType.DMA((2, chips, chunks)),
            pltpu.SemaphoreType.DMA((2, chips, chunks)),
            pltpu.SemaphoreType.DMA((chips, chunks)),
            pltpu.SemaphoreType.DMA((chips, chunks)),
            pltpu.SemaphoreType.DMA,
        ],
        compiler_params=pltpu.CompilerParams(
            collective_id=collective_id, has_side_effects=True
        ),
        cost_estimate=pl.CostEstimate(flops=0, bytes_accessed=70_000_000, transcendentals=0),
    )(x)


def project_kernel(joined, rows_ref, weight_ref, out_ref, *rest):
    each = rows_ref.shape[0]
    rows = rows_ref[...]
    floats = rows.astype(F32)
    squares = floats * floats
    coarse = squares.astype(BF16)
    fine = (squares - coarse.astype(F32)).astype(BF16)
    ones = jnp.ones((8, rows.shape[1]), BF16)
    dims = (((1,), (1,)), ((), ()))
    sums = lax.dot_general(ones, coarse, dims, preferred_element_type=F32)
    sums += lax.dot_general(ones, fine, dims, preferred_element_type=F32)
    for half in range(2):
        for pair in range(KVH // 2):
            first = (half * KVH + pair * 2) * HD
            raw = jnp.dot(
                rows, weight_ref[:, first : first + 2 * HD], preferred_element_type=F32
            ).astype(out_ref.dtype)
            for i in range(2):
                out_ref[pair * 2 + i, 0, :each, half * HD : (half + 1) * HD] = raw[
                    :, i * HD : (i + 1) * HD
                ]
    for h in range(KVH):
        if joined:
            out_ref[h, 0, each:, :] = sums[:, : 2 * HD]
            for part in range(1, each // (2 * HD)):
                out_ref[h, 0, each + part : each + part + 1, :] = sums[
                    :1, part * 2 * HD : (part + 1) * 2 * HD
                ]
        else:
            rest[0][h, 0] = sums


def project(rows, weight, parts, joined):
    count, depth = rows.shape
    each = count // parts
    if joined:
        shapes = [jax.ShapeDtypeStruct((KVH, parts, each + 8, 2 * HD), F32)]
    else:
        shapes = [
            jax.ShapeDtypeStruct((KVH, parts, each, 2 * HD), BF16),
            jax.ShapeDtypeStruct((KVH, parts, 8, each), F32),
        ]
    outs = pl.pallas_call(
        functools.partial(project_kernel, joined),
        grid=(parts,),
        out_shape=shapes,
        in_specs=[
            pl.BlockSpec((each, depth), lambda p: (p, 0)),
            pl.BlockSpec(weight.shape, lambda p: (0, 0)),
        ],
        out_specs=[
            pl.BlockSpec((KVH, 1) + shape.shape[2:], lambda p: (0, p, 0, 0)) for shape in shapes
        ],
        cost_estimate=pl.CostEstimate(
            flops=2 * count * depth * KVH * 2 * HD,
            bytes_accessed=count * depth * 10,
            transcendentals=0,
        ),
    )(rows, weight)
    return [out.reshape((KVH * parts,) + out.shape[2:]) for out in outs]


def whole_text(total):
    total = total[0]
    each = total.shape[0] - 8
    squares = total[each : each + each // (2 * HD)].reshape(each)
    inverse = lax.rsqrt(squares / D + EPS)
    share = (total[:each] * inverse[:, None]).astype(BF16)
    return lax.all_gather(share, ("ctx",) + SUB, axis=0, tiled=True)


def whole_image(visual, weight, parts):
    pieces, squares = project(visual, weight, parts, False)
    pieces, squares = exchange((pieces, squares), VIS, False, 3)
    total = jnp.sum(pieces.astype(F32), axis=0)
    inverse = lax.rsqrt(jnp.sum(squares[:, 0, :], axis=0) / D + EPS)
    share = (total * inverse[:, None]).astype(BF16)
    (whole,) = exchange((share,), ("ctx",) + SUB, True, 4)
    return whole.reshape(-1, 2 * HD)


def per_device(
    patches,
    vis_gain,
    w_qkv,
    w_out,
    merge_gain,
    w_merge,
    token_dest,
    token_row,
    prompt_text,
    kv_gain,
    w_kv,
    queries,
    resp_kv,
    resp_len,
):
    parts = lax.axis_size("vh") * lax.axis_size("core")
    vis_count = lax.axis_size("vk") * parts
    ctx_count = lax.axis_size("ctx")
    vis_index = flat_index(VIS, tuple(lax.axis_size(name) for name in VIS))
    patch_count = patches.shape[0]
    shard_rows = prompt_text.shape[0]
    local_heads = VHEADS // vis_count

    floats = patches.astype(F32)
    normed = layer_norm(floats, vis_gain).astype(BF16)
    gathered = line_gather(normed, 2, 0).reshape(-1, VD)
    few = w_out.shape[0] // ctx_count
    w_out_all = lax.all_gather(
        lax.dynamic_slice_in_dim(w_out, lax.axis_index("ctx") * few, few, 0),
        ("ctx",) + VIS,
        axis=0,
        tiled=True,
    )

    weight = (w_kv.astype(F32) * kv_gain[:, None]).astype(BF16)

    qkv = jnp.dot(gathered, w_qkv, preferred_element_type=F32).astype(BF16)
    heads = vision_attention(qkv, local_heads)
    heads = heads.reshape(-1, vis_count, patch_count).transpose(1, 0, 2)
    (returned,) = exchange((heads,), VIS, False, 1)
    weight, returned, w_out_all = lax.optimization_barrier((weight, returned, w_out_all))
    text_total = lax.psum_scatter(
        project(prompt_text, weight, parts, True)[0], VIS, scatter_dimension=0, tiled=True
    )
    returned = returned.reshape(vis_count, ctx_count, few, patch_count).transpose(1, 0, 2, 3)
    projected = jnp.einsum(
        "dp,de->pe", returned.reshape(VD, patch_count), w_out_all, preferred_element_type=F32
    )
    mixed = floats + projected
    merged = layer_norm(mixed, merge_gain).astype(BF16).reshape(patch_count // 4, MD)
    merged = line_gather(merged, 2, 2).reshape(-1, MD)
    visual = jnp.dot(merged, w_merge, preferred_element_type=F32).astype(BF16)
    visual, text_total = lax.optimization_barrier((visual, text_total))
    text_kv = whole_text(text_total)
    image_kv = whole_image(visual, weight, parts)

    flat = (token_dest * shard_rows + token_row).reshape(-1)
    positions = jnp.arange(ctx_count * shard_rows, dtype=jnp.int32)
    taken = jnp.any(positions[:, None] == flat[None, :], axis=1)

    width = KVH * HD
    group = QH // KVH
    mine = QH // vis_count
    resp_rows = queries.shape[0]
    scale = 1.0 / math.sqrt(HD)
    query = lax.dynamic_slice_in_dim(queries, vis_index * mine * HD, mine * HD, 1)
    query = query.reshape(resp_rows, mine, HD).transpose(1, 0, 2).reshape(mine * resp_rows, HD)
    kv_head = (vis_index * mine) // group
    own_keys = lax.dynamic_slice_in_dim(resp_kv, kv_head * HD, HD, 1)
    own_values = lax.dynamic_slice_in_dim(resp_kv, width + kv_head * HD, HD, 1)
    early_keys = jnp.concatenate([text_kv[:, :HD], own_keys], axis=0)
    early_values = jnp.concatenate([text_kv[:, HD:], own_values], axis=0)
    query_positions = jnp.arange(resp_rows, dtype=jnp.int32)
    causal = query_positions[None, :] <= query_positions[:, None]
    visible = jnp.concatenate(
        [jnp.broadcast_to(~taken[None, :], (resp_rows, taken.shape[0])), causal], axis=1
    )
    visible = jnp.broadcast_to(visible[None], (mine,) + visible.shape).reshape(
        mine * resp_rows, -1
    )

    def scores_of(keys):
        return jnp.einsum("qd,kd->qk", query, keys, preferred_element_type=F32) * scale

    scores = jnp.where(visible, scores_of(early_keys), -1e30)
    early_high = jnp.max(scores, axis=1, keepdims=True)
    expo = jnp.where(visible, jnp.exp(scores - early_high), 0.0)
    early_sum = jnp.sum(expo, axis=1, keepdims=True)
    early_mix = jnp.dot(expo.astype(BF16), early_values, preferred_element_type=F32)

    late_scores = scores_of(image_kv[:, :HD])
    high = jnp.maximum(early_high, jnp.max(late_scores, axis=1, keepdims=True))
    late = jnp.exp(late_scores - high)
    fade = jnp.exp(early_high - high)
    summed = early_sum * fade + jnp.sum(late, axis=1, keepdims=True)
    mix = early_mix * fade + jnp.dot(
        late.astype(BF16), image_kv[:, HD:], preferred_element_type=F32
    )
    live = jnp.tile(query_positions < resp_len[0], mine)[:, None]
    result = jnp.where(live, mix / summed, 0.0).astype(BF16)
    result = result.reshape(mine, resp_rows, HD).transpose(1, 0, 2)
    whole = line_gather(result.reshape(resp_rows, mine * HD), 2, 5)
    return whole.transpose(1, 0, 2).reshape(resp_rows, QH * HD)


def solution(mesh):
    ctx_count, vis_count = mesh.shape["ctx"], mesh.shape["vis"]
    parts = vis_count // KVH
    shape = (ctx_count, vis_count // parts, parts // 2, 2)
    fine = Mesh(mesh.devices.reshape(shape), ("ctx",) + VIS)
    return jax.shard_map(
        per_device,
        mesh=fine,
        in_specs=(
            P(("ctx",) + VIS, None),
            P(),
            P(None, VIS),
            P(VIS, None),
            P(),
            P(None, VIS),
            P(),
            P(),
            P("ctx", VIS),
            P(VIS),
            P(VIS, None),
            P("ctx", None),
            P("ctx", None),
            P("ctx"),
        ),
        out_specs=P("ctx", None),
        check_vma=False,
    )
```

profile of v0, /device:TPU:0, one launch (start us, length us, event | category | flops | bytes accessed | tf_op | source)
XLA Modules:
  0.0 231.9 jit_solution(11086953934012513014)
XLA Ops:
  6.5 1.6 constant_dynamic-slice_fusion.2
  8.2 1.1 convert_reduce_fusion.1
  9.4 1.2 fusion.39
  10.6 1.9 fusion.41.x_ref
  12.5 33.7 %shard_map.136 = bf16[8,128,1280]{2,1,0:T(8,128)(2,1)} custom-call(bf16[128,1280]{1,0:T(8,128)(2,1)} %fusion.41.x_ref), custom_call_target="tpu_custom_call" | custom-call | bytes 70000000 | tf_op jit(solution)/shard_map/pallas_call | solution.py:242
  46.2 3.2 %convolution_convert_fusion = bf16[1024,480]{0,1:T(8,128)(2,1)S(1)} fusion(bf16[1024,1280]{1,0:T(8,128)(2,1)} %bitcast.62, bf16[1280,480]{0,1:T(8,128)(2,1)S(1)} %copy-done), kind=kOutput, calls=%fused_computation.23 | convolution fusion | flops 1258782720 | bytes 4833280 | tf_op jit(solution)/shard_map/dot_general | solution.py:379
  49.4 0.8 multiply_reduce_fusion.1
  50.2 0.7 fusion.3
  50.9 0.8 multiply_reduce_fusion
  51.7 0.7 fusion.5
  52.4 0.8 fusion.24
  53.3 0.8 fusion.21
  54.1 0.8 bitcast_bitcast_fusion.refs_0_
  54.9 13.7 %shard_map.137 = bf16[8,160,128]{2,1,0:T(8,128)(2,1)} custom-call(bf16[8,160,128]{2,1,0:T(8,128)(2,1)} %bitcast_bitcast_fusion.refs_0_), custom_call_target="tpu_custom_call" | custom-call | bytes 30000000 | tf_op jit(solution)/shard_map/pallas_call | solution.py:109
  68.6 1.8 multiply_convert_fusion.weight_ref
  70.4 6.0 %all-gather.3.cloned.1.call-done = bf16[1280,1280]{1,0:T(8,128)(2,1)} async-done(((bf16[40,1280]{1,0:T(8,128)(2,1)}), bf16[1280,1280]{1,0:T(8,128)(2,1)}) %all-gather.3.cloned.1.call-update) | async-done | bytes 3276816 | tf_op jit(solution)/shard_map/all_gather | solution.py:370
  76.4 7.0 %shard_map.139 = f32[4,2,520,256]{3,2,1,0:T(8,128)} custom-call(bf16[1024,1024]{1,0:T(8,128)(2,1)} %rows_ref.1, bf16[1024,1024]{1,0:T(8,128)(2,1)} %multiply_convert_fusion.weight_ref), custom_call_target="tpu_custom_call" | custom-call | flops 2147483648 | bytes 10485760 | tf_op jit(solution)/shard_map/pallas_call | solution.py:303
  83.5 0.9 copy-done.4
  84.4 2.6 %fusion.60 = (f32[128]{0:T(128)S(1)}, f32[128,1280]{1,0:T(8,128)S(1)}) fusion(bf16[1280,128]{1,0:T(8,128)(2,1)S(1)} %bitcast.64, bf16[1280,1280]{1,0:T(8,128)(2,1)} %all-gather.3.cloned.1.call-done, bf16[128,1280]{1,0:T(8,128)(2,1)S(1)} %copy-done.2), kind=kOutput, calls=%fused_computation.92 | convolution fusion | flops 419921792 | bytes 4588032 | tf_op jit(solution)/shard_map/dp,de->pe/dot_general | solution.py:388
  87.1 0.2 multiply_reduce_fusion.3
  87.3 0.2 multiply_convert_fusion.1
  87.5 0.9 reshape.145.x_ref
  88.4 53.8 %shard_map.138 = bf16[8,32,5120]{2,1,0:T(8,128)(2,1)} custom-call(bf16[32,5120]{1,0:T(8,128)(2,1)} %reshape.145.x_ref), custom_call_target="tpu_custom_call" | custom-call | bytes 70000000 | tf_op jit(solution)/shard_map/pallas_call | solution.py:242
  142.3 8.6 %convolution_convert_fusion.1.rows_ref = bf16[256,1024]{1,0:T(8,128)(2,1)} fusion(bf16[256,5120]{1,0:T(8,128)(2,1)} %bitcast.63, bf16[5120,1024]{1,0:T(8,128)(2,1)} %param.19), kind=kOutput, calls=%fused_computation.24 | convolution fusion | flops 2684616704 | bytes 13631488 | tf_op jit(solution)/shard_map/dot_general | solution.py:394
  150.8 1.8 reduce-scatter.2.cloned.1.call-done
  152.6 0.7 rsqrt_bitcast_fusion
  153.3 1.9 fusion.42
  156.0 2.0 fusion
  157.9 0.9 constant_dynamic-slice_fusion.3
  159.2 0.8 constant_dynamic-slice_fusion
  160.0 0.1 pad_add_fusion
  160.2 3.6 %shard_map.140 = (bf16[4,2,128,256]{3,2,1,0:T(8,128)(2,1)}, f32[4,2,8,128]{3,2,1,0:T(8,128)}) custom-call(bf16[256,1024]{1,0:T(8,128)(2,1)} %convolution_convert_fusion.1.rows_ref, bf16[1024,1024]{1,0:T(8,128)(2,1)} %multiply_convert_fusion.weight_ref), custom_call_target="tpu_custom_call" | custom-call | flops 536870912 | bytes 2621440 | tf_op jit(solution)/shard_map/pallas_call | solution.py:303
  163.7 15.0 %shard_map.141 = (bf16[8,128,256]{2,1,0:T(8,128)(2,1)}, f32[8,8,128]{2,1,0:T(8,128)}) custom-call(bf16[8,128,256]{2,1,0:T(8,128)(2,1)} %bitcast.71, f32[8,8,128]{2,1,0:T(8,128)} %bitcast.75), custom_call_target="tpu_custom_call" | custom-call | bytes 30000000 | tf_op jit(solution)/shard_map/pallas_call | solution.py:109
  178.7 0.8 slice_reduce_fusion
  179.5 1.1 convert_reduce_fusion
  180.6 0.7 multiply_convert_fusion.2.refs_0_
  181.3 11.5 %shard_map.142 = bf16[8,128,256]{2,1,0:T(8,128)(2,1)} custom-call(bf16[128,256]{1,0:T(8,128)(2,1)} %multiply_convert_fusion.2.refs_0_), custom_call_target="tpu_custom_call" | custom-call | bytes 30000000 | tf_op jit(solution)/shard_map/pallas_call | solution.py:109
  192.8 1.5 multiply_reduce_fusion.2
  194.3 1.7 fusion.59
  196.0 2.0 fusion.61
  198.0 2.8 %fusion.1 = (f32[512]{0:T(512)S(1)}, bf16[512,4224]{1,0:T(8,128)(2,1)S(1)}) fusion(f32[512,4224]{1,0:T(8,128)S(1)} %get-tuple-element.38, f32[512]{0:T(512)S(1)} %get-tuple-element.37, pred[128,4224]{1,0:T(8,128)(4,1)S(1)} %pad_add_fusion), kind=kLoop, calls=%fused_computation.4 | loop fusion | flops 8650240 | bytes 13520896 | tf_op jit(solution)/shard_map/reduce_sum | solution.py:430
  200.8 0.5 fusion.11
  201.3 1.3 convolution_multiply_fusion
  202.6 0.6 fusion.27
  203.3 0.7 copy.42
  204.0 18.5 %shard_map.143 = bf16[8,128,512]{2,1,0:T(8,128)(2,1)} custom-call(bf16[128,512]{1,0:T(8,128)(2,1)} %bitcast.70), custom_call_target="tpu_custom_call" | custom-call | bytes 70000000 | tf_op jit(solution)/shard_map/pallas_call | solution.py:242
  222.5 1.6 copy.33
  224.1 1.3 copy.34
  (45 shorter events, 0.8 us)
Async XLA Ops:
  6.5 39.6 %copy-start = (bf16[1280,480]{0,1:T(8,128)(2,1)S(1)}, bf16[1280,480]{0,1:T(8,128)(2,1)}, u32[]{:S(2)}) copy-start(bf16[1280,480]{0,1:T(8,128)(2,1)} %param.16) | copy-start | bytes 3686404
  6.5 69.9 %all-gather.3.cloned.1.call-start = ((), (), s32[]{:S(2)}) async-start(), calls=%async_computation.1 | async-start | bytes 3379200 | tf_op jit(solution)/shard_map/all_gather | solution.py:370
  8.2 144.4 %reduce-scatter.2.cloned.1.call-start = ((), (), s32[]{:S(2)}) async-start(), calls=%async_computation.2 | async-start | bytes 4792320 | tf_op jit(solution)/shard_map/reduce_scatter | solution.py:384
  53.3 15.3 %copy-start.3 = (bf16[1024,1024]{1,0:T(8,128)(2,1)S(1)}, bf16[1024,1024]{1,0:T(8,128)(2,1)}, u32[]{:S(2)}) copy-start(bf16[1024,1024]{1,0:T(8,128)(2,1)} %param.24) | copy-start | bytes 6291460
  53.3 15.3 %copy-start.7 = (f32[1024]{0:T(1024)S(1)}, f32[1024]{0:T(1024)}, u32[]{:S(2)}) copy-start(f32[1024]{0:T(1024)} %param.23) | copy-start | bytes 12292
  83.4 1.0 copy-start.4
  83.4 1.1 copy-start.2
  83.4 4.0 %copy-start.6 = (f32[1280]{0:T(1024)S(1)}, f32[1280]{0:T(1024)}, u32[]{:S(2)}) copy-start(f32[1280]{0:T(1024)} %param.18) | copy-start | bytes 15364
  83.4 110.9 %all-gather.5.cloned.1.call-start = ((), (), s32[]{:S(2)}) async-start(), calls=%async_computation.3 | async-start | bytes 2359296 | tf_op jit(solution)/shard_map/all_gather | solution.py:329
  142.3 13.7 %copy-start.8 = (s32[4,256]{1,0:T(4,128)S(1)}, s32[4,256]{1,0:T(4,128)}, u32[]{:S(2)}) copy-start(s32[4,256]{1,0:T(4,128)} %param.21) | copy-start | bytes 12292
  142.3 13.7 %copy-start.9 = (s32[4,256]{1,0:T(4,128)S(1)}, s32[4,256]{1,0:T(4,128)}, u32[]{:S(2)}) copy-start(s32[4,256]{1,0:T(4,128)} %param.20) | copy-start | bytes 12292
  200.8 1.8 copy-start.5
  202.6 22.8 %copy-start.1 = (bf16[1280,480]{0,1:T(8,128)(2,1)S(1)}, bf16[1280,480]{0,1:T(8,128)(2,1)}, u32[]{:S(2)}) copy-start(bf16[1280,480]{0,1:T(8,128)(2,1)} %param.16) | copy-start | bytes 3686404
Sparse Core Ops, SparseCore 0:
  10.2 66.1 all-gather.2
  83.5 69.0 reduce-scatter.1
  155.4 28.4 all-gather.4
where the time goes:
time: 233 us; the launch traced here: 232 us
  Pallas kernels  157 us (67%)
  matrix products  22.9 us (10%)
  other arithmetic  19.4 us (8%)
  between operations  14.1 us (6%)
  local copies, waits for them, and re-layouts  11 us (5%)
  waiting for transfers between devices  7.82 us (3%)
    pallas_call x3, Pallas kernels, line_gather(): pl.pallas_call(functools.partial(line_kernel, sizes, chunks), out_shape=j...  106 us
    pallas_call x3, Pallas kernels, exchange(): pl.pallas_call(functools.partial(exchange_kernel, names, sizes, spread, c...  40.1 us
    pallas_call x2, Pallas kernels, project(): pl.pallas_call(functools.partial(project_kernel, joined), grid=(parts,),...  10.5 us
    dot_general x1, matrix products, per_device(): visual = jnp.dot(merged, w_merge, preferred_element_type=F32).astype(BF16)  8.56 us
    all_gather x1, waiting for transfers between devices, per_device(): lax.all_gather(lax.dynamic_slice_in_dim(w_out, lax.axis_index('ctx') * fe...  5.98 us
  transfers between devices with their start and end apart: 3, of which 2 were waited for; matrix products, arithmetic and copies ran while one was open for 15% of the time, Pallas kernels for 57%

commit v1 on v0

--- a/solution.py
+++ b/solution.py
@@ -23,30 +23,19 @@
 SUB = ("vh", "core")
 MESH = pl.DeviceIdType.MESH
 VMEM = pl.BlockSpec(memory_space=pltpu.VMEM)
+ANY = pl.BlockSpec(memory_space=pl.ANY)
 F32 = jnp.float32
 BF16 = jnp.bfloat16
+PIECES = 2
+SUBROWS = 256
+LNROWS = 64
+LANES = 256
 
 
 def layer_norm(values, gain):
     center = values - jnp.mean(values, axis=-1, keepdims=True)
     spread = jnp.mean(center * center, axis=-1, keepdims=True)
     return center * lax.rsqrt(spread + EPS) * gain
-
-
-def vision_attention(qkv, local_heads):
-    scale = 1.0 / math.sqrt(VHD)
-    outs = []
-    for h in range(local_heads):
-        base = h * 3 * VHD
-        query = qkv[:, base : base + VHD]
-        keys = qkv[:, base + VHD : base + 2 * VHD]
-        values = qkv[:, base + 2 * VHD : base + 3 * VHD]
-        scores = jnp.einsum("qd,kd->qk", query, keys, preferred_element_type=F32) * scale
-        expo = jnp.exp(scores - jnp.max(scores, axis=1, keepdims=True))
-        summed = jnp.sum(expo, axis=1, keepdims=True)
-        mixed = jnp.einsum("qk,kd->dq", expo.astype(BF16), values, preferred_element_type=F32)
-        outs.append((mixed / summed.reshape(1, -1)).astype(BF16))
-    return jnp.concatenate(outs, axis=0)
 
 
 def flat_index(names, sizes):
@@ -258,6 +247,756 @@
     )(x)
 
 
+def front_kernel(sizes, *refs):
+    (
+        patches_ref, gain_ref, tgain_ref, wqkv_hbm, text_hbm, wkv_hbm,
+        qkv_ref, held, chain_last, mine_ref, mine_sq,
+        wqkv, wpad, text, wkv, normed, own, own_sq, pair_out, pair_in, chain_out, chain_in,
+        load_sem, send_sem, recv_sem, near_send, near_recv, pair_sem, chain_send, chain_recv,
+    ) = refs
+    chips, vh = sizes[0] * sizes[1], sizes[1]
+    core = lax.axis_index("core")
+    chip = lax.axis_index("vk") * vh + lax.axis_index("vh")
+    count = patches_ref.shape[0]
+    half = count // PIECES
+    each = mine_ref.shape[0]
+    subs = each // SUBROWS
+
+    def at(where, which):
+        return {"vk": where // vh, "vh": where % vh, "core": which}
+
+    def neighbour(direction):
+        return chip + 1 if direction == 0 else chip - 1
+
+    def has(direction):
+        return chip < chips - 1 if direction == 0 else chip > 0
+
+    def remote(src, dst, send, recv, where, which):
+        return pltpu.make_async_remote_copy(
+            src_ref=src, dst_ref=dst, send_sem=send, recv_sem=recv,
+            device_id=at(where, which), device_id_type=MESH,
+        )
+
+    loads = [
+        pltpu.make_async_copy(text_hbm, text, load_sem.at[0]),
+        pltpu.make_async_copy(wkv_hbm, wkv, load_sem.at[1]),
+        pltpu.make_async_copy(wqkv_hbm, wqkv, load_sem.at[2]),
+    ]
+    for load in loads:
+        load.start()
+
+    barrier = pltpu.get_barrier_semaphore()
+    pl.semaphore_signal(barrier, inc=1, device_id=at(chip, 1 - core), device_id_type=MESH)
+    for direction in range(2):
+        @pl.when(has(direction))
+        def _():
+            pl.semaphore_signal(
+                barrier, inc=1, device_id=at(neighbour(direction), core), device_id_type=MESH
+            )
+    pl.semaphore_wait(barrier, 1 + jnp.where(has(0), 1, 0) + jnp.where(has(1), 1, 0))
+
+    def slot(origin, which, piece):
+        return held.at[origin * 2 + which, pl.ds(piece * half, half)]
+
+    def source(origin, piece, hop):
+        return patches_ref.at[pl.ds(piece * half, half)] if hop == 0 else slot(origin, core, piece)
+
+    def origin_of(direction, hop):
+        return chip - hop if direction == 0 else chip + hop
+
+    def exists(direction, hop):
+        return chip >= hop if direction == 0 else chip + hop < chips
+
+    def pass_on(direction, hop, piece):
+        origin = origin_of(direction, hop)
+        return remote(
+            source(origin, piece, hop), slot(origin, core, piece),
+            send_sem.at[direction, hop, piece], recv_sem.at[direction, hop, piece],
+            neighbour(direction), core,
+        )
+
+    def arrival(direction, hop, piece):
+        origin = origin_of(direction, hop)
+        return remote(
+            slot(origin, core, piece), slot(origin, core, piece),
+            send_sem.at[direction, hop - 1, piece], recv_sem.at[direction, hop - 1, piece],
+            chip, 1 - core,
+        )
+
+    def give(origin, piece, hop):
+        return remote(
+            source(origin, piece, hop), slot(origin, core, piece),
+            near_send.at[origin, piece], near_recv.at[origin, piece], chip, 1 - core,
+        )
+
+    def taken(origin, piece):
+        return remote(
+            slot(origin, 1 - core, piece), slot(origin, 1 - core, piece),
+            near_send.at[origin, piece], near_recv.at[origin, piece], chip, 1 - core,
+        )
+
+    for piece in range(PIECES):
+        for direction in range(2):
+            @pl.when(has(direction))
+            def _():
+                pass_on(direction, 0, piece).start()
+    mine = pltpu.make_async_copy(patches_ref, held.at[chip * 2 + core], load_sem.at[3])
+    mine.start()
+    for piece in range(PIECES):
+        give(chip, piece, 0).start()
+
+    def relay(hop):
+        for piece in range(PIECES):
+            for direction in range(2):
+                @pl.when(exists(direction, hop))
+                def _():
+                    arrival(direction, hop, piece).wait_recv()
+                    if hop < chips - 1:
+                        @pl.when(has(direction))
+                        def _():
+                            pass_on(direction, hop, piece).start()
+                    give(origin_of(direction, hop), piece, hop).start()
+
+    def text_rows(v, which, write):
+        for s in range(subs):
+            first = pl.multiple_of((v * 2 + which) * each + s * SUBROWS, SUBROWS)
+            rows = text[pl.ds(first, SUBROWS), :].astype(F32)
+            total = jnp.sum(rows * rows, axis=1, keepdims=True)
+            line = jnp.transpose(jnp.broadcast_to(total, (SUBROWS, 128)))
+            own_sq[v, s : s + 1, :] = line[0:1]
+            scaled = (rows * tgain_ref[...]).astype(BF16)
+            for side in range(2):
+                for pair in range(KVH // 2):
+                    begin = (side * KVH + pair * 2) * HD
+                    raw = jnp.dot(scaled, wkv[:, begin : begin + 2 * HD], preferred_element_type=F32)
+                    for i in range(2):
+                        write((pair * 2 + i) * vh + v, s, side, raw[:, i * HD : (i + 1) * HD])
+
+    def tail(total):
+        coarse = total.astype(BF16).astype(F32)
+        return jnp.concatenate([coarse, total - coarse], axis=0).astype(BF16)
+
+    def untail(block):
+        block = block.astype(F32)
+        return block[:8] + block[8:]
+
+    def write_pair(d, s, side, value):
+        pair_out[d, s * SUBROWS : (s + 1) * SUBROWS, side * HD : (side + 1) * HD] = value.astype(BF16)
+
+    def write_own(d, s, side, value):
+        own[d, s * SUBROWS : (s + 1) * SUBROWS, side * HD : (side + 1) * HD] = value
+
+    own_sq[...] = jnp.zeros_like(own_sq)
+    loads[0].wait()
+    loads[1].wait()
+    for v in range(vh):
+        text_rows(v, 1 - core, write_pair)
+        for h in range(KVH):
+            pair_out[h * vh + v, each:, :] = tail(own_sq[v])
+    swap = remote(pair_out, pair_in, pair_sem.at[0], pair_sem.at[1], chip, 1 - core)
+    swap.start()
+    for v in range(vh):
+        text_rows(v, core, write_own)
+
+    loads[2].wait()
+    wpad[...] = jnp.zeros_like(wpad)
+    for part in range(wqkv.shape[1] // VHD):
+        wpad[:, part * 128 : part * 128 + VHD] = wqkv[:, part * VHD : (part + 1) * VHD]
+
+    def project(origin):
+        def norm_rows(i, carry):
+            which = i // (count // LNROWS)
+            begin = pl.multiple_of((i % (count // LNROWS)) * LNROWS, LNROWS)
+            floats = held[origin * 2 + which, pl.ds(begin, LNROWS), :].astype(F32)
+            place = pl.multiple_of(i * LNROWS, LNROWS)
+            normed[pl.ds(place, LNROWS), :] = layer_norm(floats, gain_ref[...]).astype(BF16)
+            return carry
+
+        lax.fori_loop(0, 2 * count // LNROWS, norm_rows, 0)
+        first = pl.multiple_of(origin * 2 * count, 2 * count)
+        qkv_ref[pl.ds(first, 2 * count), :] = jnp.dot(
+            normed[...], wpad[...], preferred_element_type=F32
+        ).astype(BF16)
+
+    def project_hop(hop):
+        for direction in range(2 if hop else 1):
+            @pl.when(exists(direction, hop))
+            def _():
+                origin = origin_of(direction, hop)
+                for piece in range(PIECES):
+                    taken(origin, piece).wait_recv()
+                project(origin)
+
+    def link(direction, d):
+        return remote(
+            chain_out.at[direction, d], chain_in.at[direction, d],
+            chain_send.at[direction, d], chain_recv.at[direction, d], neighbour(direction), core,
+        )
+
+    def sum_up(d, source, put, put_square):
+        def body(i, carry):
+            rows = pl.ds(pl.multiple_of(i * 128, 128), 128)
+            value = own[d, rows, :] + pair_in[d, rows, :].astype(F32)
+            if source is not None:
+                value += source[rows, :].astype(F32)
+            put(rows, value)
+            return carry
+
+        lax.fori_loop(0, each // 128, body, 0)
+        square = own_sq[d % vh] + untail(pair_in[d, each:, :])
+        if source is not None:
+            square += untail(source[each:, :])
+        put_square(square)
+
+    def chain(step):
+        for direction in range(2):
+            rank = chip if direction == 0 else chips - 1 - chip
+            ahead = chips - step
+            d = chip + ahead if direction == 0 else chip - ahead
+            last = step == chips - 1
+
+            def block():
+                return chain_last.at[direction] if last else chain_out.at[direction, d]
+
+            def put(rows, value):
+                block()[rows, :] = value.astype(BF16)
+
+            def put_square(square):
+                block()[each:, :] = tail(square)
+
+            @pl.when(rank < step)
+            def _():
+                @pl.when(rank == 0)
+                def _():
+                    sum_up(d, None, put, put_square)
+
+                if step > 1:
+                    @pl.when(rank > 0)
+                    def _():
+                        link(direction, d).wait_recv()
+                        sum_up(d, chain_in.at[direction, d], put, put_square)
+
+                if not last:
+                    link(direction, d).start()
+
+    relay(1)
+    swap.wait_recv()
+    if chips > 2:
+        chain(1)
+    mine.wait()
+    project_hop(0)
+    for hop in range(2, chips):
+        relay(hop)
+        if hop < chips - 1:
+            chain(hop)
+        project_hop(hop - 1)
+
+    def put_mine(rows, value):
+        mine_ref[rows, :] = value
+
+    def put_mine_square(square):
+        mine_sq[...] = square
+
+    sum_up(chip, None, put_mine, put_mine_square)
+    chain(chips - 1)
+    project_hop(chips - 1)
+
+    swap.wait_send()
+    for piece in range(PIECES):
+        give(chip, piece, 0).wait_send()
+        for direction in range(2):
+            for hop in range(chips):
+                if hop < chips - 1:
+                    @pl.when(jnp.logical_and(exists(direction, hop), has(direction)))
+                    def _():
+                        pass_on(direction, hop, piece).wait_send()
+                if hop > 0:
+                    @pl.when(exists(direction, hop))
+                    def _():
+                        give(origin_of(direction, hop), piece, hop).wait_send()
+    for direction in range(2):
+        for d in range(chips):
+            @pl.when(chip < d - 1 if direction == 0 else chip > d + 1)
+            def _():
+                link(direction, d).wait_send()
+
+
+def front(patches, vis_gain, w_qkv, text, kv_gain, w_kv, collective_id):
+    sizes = tuple(lax.axis_size(name) for name in VIS)
+    chips = sizes[0] * sizes[1]
+    parts = sizes[1] * 2
+    count, width = patches.shape
+    rows, features = text.shape
+    each = rows // parts
+    heads3 = w_qkv.shape[1] // VHD
+    block = (each + 16, 2 * HD)
+    DMA = pltpu.SemaphoreType.DMA
+    return pl.pallas_call(
+        functools.partial(front_kernel, sizes),
+        out_shape=[
+            jax.ShapeDtypeStruct((2 * chips * count, heads3 * 128), BF16),
+            jax.ShapeDtypeStruct((2 * chips, count, width), BF16),
+            jax.ShapeDtypeStruct((2,) + block, BF16),
+            jax.ShapeDtypeStruct((each, 2 * HD), F32),
+            jax.ShapeDtypeStruct((8, SUBROWS), F32),
+        ],
+        in_specs=[VMEM] * 3 + [ANY] * 3,
+        out_specs=[VMEM] * 5,
+        scratch_shapes=[
+            pltpu.VMEM(w_qkv.shape, BF16),
+            pltpu.VMEM((width, heads3 * 128), BF16),
+            pltpu.VMEM(text.shape, BF16),
+            pltpu.VMEM(w_kv.shape, BF16),
+            pltpu.VMEM((2 * count, width), BF16),
+            pltpu.VMEM((chips,) + (each, 2 * HD), F32),
+            pltpu.VMEM((sizes[1], 8, SUBROWS), F32),
+            pltpu.VMEM((chips,) + block, BF16),
+            pltpu.VMEM((chips,) + block, BF16),
+            pltpu.VMEM((2, chips) + block, BF16),
+            pltpu.VMEM((2, chips) + block, BF16),
+            DMA((4,)),
+            DMA((2, chips, PIECES)),
+            DMA((2, chips, PIECES)),
+            DMA((chips, PIECES)),
+            DMA((chips, PIECES)),
+            DMA((2,)),
+            DMA((2, chips)),
+            DMA((2, chips)),
+        ],
+        compiler_params=pltpu.CompilerParams(
+            collective_id=collective_id, has_side_effects=True, vmem_limit_bytes=48 * 2**20
+        ),
+    )(patches, vis_gain.reshape(1, -1), kv_gain.reshape(1, -1), w_qkv, text, w_kv)
+
+
+def spread_of(rows, width, places):
+    best = (1, 1)
+    for down in range(1, rows // 16 + 1):
+        for across in range(1, width // 128 + 1):
+            if rows % (16 * down) or width % (128 * across) or down * across > places:
+                continue
+            if down * across > best[0] * best[1]:
+                best = (down, across)
+    return best
+
+
+def middle_kernel(sizes, ctxs, *refs):
+    (
+        qkv_ref, patches_ref, wout_ref, gain_ref, chain_ref, mine_ref, sq_ref, wmerge_hbm,
+        visual_ref, text_ref,
+        held, wall, wmerge, mixed, merged, values, chain_in,
+        load_sem, send_sem, recv_sem, near_send, near_recv, chain_send, chain_recv,
+        line_send, line_recv, plane_send, plane_recv, pair_send, pair_recv,
+        text_send, text_recv, twin_send, twin_recv,
+    ) = refs
+    chips, vh = sizes[0] * sizes[1], sizes[1]
+    core, ctx = lax.axis_index("core"), lax.axis_index("ctx")
+    vk_index, vh_index = lax.axis_index("vk"), lax.axis_index("vh")
+    chip = vk_index * vh + vh_index
+    me = chip * 2 + core
+    each = mine_ref.shape[0]
+    subs = each // SUBROWS
+    deep, width = wout_ref.shape
+    total = qkv_ref.shape[0]
+    blocks = total // LANES
+    heads = deep // VHD
+    planes = ctxs * vh
+    plane = ctx * vh + vh_index
+
+    def at(where, which):
+        return {"vk": where // vh, "vh": where % vh, "core": which}
+
+    def beside(where):
+        return {"ctx": where // vh, "vh": where % vh}
+
+    def neighbour(direction):
+        return chip + 1 if direction == 0 else chip - 1
+
+    def has(direction):
+        return chip < chips - 1 if direction == 0 else chip > 0
+
+    def remote(src, dst, send, recv, device):
+        return pltpu.make_async_remote_copy(
+            src_ref=src, dst_ref=dst, send_sem=send, recv_sem=recv,
+            device_id=device, device_id_type=MESH,
+        )
+
+    twin = at(chip, 1 - core)
+    load = pltpu.make_async_copy(wmerge_hbm, wmerge, load_sem.at[0])
+    load.start()
+    my_rows = pl.ds(pl.multiple_of(me * deep, 16), deep)
+    keep = pltpu.make_async_copy(wout_ref, wall.at[my_rows], load_sem.at[1])
+    keep.start()
+
+    barrier = pltpu.get_barrier_semaphore()
+    pl.semaphore_signal(barrier, inc=1, device_id=twin, device_id_type=MESH)
+    for k in range(1, chips):
+        pl.semaphore_signal(
+            barrier, inc=1, device_id=at((chip + k) % chips, core), device_id_type=MESH
+        )
+    for j in range(1, planes):
+        pl.semaphore_signal(
+            barrier, inc=1, device_id=beside((plane + j) % planes), device_id_type=MESH
+        )
+    pl.semaphore_wait(barrier, chips + planes - 1)
+
+    def last_link(direction):
+        return remote(
+            chain_ref.at[direction], chain_in.at[direction],
+            chain_send.at[direction], chain_recv.at[direction], at(neighbour(direction), core),
+        )
+
+    for direction in range(2):
+        @pl.when(has(direction))
+        def _():
+            last_link(direction).start()
+
+    down, across = spread_of(deep, width, ctxs)
+    used, high, wide = down * across, deep // down, width // across
+
+    def part(origin, which, index):
+        first = pl.multiple_of((origin * 2 + which) * deep + (index // across) * high, 16)
+        lane = pl.multiple_of((index % across) * wide, 128)
+        return wall.at[pl.ds(first, high), pl.ds(lane, wide)]
+
+    def line_part(k):
+        first = pl.multiple_of((ctx // across) * high, 16)
+        lane = pl.multiple_of((ctx % across) * wide, 128)
+        return remote(
+            wout_ref.at[pl.ds(first, high), pl.ds(lane, wide)], part(chip, core, ctx),
+            line_send.at[k], line_recv.at[k], at((chip + k) % chips, core),
+        )
+
+    def from_line(k, j):
+        block = part((chip - k) % chips, core, ctx)
+        return remote(
+            block, block, plane_send.at[k, j], plane_recv.at[k, j], {"ctx": (ctx + j) % ctxs}
+        )
+
+    def to_twin(k, j, which):
+        block = part((chip - k) % chips, which, (ctx - j) % ctxs)
+        return remote(block, block, pair_send.at[k, j], pair_recv.at[k, j], twin)
+
+    def own_to_twin():
+        return remote(wout_ref, wall.at[my_rows], pair_send.at[0, 0], pair_recv.at[0, 0], twin)
+
+    for k in range(1, chips):
+        @pl.when(ctx < used)
+        def _():
+            line_part(k).start()
+    own_to_twin().start()
+
+    def slot(origin, which, piece):
+        first = pl.multiple_of((origin * 2 + which) * deep, 16)
+        return held.at[pl.ds(first, deep), pl.ds(pl.multiple_of(piece * LANES, LANES), LANES)]
+
+    def origin_of(direction, hop):
+        return chip - hop if direction == 0 else chip + hop
+
+    def exists(direction, hop):
+        return chip >= hop if direction == 0 else chip + hop < chips
+
+    def pass_on(direction, hop, piece):
+        block = slot(origin_of(direction, hop), core, piece)
+        return remote(
+            block, block, send_sem.at[direction, hop, piece], recv_sem.at[direction, hop, piece],
+            at(neighbour(direction), core),
+        )
+
+    def arrival(direction, hop, piece):
+        block = slot(origin_of(direction, hop), core, piece)
+        return remote(
+            block, block, send_sem.at[direction, hop - 1, piece],
+            recv_sem.at[direction, hop - 1, piece], twin,
+        )
+
+    def give(origin, piece, which):
+        block = slot(origin, which, piece)
+        return remote(
+            block, block, near_send.at[origin, piece], near_recv.at[origin, piece], twin
+        )
+
+    scale = 1.0 / math.sqrt(VHD)
+    for h in range(heads):
+        first = (h * 3 + 2) * 128
+        values[h] = jnp.transpose(qkv_ref[:, first : first + 128].astype(F32)).astype(BF16)
+
+    def attend(b, carry):
+        lanes = pl.ds(pl.multiple_of(b * LANES, LANES), LANES)
+        for h in range(heads):
+            first = h * 3 * 128
+            query = qkv_ref[lanes, first : first + 128]
+            keys = qkv_ref[:, first + 128 : first + 256]
+            scores = lax.dot_general(
+                keys, query, (((1,), (1,)), ((), ())), preferred_element_type=F32
+            ) * scale
+            expo = jnp.exp(scores - jnp.max(scores, axis=0, keepdims=True))
+            summed = jnp.sum(expo, axis=0, keepdims=True)
+            mix = jnp.dot(values[h], expo.astype(BF16), preferred_element_type=F32)
+            rows = pl.ds(pl.multiple_of(me * deep + h * VHD, 16), VHD)
+            held[rows, lanes] = (mix[:VHD] / summed).astype(BF16)
+        for direction in range(2):
+            @pl.when(has(direction))
+            def _():
+                pass_on(direction, 0, b).start()
+        give(chip, b, core).start()
+        return carry
+
+    lax.fori_loop(0, blocks, attend, 0)
+
+    def relay(hop):
+        def body(piece, carry):
+            for direction in range(2):
+                @pl.when(exists(direction, hop))
+                def _():
+                    arrival(direction, hop, piece).wait_recv()
+                    if hop < chips - 1:
+                        @pl.when(has(direction))
+                        def _():
+                            pass_on(direction, hop, piece).start()
+                    give(origin_of(direction, hop), piece, core).start()
+            return carry
+
+        lax.fori_loop(0, blocks, body, 0)
+
+    def text_slot(place, which):
+        return text_ref.at[pl.ds(pl.multiple_of((place * 2 + which) * each, 16), each)]
+
+    def text_link(j):
+        block = text_slot(plane, core)
+        return remote(
+            block, block, text_send.at[j], text_recv.at[j], beside((plane + j) % planes)
+        )
+
+    def text_from(j):
+        block = text_slot((plane - j) % planes, core)
+        return remote(block, block, text_send.at[j], text_recv.at[j], twin)
+
+    def text_twin(j, which):
+        block = text_slot((plane - j) % planes, which)
+        return remote(block, block, twin_send.at[j], twin_recv.at[j], twin)
+
+    def untail(block):
+        block = block.astype(F32)
+        return block[:8] + block[8:]
+
+    def gain_from(direction):
+        last_link(direction).wait_recv()
+
+        def body(i, carry):
+            rows = pl.ds(pl.multiple_of(i * 128, 128), 128)
+            mine_sum[rows, :] += chain_in[direction, rows, :].astype(F32)
+            return carry
+
+        lax.fori_loop(0, each // 128, body, 0)
+        squares[...] += untail(chain_in[direction, each:, :])
+
+    def finish_text(sum_ref, square_ref):
+        nonlocal mine_sum, squares
+        mine_sum, squares = sum_ref, square_ref
+        mine_sum[...] = mine_ref[...]
+        squares[...] = sq_ref[...]
+        for direction in range(2):
+            @pl.when(has(1 - direction))
+            def _():
+                gain_from(direction)
+        inverse = lax.rsqrt(squares[...] / D + EPS)
+        for s in range(subs):
+            factor = jnp.transpose(jnp.broadcast_to(inverse[s : s + 1], (128, SUBROWS)))
+            place = pl.multiple_of((plane * 2 + core) * each + s * SUBROWS, 16)
+            for side in range(2):
+                lanes = slice(side * HD, (side + 1) * HD)
+                value = mine_sum[s * SUBROWS : (s + 1) * SUBROWS, lanes] * factor
+                text_ref[pl.ds(place, SUBROWS), lanes] = value.astype(BF16)
+
+    mine_sum = squares = None
+    pl.run_scoped(
+        finish_text, pltpu.VMEM((each, 2 * HD), F32), pltpu.VMEM((8, SUBROWS), F32)
+    )
+    for j in range(1, planes):
+        text_link(j).start()
+    text_twin(0, core).start()
+
+    relay(1)
+    for k in range(1, chips):
+        @pl.when(ctx < used)
+        def _():
+            line_part(k).wait_recv()
+            for j in range(1, ctxs):
+                from_line(k, j).start()
+            to_twin(k, 0, core).start()
+
+    def add_chip(origin, fresh):
+        rows = pl.ds(pl.multiple_of(origin * 2 * deep, 16), 2 * deep)
+
+        def body(i, carry):
+            places = pl.ds(pl.multiple_of(i * LANES, LANES), LANES)
+            product = lax.dot_general(
+                held[rows, places], wall[rows, :], (((0,), (0,)), ((), ())),
+                preferred_element_type=F32,
+            )
+            if fresh:
+                product += patches_ref[places, :].astype(F32)
+            for c in range(width // 128):
+                lanes = product[:, c * 128 : (c + 1) * 128]
+                mixed[c, places, :] = lanes if fresh else mixed[c, places, :] + lanes
+            return carry
+
+        lax.fori_loop(0, blocks, body, 0)
+
+    def add_hop(hop):
+        for direction in range(2 if hop else 1):
+            @pl.when(exists(direction, hop))
+            def _():
+                origin = origin_of(direction, hop)
+                for piece in range(blocks):
+                    give(origin, piece, 1 - core).wait_recv()
+                add_chip(origin, hop == 0)
+
+    keep.wait()
+    own_to_twin().wait_recv()
+    add_hop(0)
+    if chips > 2:
+        relay(2)
+    for j in range(1, planes):
+        text_from(j).wait_recv()
+        text_twin(j, core).start()
+    for k in range(1, chips):
+        for j in range(1, ctxs):
+            @pl.when((ctx - j) % ctxs < used)
+            def _():
+                block = part((chip - k) % chips, core, (ctx - j) % ctxs)
+                remote(
+                    block, block, plane_send.at[k, j], plane_recv.at[k, j], twin
+                ).wait_recv()
+                to_twin(k, j, core).start()
+    for k in range(1, chips):
+        for j in range(ctxs):
+            @pl.when((ctx - j) % ctxs < used)
+            def _():
+                to_twin(k, j, 1 - core).wait_recv()
+    add_hop(1)
+    for hop in range(3, chips):
+        relay(hop)
+        add_hop(hop - 1)
+    if chips > 2:
+        add_hop(chips - 1)
+
+    load.wait()
+    tokens = total // 4
+    for r in range(4):
+        def norm_rows(i, carry):
+            every = pl.ds(i * 4 * LNROWS + r, LNROWS, stride=4)
+            rows = jnp.concatenate([mixed[c, every, :] for c in range(width // 128)], axis=1)
+            place = pl.ds(pl.multiple_of(i * LNROWS, LNROWS), LNROWS)
+            merged[r, place, :] = layer_norm(rows, gain_ref[...]).astype(BF16)
+            return carry
+
+        lax.fori_loop(0, tokens // LNROWS, norm_rows, 0)
+
+    def column(c, carry):
+        lanes = pl.ds(pl.multiple_of(c * LANES, LANES), LANES)
+        value = jnp.dot(merged[0], wmerge[:width, lanes], preferred_element_type=F32)
+        for r in range(1, 4):
+            value += jnp.dot(
+                merged[r], wmerge[r * width : (r + 1) * width, lanes], preferred_element_type=F32
+            )
+        visual_ref[:, lanes] = value.astype(BF16)
+        return carry
+
+    lax.fori_loop(0, visual_ref.shape[1] // LANES, column, 0)
+
+    for j in range(planes):
+        text_twin(j, 1 - core).wait_recv()
+        text_twin(j, core).wait_send()
+        if j:
+            text_link(j).wait_send()
+    own_to_twin().wait_send()
+    for k in range(1, chips):
+        @pl.when(ctx < used)
+        def _():
+            line_part(k).wait_send()
+            for j in range(1, ctxs):
+                from_line(k, j).wait_send()
+        for j in range(ctxs):
+            @pl.when((ctx - j) % ctxs < used)
+            def _():
+                to_twin(k, j, core).wait_send()
+    for direction in range(2):
+        @pl.when(has(direction))
+        def _():
+            last_link(direction).wait_send()
+
+    def drain(piece, carry):
+        give(chip, piece, core).wait_send()
+        for direction in range(2):
+            for hop in range(chips):
+                if hop < chips - 1:
+                    @pl.when(jnp.logical_and(exists(direction, hop), has(direction)))
+                    def _():
+                        pass_on(direction, hop, piece).wait_send()
+                if hop > 0:
+                    @pl.when(exists(direction, hop))
+                    def _():
+                        give(origin_of(direction, hop), piece, core).wait_send()
+        return carry
+
+    lax.fori_loop(0, blocks, drain, 0)
+
+
+def middle(qkv, gathered, w_out, merge_gain, w_merge, chain_last, mine, mine_sq, collective_id):
+    sizes = tuple(lax.axis_size(name) for name in VIS)
+    ctxs = lax.axis_size("ctx")
+    chips, planes = sizes[0] * sizes[1], ctxs * sizes[1]
+    total, width = qkv.shape[0], w_out.shape[1]
+    each = mine.shape[0]
+    blocks = total // LANES
+    heads = w_out.shape[0] // VHD
+    tokens = total // 4
+    DMA = pltpu.SemaphoreType.DMA
+    return pl.pallas_call(
+        functools.partial(middle_kernel, sizes, ctxs),
+        out_shape=[
+            jax.ShapeDtypeStruct((tokens, w_merge.shape[1]), BF16),
+            jax.ShapeDtypeStruct((planes * 2 * each, 2 * HD), BF16),
+        ],
+        in_specs=[VMEM] * 7 + [ANY],
+        out_specs=[VMEM] * 2,
+        scratch_shapes=[
+            pltpu.VMEM((VD, total), BF16),
+            pltpu.VMEM((VD, width), BF16),
+            pltpu.VMEM(w_merge.shape, BF16),
+            pltpu.VMEM((width // 128, total, 128), F32),
+            pltpu.VMEM((4, tokens, width), BF16),
+            pltpu.VMEM((heads, 128, total), BF16),
+            pltpu.VMEM(chain_last.shape, BF16),
+            DMA((2,)),
+            DMA((2, chips, blocks)),
+            DMA((2, chips, blocks)),
+            DMA((chips, blocks)),
+            DMA((chips, blocks)),
+            DMA((2,)),
+            DMA((2,)),
+            DMA((chips,)),
+            DMA((chips,)),
+            DMA((chips, ctxs)),
+            DMA((chips, ctxs)),
+            DMA((chips, ctxs)),
+            DMA((chips, ctxs)),
+            DMA((planes,)),
+            DMA((planes,)),
+            DMA((planes,)),
+            DMA((planes,)),
+        ],
+        compiler_params=pltpu.CompilerParams(
+            collective_id=collective_id, has_side_effects=True, vmem_limit_bytes=52 * 2**20
+        ),
+    )(
+        qkv, gathered.reshape(total, width), w_out, merge_gain.reshape(1, -1), chain_last, mine,
+        mine_sq, w_merge,
+    )
+
+
 def project_kernel(joined, rows_ref, weight_ref, out_ref, *rest):
     each = rows_ref.shape[0]
     rows = rows_ref[...]
@@ -320,15 +1059,6 @@
     return [out.reshape((KVH * parts,) + out.shape[2:]) for out in outs]
 
 
-def whole_text(total):
-    total = total[0]
-    each = total.shape[0] - 8
-    squares = total[each : each + each // (2 * HD)].reshape(each)
-    inverse = lax.rsqrt(squares / D + EPS)
-    share = (total[:each] * inverse[:, None]).astype(BF16)
-    return lax.all_gather(share, ("ctx",) + SUB, axis=0, tiled=True)
-
-
 def whole_image(visual, weight, parts):
     pieces, squares = project(visual, weight, parts, False)
     pieces, squares = exchange((pieces, squares), VIS, False, 3)
@@ -359,41 +1089,16 @@
     vis_count = lax.axis_size("vk") * parts
     ctx_count = lax.axis_size("ctx")
     vis_index = flat_index(VIS, tuple(lax.axis_size(name) for name in VIS))
-    patch_count = patches.shape[0]
     shard_rows = prompt_text.shape[0]
-    local_heads = VHEADS // vis_count
-
-    floats = patches.astype(F32)
-    normed = layer_norm(floats, vis_gain).astype(BF16)
-    gathered = line_gather(normed, 2, 0).reshape(-1, VD)
-    few = w_out.shape[0] // ctx_count
-    w_out_all = lax.all_gather(
-        lax.dynamic_slice_in_dim(w_out, lax.axis_index("ctx") * few, few, 0),
-        ("ctx",) + VIS,
-        axis=0,
-        tiled=True,
+
+    qkv, gathered, chain_last, text_mine, text_sq = front(
+        patches, vis_gain, w_qkv, prompt_text, kv_gain, w_kv, 0
     )
-
+    visual, text_kv = middle(
+        qkv, gathered, w_out, merge_gain, w_merge, chain_last, text_mine, text_sq, 1
+    )
     weight = (w_kv.astype(F32) * kv_gain[:, None]).astype(BF16)
 
-    qkv = jnp.dot(gathered, w_qkv, preferred_element_type=F32).astype(BF16)
-    heads = vision_attention(qkv, local_heads)
-    heads = heads.reshape(-1, vis_count, patch_count).transpose(1, 0, 2)
-    (returned,) = exchange((heads,), VIS, False, 1)
-    weight, returned, w_out_all = lax.optimization_barrier((weight, returned, w_out_all))
-    text_total = lax.psum_scatter(
-        project(prompt_text, weight, parts, True)[0], VIS, scatter_dimension=0, tiled=True
-    )
-    returned = returned.reshape(vis_count, ctx_count, few, patch_count).transpose(1, 0, 2, 3)
-    projected = jnp.einsum(
-        "dp,de->pe", returned.reshape(VD, patch_count), w_out_all, preferred_element_type=F32
-    )
-    mixed = floats + projected
-    merged = layer_norm(mixed, merge_gain).astype(BF16).reshape(patch_count // 4, MD)
-    merged = line_gather(merged, 2, 2).reshape(-1, MD)
-    visual = jnp.dot(merged, w_merge, preferred_element_type=F32).astype(BF16)
-    visual, text_total = lax.optimization_barrier((visual, text_total))
-    text_kv = whole_text(text_total)
     image_kv = whole_image(visual, weight, parts)
 
     flat = (token_dest * shard_rows + token_row).reshape(-1)

time: 233 us -> 168 us (0.72)
  Pallas kernels: 157 us -> 139 us
  matrix products: 22.9 us -> 5.5 us
  between operations: 14.1 us -> 0.94 us
  other arithmetic: 19.4 us -> 10.9 us
  waiting for transfers between devices: 7.82 us -> 0 us
    pallas_call x0 -> x2, Pallas kernels: none -> 88.9 us  [the longest x1 57.1 us: middle(): pl.pallas_call(functools.partial(middle_kernel, sizes, ctxs), out_shape=[...]
    pallas_call x3 -> x1, Pallas kernels: 106 us -> 18.5 us  [line_gather(): pl.pallas_call(functools.partial(line_kernel, sizes, chunks), out_shape=j...]
    dot_general x7 -> x0, matrix products: 17.6 us -> none  [the longest x1 8.56 us: per_device(): visual = jnp.dot(merged, w_merge, preferred_element_type=F32).astype(BF16)]
    pallas_call x3 -> x2, Pallas kernels: 40.1 us -> 27.6 us  [exchange(): pl.pallas_call(functools.partial(exchange_kernel, names, sizes, spread, c...]
    pallas_call x2 -> x1, Pallas kernels: 10.5 us -> 3.58 us  [project(): pl.pallas_call(functools.partial(project_kernel, joined), grid=(parts,),...]
    all_gather x2 -> x0, waiting for transfers between devices: 6 us -> none  [the longest x1 5.98 us: per_device(): lax.all_gather(lax.dynamic_slice_in_dim(w_out, lax.axis_index('ctx') * fe...]
    reduce_sum x5 -> x0, other arithmetic: 4 us -> none  [the longest x2 1.47 us: vision_attention(): summed = jnp.sum(expo, axis=1, keepdims=True)]
    convert_element_type x3 -> x0, other arithmetic: 3.99 us -> none  [the longest x1 1.93 us: per_device(): normed = layer_norm(floats, vis_gain).astype(BF16)]
  transfers between devices with their start and end apart: 3 -> 0, of which waited for: 2 -> 0; matrix products, arithmetic and copies ran while one was open for 15% -> 0% of each run, Pallas kernels for 57% -> 0%
where the time goes in v1:
time: 168 us; the launch traced here: 167 us
  Pallas kernels  139 us (83%)
  local copies, waits for them, and re-layouts  11.5 us (7%)
  other arithmetic  10.9 us (6%)
  matrix products  5.5 us (3%)
    pallas_call x1, Pallas kernels, middle(): pl.pallas_call(functools.partial(middle_kernel, sizes, ctxs), out_shape=[...  57.1 us
    pallas_call x1, Pallas kernels, front(): pl.pallas_call(functools.partial(front_kernel, sizes), out_shape=[jax.Sha...  31.8 us
    pallas_call x2, Pallas kernels, exchange(): pl.pallas_call(functools.partial(exchange_kernel, names, sizes, spread, c...  27.6 us
    pallas_call x1, Pallas kernels, line_gather(): pl.pallas_call(functools.partial(line_kernel, sizes, chunks), out_shape=j...  18.5 us
    unnamed x28, local copies, waits for them, and re-layouts  4.93 us
    reduce_sum x1, other arithmetic, per_device(): early_sum = jnp.sum(expo, axis=1, keepdims=True)  3.88 us
    dot_general x2, matrix products, scores_of(): jnp.einsum('qd,kd->qk', query, keys, preferred_element_type=F32) * scale  3.65 us
    pallas_call x1, Pallas kernels, project(): pl.pallas_call(functools.partial(project_kernel, joined), grid=(parts,),...  3.58 us

profile of v1, /device:TPU:0, one launch (start us, length us, event | category | flops | bytes accessed | tf_op | source)
XLA Modules:
  0.0 167.4 jit_solution(9842661149415777392)
XLA Ops:
  0.0 0.0 copy-start
  0.0 1.2 copy-done
  1.2 0.1 copy.33
  1.4 0.1 copy.28
  1.5 0.8 constant_dynamic-slice_fusion
  2.3 0.7 reshape.86.refs_1_
  3.0 1.6 copy.29.refs_3_
  4.6 0.0 copy-done.4
  4.6 0.0 copy-done.5
  4.6 0.0 copy-start.9
  4.6 0.0 copy-start.3
  4.7 31.8 %shard_map.136 = (bf16[1024,768]{1,0:T(8,128)(2,1)S(1)}, bf16[8,128,1280]{2,1,0:T(8,128)(2,1)}, bf16[2,528,256]{2,1,0:T(8,128)(2,1)S(1)}, f32[512,256]{1,0:T(8,128)S(1)}, f32[8,256]{1,0:T(8,128)S(1)}) custom-call(bf16[128,1280]{1,0:T(8,128)(2,1)S(1)} %copy-done.4, f32[1,1280]{1,0:T(1,128)S(1)} %reshape.86.refs_1_, f32[1,1024]{1,0:T(1,128)S(1)} %bitcast.34, ...), custom_call_target="tpu_custom_call" | custom-call | tf_op jit(solution)/shard_map/pallas_call | solution.py:534
  36.5 0.0 copy-start.1
  36.5 1.2 copy-done.1
  37.7 0.0 copy-done.9
  37.7 0.0 copy-done.3
  37.7 57.1 %shard_map.137 = (bf16[256,1024]{1,0:T(8,128)(2,1)S(1)}, bf16[4096,256]{1,0:T(8,128)(2,1)}) custom-call(bf16[1024,768]{1,0:T(8,128)(2,1)} %copy-done.1, bf16[1024,1280]{1,0:T(8,128)(2,1)} %bitcast.37, bf16[160,1280]{1,0:T(8,128)(2,1)S(1)} %copy-done.3, f32[1,1280]{1,0:T(1,128)S(1)} %reshape.89.refs_3_, bf16[2,528,256]{2,1,0:T(8,128)(2,1)S(1)} %get-tuple-element.18.refs_4_, ...), custom_call_target="tpu_custom_call" | custom-call | tf_op jit(solution)/shard_map/pallas_call | solution.py:957
  94.8 0.0 copy-start.2
  94.8 0.0 copy-start.10
  94.8 0.0 copy-start.11
  94.8 1.9 %fusion.23 = (bf16[4096,128]{1,0:T(8,128)(2,1)S(1)}, bf16[4096,128]{1,0:T(8,128)(2,1)S(1)}) fusion(bf16[4096,256]{1,0:T(8,128)(2,1)} %get-tuple-element.21), kind=kLoop, calls=%fused_computation.45 | loop fusion | bytes 4194304 | tf_op jit(solution)/shard_map/slice | solution.py:1119
  96.7 0.0 copy-done.2
  96.7 0.0 copy-done.10
  96.7 0.0 copy-done.11
  96.8 2.0 %fusion = pred[4096]{0:T(1024)(128)(4,1)S(1)} fusion(s32[1024]{0:T(1024)S(1)} %bitcast.48), kind=kLoop, calls=%fused_computation.1 | loop fusion | flops 8384512 | bytes 8192 | tf_op jit(solution)/shard_map/reduce_or | solution.py:1106
  98.8 0.1 pad_add_fusion
  98.9 2.0 %fusion.24 = (f32[512]{0:T(512)S(1)}, f32[512,4224]{1,0:T(8,128)S(1)}) fusion(bf16[512,128]{1,0:T(8,128)(2,1)S(1)} %bitcast.38, bf16[128,128]{1,0:T(8,128)(2,1)S(1)} %get-tuple-element.34, bf16[4096,128]{1,0:T(8,128)(2,1)S(1)} %get-tuple-element.32, pred[128,4224]{1,0:T(8,128)(4,1)S(1)} %pad_add_fusion), kind=kOutput, calls=%fused_computation.46 | convolution fusion | flops 562298368 | bytes 10405888 | tf_op jit(solution)/shard_map/qd,kd->qk/dot_general | solution.py:1130
  101.0 3.9 %fusion.1 = (f32[512]{0:T(512)S(1)}, bf16[512,4224]{1,0:T(8,128)(2,1)}) fusion(f32[512,4224]{1,0:T(8,128)S(1)} %get-tuple-element.36, f32[512]{0:T(512)S(1)} %get-tuple-element.35, pred[128,4224]{1,0:T(8,128)(4,1)S(1)} %pad_add_fusion), kind=kLoop, calls=%fused_computation.4 | loop fusion | flops 8650240 | bytes 13520896 | tf_op jit(solution)/shard_map/reduce_sum | solution.py:1135
  104.8 0.0 copy-done.6
  104.8 1.7 %multiply_convert_fusion.weight_ref = bf16[1024,1024]{1,0:T(8,128)(2,1)} fusion(bf16[1024,1024]{1,0:T(8,128)(2,1)S(1)} %copy-done.6, f32[1024]{0:T(1024)S(1)} %copy-done.5), kind=kLoop, calls=%fused_computation.6 | loop fusion | flops 3145728 | bytes 4198400 | tf_op jit(solution)/shard_map/convert_element_type | solution.py:1100
  106.6 3.6 %shard_map.138 = (bf16[4,2,128,256]{3,2,1,0:T(8,128)(2,1)}, f32[4,2,8,128]{3,2,1,0:T(8,128)}) custom-call(bf16[256,1024]{1,0:T(8,128)(2,1)} %copy-done.2, bf16[1024,1024]{1,0:T(8,128)(2,1)} %multiply_convert_fusion.weight_ref), custom_call_target="tpu_custom_call" | custom-call | flops 536870912 | bytes 2621440 | tf_op jit(solution)/shard_map/pallas_call | solution.py:1042
  110.1 16.3 %shard_map.139 = (bf16[8,128,256]{2,1,0:T(8,128)(2,1)}, f32[8,8,128]{2,1,0:T(8,128)}) custom-call(bf16[8,128,256]{2,1,0:T(8,128)(2,1)} %bitcast.43, f32[8,8,128]{2,1,0:T(8,128)} %bitcast.47), custom_call_target="tpu_custom_call" | custom-call | bytes 30000000 | tf_op jit(solution)/shard_map/pallas_call | solution.py:98
  126.4 1.1 convert_reduce_fusion
  127.6 0.8 slice_reduce_fusion
  128.4 0.7 multiply_convert_fusion.1.refs_0_
  129.1 11.3 %shard_map.140 = bf16[8,128,256]{2,1,0:T(8,128)(2,1)} custom-call(bf16[128,256]{1,0:T(8,128)(2,1)} %multiply_convert_fusion.1.refs_0_), custom_call_target="tpu_custom_call" | custom-call | bytes 30000000 | tf_op jit(solution)/shard_map/pallas_call | solution.py:98
  140.4 0.0 copy-start.7
  140.4 1.6 multiply_reduce_fusion
  142.0 0.5 fusion.3
  142.5 0.1 copy-done.7
  142.7 1.3 convolution_multiply_fusion
  144.6 0.0 copy-done.8
  144.6 0.6 fusion.7
  145.2 0.1 copy.30
  145.3 0.7 copy.37
  146.0 18.5 %shard_map.141 = bf16[8,128,512]{2,1,0:T(8,128)(2,1)} custom-call(bf16[128,512]{1,0:T(8,128)(2,1)} %bitcast.42), custom_call_target="tpu_custom_call" | custom-call | bytes 70000000 | tf_op jit(solution)/shard_map/pallas_call | solution.py:231
  164.5 1.6 copy.31
  166.1 1.3 copy.32
  (16 shorter events, 0.1 us)
Async XLA Ops:
  0.0 1.2 copy-start
  0.0 4.6 %copy-start.4 = (bf16[128,1280]{1,0:T(8,128)(2,1)S(1)}, bf16[128,1280]{1,0:T(8,128)(2,1)}, u32[]{:S(2)}) copy-start(bf16[128,1280]{1,0:T(8,128)(2,1)} %refs_0_.1) | copy-start | bytes 983044
  0.0 4.6 %copy-start.5 = (f32[1024]{0:T(1024)S(1)}, f32[1024]{0:T(1024)}, u32[]{:S(2)}) copy-start(f32[1024]{0:T(1024)} %param.23) | copy-start | bytes 12292
  4.6 33.0 %copy-start.9 = (f32[1280]{0:T(1024)S(1)}, f32[1280]{0:T(1024)}, u32[]{:S(2)}) copy-start(f32[1280]{0:T(1024)} %param.18) | copy-start | bytes 15364
  4.6 33.0 %copy-start.3 = (bf16[160,1280]{1,0:T(8,128)(2,1)S(1)}, bf16[160,1280]{1,0:T(8,128)(2,1)}, u32[]{:S(2)}) copy-start(bf16[160,1280]{1,0:T(8,128)(2,1)} %refs_2_.1) | copy-start | bytes 1228804
  36.5 1.2 copy-start.1
  94.8 1.9 %copy-start.2 = (bf16[256,1024]{1,0:T(8,128)(2,1)}, bf16[256,1024]{1,0:T(8,128)(2,1)S(1)}, u32[]{:S(2)}) copy-start(bf16[256,1024]{1,0:T(8,128)(2,1)S(1)} %get-tuple-element.22.rows_ref) | copy-start | bytes 1572868
  94.8 1.9 %copy-start.10 = (s32[4,256]{1,0:T(4,128)S(1)}, s32[4,256]{1,0:T(4,128)}, u32[]{:S(2)}) copy-start(s32[4,256]{1,0:T(4,128)} %param.21) | copy-start | bytes 12292
  94.8 1.9 %copy-start.11 = (s32[4,256]{1,0:T(4,128)S(1)}, s32[4,256]{1,0:T(4,128)}, u32[]{:S(2)}) copy-start(s32[4,256]{1,0:T(4,128)} %param.20) | copy-start | bytes 12292
  100.9 3.9 %copy-start.6 = (bf16[1024,1024]{1,0:T(8,128)(2,1)S(1)}, bf16[1024,1024]{1,0:T(8,128)(2,1)}, u32[]{:S(2)}) copy-start(bf16[1024,1024]{1,0:T(8,128)(2,1)} %refs_5_.1) | copy-start | bytes 6291460
  140.4 2.3 %copy-start.7 = (bf16[512,4224]{1,0:T(8,128)(2,1)S(1)}, bf16[512,4224]{1,0:T(8,128)(2,1)}, u32[]{:S(2)}) copy-start(bf16[512,4224]{1,0:T(8,128)(2,1)} %get-tuple-element.30) | copy-start | bytes 12976132
  142.7 2.0 %copy-start.8 = (bf16[8,128,256]{2,1,0:T(8,128)(2,1)S(1)}, bf16[8,128,256]{2,1,0:T(8,128)(2,1)}, u32[]{:S(2)}) copy-start(bf16[8,128,256]{2,1,0:T(8,128)(2,1)} %shard_map.140) | copy-start | bytes 1572868

commit v2 on v1

--- a/solution.py
+++ b/solution.py
@@ -9,7 +9,6 @@
 from jax.sharding import Mesh, PartitionSpec as P
 
 VD = 1280
-VHEADS = 16
 D = 8192
 HD = 128
 QH = 32
@@ -20,7 +19,6 @@
 
 EPS = 1e-06
 VIS = ("vk", "vh", "core")
-SUB = ("vh", "core")
 MESH = pl.DeviceIdType.MESH
 VMEM = pl.BlockSpec(memory_space=pltpu.VMEM)
 ANY = pl.BlockSpec(memory_space=pl.ANY)
@@ -30,221 +28,13 @@
 SUBROWS = 256
 LNROWS = 64
 LANES = 256
+KEYS = 512
 
 
 def layer_norm(values, gain):
     center = values - jnp.mean(values, axis=-1, keepdims=True)
     spread = jnp.mean(center * center, axis=-1, keepdims=True)
     return center * lax.rsqrt(spread + EPS) * gain
-
-
-def flat_index(names, sizes):
-    index = 0
-    for name, size in zip(names, sizes):
-        index = index * size + lax.axis_index(name)
-    return index
-
-
-def coordinates(index, names, sizes):
-    place = {}
-    for name, size in reversed(list(zip(names, sizes))):
-        place[name] = index % size
-        index = index // size
-    return place
-
-
-def exchange_kernel(names, sizes, spread, count, *refs):
-    xs, outs = refs[:count], refs[count : 2 * count]
-    send_sem, recv_sem, local_sem = refs[2 * count :]
-    total = math.prod(sizes)
-    me = flat_index(names, sizes)
-    barrier = pltpu.get_barrier_semaphore()
-    for step in range(1, total):
-        pl.semaphore_signal(
-            barrier,
-            inc=1,
-            device_id=coordinates((me + step) % total, names, sizes),
-            device_id_type=MESH,
-        )
-    pl.semaphore_wait(barrier, total - 1)
-    copies = []
-    for step in range(1, total):
-        target = (me + step) % total
-        for i in range(count):
-            copy = pltpu.make_async_remote_copy(
-                src_ref=xs[i] if spread else xs[i].at[target],
-                dst_ref=outs[i].at[me],
-                send_sem=send_sem.at[i, step],
-                recv_sem=recv_sem.at[i, step],
-                device_id=coordinates(target, names, sizes),
-                device_id_type=MESH,
-            )
-            copy.start()
-            copies.append(copy)
-    for i in range(count):
-        own = pltpu.make_async_copy(
-            xs[i] if spread else xs[i].at[me], outs[i].at[me], local_sem.at[i]
-        )
-        own.start()
-        copies.append(own)
-    for copy in copies:
-        copy.wait()
-
-
-def exchange(xs, names, spread, collective_id):
-    sizes = tuple(lax.axis_size(name) for name in names)
-    total, count = math.prod(sizes), len(xs)
-    shapes = [((total,) + x.shape) if spread else x.shape for x in xs]
-    return pl.pallas_call(
-        functools.partial(exchange_kernel, names, sizes, spread, count),
-        out_shape=[jax.ShapeDtypeStruct(sh, x.dtype) for sh, x in zip(shapes, xs)],
-        in_specs=[VMEM] * count,
-        out_specs=[VMEM] * count,
-        scratch_shapes=[
-            pltpu.SemaphoreType.DMA((count, total)),
-            pltpu.SemaphoreType.DMA((count, total)),
-            pltpu.SemaphoreType.DMA((count,)),
-        ],
-        compiler_params=pltpu.CompilerParams(
-            collective_id=collective_id, has_side_effects=True
-        ),
-        cost_estimate=pl.CostEstimate(flops=0, bytes_accessed=30_000_000, transcendentals=0),
-    )(*xs)
-
-
-def line_kernel(sizes, chunks, x_ref, out_ref, send_sem, recv_sem, share_send, share_recv, local_sem):
-    chips = sizes[0] * sizes[1]
-    core = lax.axis_index("core")
-    chip = lax.axis_index("vk") * sizes[1] + lax.axis_index("vh")
-    rows = x_ref.shape[0] // chunks
-
-    def at(where, which):
-        return {"vk": where // sizes[1], "vh": where % sizes[1], "core": which}
-
-    def neighbour(direction):
-        return chip + 1 if direction == 0 else chip - 1
-
-    def has(direction):
-        return chip < chips - 1 if direction == 0 else chip > 0
-
-    barrier = pltpu.get_barrier_semaphore()
-    pl.semaphore_signal(barrier, inc=1, device_id=at(chip, 1 - core), device_id_type=MESH)
-    for direction in range(2):
-        @pl.when(has(direction))
-        def _():
-            pl.semaphore_signal(
-                barrier, inc=1, device_id=at(neighbour(direction), core), device_id_type=MESH
-            )
-    pl.semaphore_wait(barrier, 1 + jnp.where(has(0), 1, 0) + jnp.where(has(1), 1, 0))
-
-    def slot(origin, which, piece):
-        return out_ref.at[origin * 2 + which, pl.ds(piece * rows, rows)]
-
-    def source(origin, piece, hop):
-        return x_ref.at[pl.ds(piece * rows, rows)] if hop == 0 else slot(origin, core, piece)
-
-    def origin_of(direction, hop):
-        return chip - hop if direction == 0 else chip + hop
-
-    def exists(direction, hop):
-        return chip >= hop if direction == 0 else chip + hop < chips
-
-    def pass_on(direction, hop, piece):
-        origin = origin_of(direction, hop)
-        return pltpu.make_async_remote_copy(
-            src_ref=source(origin, piece, hop),
-            dst_ref=slot(origin, core, piece),
-            send_sem=send_sem.at[direction, hop, piece],
-            recv_sem=recv_sem.at[direction, hop, piece],
-            device_id=at(neighbour(direction), core),
-            device_id_type=MESH,
-        )
-
-    def arrival(direction, hop, piece):
-        origin = origin_of(direction, hop)
-        return pltpu.make_async_remote_copy(
-            src_ref=slot(origin, core, piece),
-            dst_ref=slot(origin, core, piece),
-            send_sem=send_sem.at[direction, hop - 1, piece],
-            recv_sem=recv_sem.at[direction, hop - 1, piece],
-            device_id=at(chip, 1 - core),
-            device_id_type=MESH,
-        )
-
-    def share(origin, piece, hop):
-        return pltpu.make_async_remote_copy(
-            src_ref=source(origin, piece, hop),
-            dst_ref=slot(origin, core, piece),
-            send_sem=share_send.at[origin, piece],
-            recv_sem=share_recv.at[origin, piece],
-            device_id=at(chip, 1 - core),
-            device_id_type=MESH,
-        )
-
-    for piece in range(chunks):
-        for direction in range(2):
-            @pl.when(has(direction))
-            def _():
-                pass_on(direction, 0, piece).start()
-    own = pltpu.make_async_copy(x_ref, out_ref.at[chip * 2 + core], local_sem)
-    own.start()
-    for piece in range(chunks):
-        share(chip, piece, 0).start()
-    for hop in range(1, chips):
-        for piece in range(chunks):
-            for direction in range(2):
-                @pl.when(exists(direction, hop))
-                def _():
-                    arrival(direction, hop, piece).wait_recv()
-                    if hop < chips - 1:
-                        @pl.when(has(direction))
-                        def _():
-                            pass_on(direction, hop, piece).start()
-                    share(origin_of(direction, hop), piece, hop).start()
-    own.wait()
-    for piece in range(chunks):
-        share(chip, piece, 0).wait_send()
-        for direction in range(2):
-            for hop in range(chips):
-                if hop < chips - 1:
-                    @pl.when(jnp.logical_and(exists(direction, hop), has(direction)))
-                    def _():
-                        pass_on(direction, hop, piece).wait_send()
-                if hop > 0:
-                    @pl.when(exists(direction, hop))
-                    def _():
-                        share(origin_of(direction, hop), piece, hop).wait_send()
-        for origin in range(chips):
-            pltpu.make_async_remote_copy(
-                src_ref=slot(origin, 1 - core, piece),
-                dst_ref=slot(origin, 1 - core, piece),
-                send_sem=share_send.at[origin, piece],
-                recv_sem=share_recv.at[origin, piece],
-                device_id=at(chip, 1 - core),
-                device_id_type=MESH,
-            ).wait_recv()
-
-
-def line_gather(x, chunks, collective_id):
-    sizes = tuple(lax.axis_size(name) for name in VIS)
-    chips = sizes[0] * sizes[1]
-    return pl.pallas_call(
-        functools.partial(line_kernel, sizes, chunks),
-        out_shape=jax.ShapeDtypeStruct((2 * chips,) + x.shape, x.dtype),
-        in_specs=[VMEM],
-        out_specs=VMEM,
-        scratch_shapes=[
-            pltpu.SemaphoreType.DMA((2, chips, chunks)),
-            pltpu.SemaphoreType.DMA((2, chips, chunks)),
-            pltpu.SemaphoreType.DMA((chips, chunks)),
-            pltpu.SemaphoreType.DMA((chips, chunks)),
-            pltpu.SemaphoreType.DMA,
-        ],
-        compiler_params=pltpu.CompilerParams(
-            collective_id=collective_id, has_side_effects=True
-        ),
-        cost_estimate=pl.CostEstimate(flops=0, bytes_accessed=70_000_000, transcendentals=0),
-    )(x)
 
 
 def front_kernel(sizes, *refs):
@@ -997,76 +787,353 @@
     )
 
 
-def project_kernel(joined, rows_ref, weight_ref, out_ref, *rest):
-    each = rows_ref.shape[0]
-    rows = rows_ref[...]
-    floats = rows.astype(F32)
-    squares = floats * floats
-    coarse = squares.astype(BF16)
-    fine = (squares - coarse.astype(F32)).astype(BF16)
-    ones = jnp.ones((8, rows.shape[1]), BF16)
-    dims = (((1,), (1,)), ((), ()))
-    sums = lax.dot_general(ones, coarse, dims, preferred_element_type=F32)
-    sums += lax.dot_general(ones, fine, dims, preferred_element_type=F32)
-    for half in range(2):
-        for pair in range(KVH // 2):
-            first = (half * KVH + pair * 2) * HD
-            raw = jnp.dot(
-                rows, weight_ref[:, first : first + 2 * HD], preferred_element_type=F32
-            ).astype(out_ref.dtype)
-            for i in range(2):
-                out_ref[pair * 2 + i, 0, :each, half * HD : (half + 1) * HD] = raw[
-                    :, i * HD : (i + 1) * HD
-                ]
-    for h in range(KVH):
-        if joined:
-            out_ref[h, 0, each:, :] = sums[:, : 2 * HD]
-            for part in range(1, each // (2 * HD)):
-                out_ref[h, 0, each + part : each + part + 1, :] = sums[
-                    :1, part * 2 * HD : (part + 1) * 2 * HD
-                ]
-        else:
-            rest[0][h, 0] = sums
-
-
-def project(rows, weight, parts, joined):
-    count, depth = rows.shape
-    each = count // parts
-    if joined:
-        shapes = [jax.ShapeDtypeStruct((KVH, parts, each + 8, 2 * HD), F32)]
-    else:
-        shapes = [
-            jax.ShapeDtypeStruct((KVH, parts, each, 2 * HD), BF16),
-            jax.ShapeDtypeStruct((KVH, parts, 8, each), F32),
-        ]
-    outs = pl.pallas_call(
-        functools.partial(project_kernel, joined),
-        grid=(parts,),
-        out_shape=shapes,
-        in_specs=[
-            pl.BlockSpec((each, depth), lambda p: (p, 0)),
-            pl.BlockSpec(weight.shape, lambda p: (0, 0)),
+def tail_kernel(sizes, ctxs, mine, shard_rows, *refs):
+    (
+        visual_ref, tgain_ref, dest_ref, row_ref, len_ref, text_ref, wkv_hbm, query_hbm, own_hbm,
+        out_ref,
+        wkv, query_in, query, own_kv, bias, image, own, own_sq, pair_out, pair_in, line_out, line_in,
+        high, summed, mix,
+        load_sem, swap_sem, line_send, line_recv, plane_send, plane_recv, twin_send, twin_recv,
+        send_sem, recv_sem, near_send, near_recv,
+    ) = refs
+    chips, vh = sizes[0] * sizes[1], sizes[1]
+    core, ctx = lax.axis_index("core"), lax.axis_index("ctx")
+    vh_index = lax.axis_index("vh")
+    chip = lax.axis_index("vk") * vh + vh_index
+    me = chip * 2 + core
+    parts = 2 * vh
+    each = visual_ref.shape[0] // parts
+    planes = ctxs * vh
+    plane = ctx * vh + vh_index
+    resp = query_in.shape[0]
+    group = QH // KVH
+
+    def at(where, which):
+        return {"vk": where // vh, "vh": where % vh, "core": which}
+
+    def beside(where):
+        return {"ctx": where // vh, "vh": where % vh}
+
+    def neighbour(direction):
+        return chip + 1 if direction == 0 else chip - 1
+
+    def has(direction):
+        return chip < chips - 1 if direction == 0 else chip > 0
+
+    def remote(src, dst, send, recv, device):
+        return pltpu.make_async_remote_copy(
+            src_ref=src, dst_ref=dst, send_sem=send, recv_sem=recv,
+            device_id=device, device_id_type=MESH,
+        )
+
+    twin = at(chip, 1 - core)
+    lane = pl.multiple_of(me * mine * HD, HD)
+    head = pl.multiple_of(((me * mine) // group) * HD, HD)
+    loads = [
+        pltpu.make_async_copy(wkv_hbm, wkv, load_sem.at[0]),
+        pltpu.make_async_copy(query_hbm.at[:, pl.ds(lane, mine * HD)], query_in, load_sem.at[1]),
+        pltpu.make_async_copy(own_hbm.at[:, pl.ds(head, HD)], own_kv.at[0], load_sem.at[2]),
+        pltpu.make_async_copy(
+            own_hbm.at[:, pl.ds(pl.multiple_of(KVH * HD + head, HD), HD)], own_kv.at[1], load_sem.at[3]
+        ),
+    ]
+    for load in loads:
+        load.start()
+
+    barrier = pltpu.get_barrier_semaphore()
+    pl.semaphore_signal(barrier, inc=1, device_id=twin, device_id_type=MESH)
+    for k in range(1, chips):
+        pl.semaphore_signal(
+            barrier, inc=1, device_id=at((chip + k) % chips, core), device_id_type=MESH
+        )
+    for j in range(1, planes):
+        pl.semaphore_signal(
+            barrier, inc=1, device_id=beside((plane + j) % planes), device_id_type=MESH
+        )
+    pl.semaphore_wait(barrier, chips + planes - 1)
+
+    def token_rows(v, which, write):
+        first = pl.multiple_of((v * 2 + which) * each, each)
+        rows = visual_ref[pl.ds(first, each), :].astype(F32)
+        total = jnp.sum(rows * rows, axis=1, keepdims=True)
+        own_sq[v, 0:1, :each] = jnp.transpose(jnp.broadcast_to(total, (each, 128)))[0:1]
+        scaled = (rows * tgain_ref[...]).astype(BF16)
+        for side in range(2):
+            for pair in range(KVH // 2):
+                begin = (side * KVH + pair * 2) * HD
+                raw = jnp.dot(scaled, wkv[:, begin : begin + 2 * HD], preferred_element_type=F32)
+                for i in range(2):
+                    write((pair * 2 + i) * vh + v, side, raw[:, i * HD : (i + 1) * HD])
+
+    def split(total):
+        coarse = total.astype(BF16).astype(F32)
+        return jnp.concatenate([coarse, total - coarse], axis=0).astype(BF16)
+
+    def joined(block):
+        block = block.astype(F32)
+        return block[:8] + block[8:]
+
+    def write_pair(d, side, value):
+        pair_out[d, :each, side * HD : (side + 1) * HD] = value.astype(BF16)
+
+    def write_own(d, side, value):
+        own[d, :, side * HD : (side + 1) * HD] = value
+
+    own_sq[...] = jnp.zeros_like(own_sq)
+    loads[0].wait()
+    for v in range(vh):
+        token_rows(v, 1 - core, write_pair)
+        for h in range(KVH):
+            pair_out[h * vh + v, each:, :] = split(own_sq[v])
+    swap = remote(pair_out, pair_in, swap_sem.at[0], swap_sem.at[1], twin)
+    swap.start()
+    for v in range(vh):
+        token_rows(v, core, write_own)
+    for load in loads[1:]:
+        load.wait()
+    for j in range(mine):
+        query[j * resp : (j + 1) * resp, :] = query_in[:, j * HD : (j + 1) * HD]
+
+    def line_link(k):
+        d = (chip + k) % chips
+        return remote(
+            line_out.at[d], line_in.at[k], line_send.at[k], line_recv.at[k], at(d, core)
+        )
+
+    swap.wait_recv()
+    for k in range(1, chips):
+        d = (chip + k) % chips
+        line_out[d, :each, :] = (own[d] + pair_in[d, :each, :].astype(F32)).astype(BF16)
+        line_out[d, each:, :] = split(own_sq[d % vh] + joined(pair_in[d, each:, :]))
+        line_link(k).start()
+
+    groups = bias.shape[0] // 128
+    padded = -(-groups // 128) * 128
+    count = jnp.zeros((128, padded), F32)
+    for i in range(dest_ref.shape[0]):
+        flat = dest_ref[i : i + 1, :] * shard_rows + row_ref[i : i + 1, :]
+        low = lax.broadcasted_iota(jnp.int32, (128, flat.shape[1]), 0) == flat % 128
+        upper = lax.broadcasted_iota(jnp.int32, (padded, flat.shape[1]), 0) == flat // 128
+        count += lax.dot_general(
+            jnp.where(low, 1.0, 0.0).astype(BF16), jnp.where(upper, 1.0, 0.0).astype(BF16),
+            (((1,), (1,)), ((), ())), preferred_element_type=F32,
+        )
+    hidden = jnp.where(count > 0.5, -1e30, 0.0)
+    for g in range(groups):
+        bias[g * 128 : (g + 1) * 128, :] = jnp.broadcast_to(hidden[:, g : g + 1], (128, 128))
+
+    high[...] = jnp.full_like(high, -1e30)
+    summed[...] = jnp.zeros_like(summed)
+    mix[...] = jnp.zeros_like(mix)
+    scale = 1.0 / math.sqrt(HD)
+
+    def attend(keys, values, mask):
+        scores = lax.dot_general(
+            keys, query[...], (((1,), (1,)), ((), ())), preferred_element_type=F32
+        ) * scale
+        scores = mask(scores)
+        top = jnp.maximum(high[...], jnp.max(scores, axis=0, keepdims=True))
+        fade = jnp.exp(high[...] - top)
+        expo = jnp.exp(scores - top)
+        high[...] = top
+        summed[...] = summed[...] * fade + jnp.sum(expo, axis=0, keepdims=True)
+        mix[...] = mix[...] * fade + jnp.dot(
+            jnp.transpose(values.astype(F32)).astype(BF16), expo.astype(BF16),
+            preferred_element_type=F32,
+        )
+
+    def causal(scores):
+        key = lax.broadcasted_iota(jnp.int32, scores.shape, 0)
+        place = lax.broadcasted_iota(jnp.int32, scores.shape, 1) % resp
+        return jnp.where(key <= place, scores, -1e30)
+
+    def text_chunk(i, carry):
+        rows = pl.ds(pl.multiple_of(i * KEYS, KEYS), KEYS)
+        attend(text_ref[rows, :HD], text_ref[rows, HD:], lambda scores: scores + bias[rows, 0:1])
+        return carry
+
+    chunks = text_ref.shape[0] // KEYS
+    early = chunks * 3 // 4
+    attend(own_kv[0], own_kv[1], causal)
+    lax.fori_loop(0, early, text_chunk, 0)
+
+    def slot(place, which):
+        return image.at[pl.ds(pl.multiple_of((place * 2 + which) * each, 16), each)]
+
+    def plane_link(j):
+        block = slot(plane, core)
+        return remote(
+            block, block, plane_send.at[j], plane_recv.at[j], beside((plane + j) % planes)
+        )
+
+    def plane_from(j):
+        block = slot((plane - j) % planes, core)
+        return remote(block, block, plane_send.at[j], plane_recv.at[j], twin)
+
+    def twin_link(j, which):
+        block = slot((plane - j) % planes, which)
+        return remote(block, block, twin_send.at[j], twin_recv.at[j], twin)
+
+    for k in range(1, chips):
+        line_link(k).wait_recv()
+    total = own[chip] + pair_in[chip, :each, :].astype(F32)
+    square = own_sq[chip % vh] + joined(pair_in[chip, each:, :])
+    for k in range(1, chips):
+        total += line_in[k, :each, :].astype(F32)
+        square += joined(line_in[k, each:, :])
+    inverse = lax.rsqrt(square / D + EPS)
+    factor = jnp.transpose(jnp.broadcast_to(inverse[0:1, :each], (128, each)))
+    place = pl.multiple_of((plane * 2 + core) * each, 16)
+    for side in range(2):
+        lanes = slice(side * HD, (side + 1) * HD)
+        image[pl.ds(place, each), lanes] = (total[:, lanes] * factor).astype(BF16)
+    for j in range(1, planes):
+        plane_link(j).start()
+    twin_link(0, core).start()
+    lax.fori_loop(early, chunks, text_chunk, 0)
+    for j in range(1, planes):
+        plane_from(j).wait_recv()
+        twin_link(j, core).start()
+    for j in range(planes):
+        twin_link(j, 1 - core).wait_recv()
+
+    def image_chunk(i, carry):
+        rows = pl.ds(pl.multiple_of(i * KEYS, KEYS), KEYS)
+        attend(image[rows, :HD], image[rows, HD:], lambda scores: scores)
+        return carry
+
+    lax.fori_loop(0, image.shape[0] // KEYS, image_chunk, 0)
+
+    piece_width = mine * HD // 2
+
+    def result_slot(origin, which, piece):
+        first = ((origin * 2 + which) * 2 + piece) * piece_width
+        return out_ref.at[:, pl.ds(pl.multiple_of(first, 128), piece_width)]
+
+    def origin_of(direction, hop):
+        return chip - hop if direction == 0 else chip + hop
+
+    def exists(direction, hop):
+        return chip >= hop if direction == 0 else chip + hop < chips
+
+    def pass_on(direction, hop, piece):
+        block = result_slot(origin_of(direction, hop), core, piece)
+        return remote(
+            block, block, send_sem.at[direction, hop, piece], recv_sem.at[direction, hop, piece],
+            at(neighbour(direction), core),
+        )
+
+    def arrival(direction, hop, piece):
+        block = result_slot(origin_of(direction, hop), core, piece)
+        return remote(
+            block, block, send_sem.at[direction, hop - 1, piece],
+            recv_sem.at[direction, hop - 1, piece], twin,
+        )
+
+    def give(origin, piece, which):
+        block = result_slot(origin, which, piece)
+        return remote(
+            block, block, near_send.at[origin, piece], near_recv.at[origin, piece], twin
+        )
+
+    live = lax.broadcasted_iota(jnp.int32, (resp, HD), 0) < len_ref[0]
+    for piece in range(2):
+        for j in range(piece * mine // 2, (piece + 1) * mine // 2):
+            lanes = slice(j * resp, (j + 1) * resp)
+            value = jnp.transpose(mix[:, lanes] / summed[:, lanes])
+            out_ref[:, pl.ds(pl.multiple_of(lane + j * HD, HD), HD)] = jnp.where(
+                live, value, 0.0
+            ).astype(BF16)
+        for direction in range(2):
+            @pl.when(has(direction))
+            def _():
+                pass_on(direction, 0, piece).start()
+        give(chip, piece, core).start()
+    for hop in range(1, chips):
+        for piece in range(2):
+            for direction in range(2):
+                @pl.when(exists(direction, hop))
+                def _():
+                    arrival(direction, hop, piece).wait_recv()
+                    if hop < chips - 1:
+                        @pl.when(has(direction))
+                        def _():
+                            pass_on(direction, hop, piece).start()
+                    give(origin_of(direction, hop), piece, core).start()
+
+    swap.wait_send()
+    for k in range(1, chips):
+        line_link(k).wait_send()
+    for j in range(planes):
+        twin_link(j, core).wait_send()
+        if j:
+            plane_link(j).wait_send()
+    for piece in range(2):
+        for origin in range(chips):
+            give(origin, piece, 1 - core).wait_recv()
+        give(chip, piece, core).wait_send()
+        for direction in range(2):
+            for hop in range(chips):
+                if hop < chips - 1:
+                    @pl.when(jnp.logical_and(exists(direction, hop), has(direction)))
+                    def _():
+                        pass_on(direction, hop, piece).wait_send()
+                if hop > 0:
+                    @pl.when(exists(direction, hop))
+                    def _():
+                        give(origin_of(direction, hop), piece, core).wait_send()
+
+
+def tail(visual, kv_gain, token_dest, token_row, resp_len, text_kv, w_kv, queries, resp_kv, shard_rows, collective_id):
+    sizes = tuple(lax.axis_size(name) for name in VIS)
+    ctxs = lax.axis_size("ctx")
+    chips, planes = sizes[0] * sizes[1], ctxs * sizes[1]
+    each = visual.shape[0] // (2 * sizes[1])
+    mine = QH // (2 * chips)
+    resp = queries.shape[0]
+    block = (chips, each + 16, 2 * HD)
+    DMA = pltpu.SemaphoreType.DMA
+    return pl.pallas_call(
+        functools.partial(tail_kernel, sizes, ctxs, mine, shard_rows),
+        out_shape=jax.ShapeDtypeStruct((resp, QH * HD), BF16),
+        in_specs=[VMEM] * 4 + [pl.BlockSpec(memory_space=pltpu.SMEM), VMEM] + [ANY] * 3,
+        out_specs=VMEM,
+        scratch_shapes=[
+            pltpu.VMEM(w_kv.shape, BF16),
+            pltpu.VMEM((resp, mine * HD), BF16),
+            pltpu.VMEM((mine * resp, HD), BF16),
+            pltpu.VMEM((2, resp, HD), BF16),
+            pltpu.VMEM((ctxs * shard_rows, 128), F32),
+            pltpu.VMEM((planes * 2 * each, 2 * HD), BF16),
+            pltpu.VMEM((chips, each, 2 * HD), F32),
+            pltpu.VMEM((sizes[1], 8, 2 * HD), F32),
+            pltpu.VMEM(block, BF16),
+            pltpu.VMEM(block, BF16),
+            pltpu.VMEM(block, BF16),
+            pltpu.VMEM(block, BF16),
+            pltpu.VMEM((1, mine * resp), F32),
+            pltpu.VMEM((1, mine * resp), F32),
+            pltpu.VMEM((HD, mine * resp), F32),
+            DMA((4,)),
+            DMA((2,)),
+            DMA((chips,)),
+            DMA((chips,)),
+            DMA((planes,)),
+            DMA((planes,)),
+            DMA((planes,)),
+            DMA((planes,)),
+            DMA((2, chips, 2)),
+            DMA((2, chips, 2)),
+            DMA((chips, 2)),
+            DMA((chips, 2)),
         ],
-        out_specs=[
-            pl.BlockSpec((KVH, 1) + shape.shape[2:], lambda p: (0, p, 0, 0)) for shape in shapes
-        ],
-        cost_estimate=pl.CostEstimate(
-            flops=2 * count * depth * KVH * 2 * HD,
-            bytes_accessed=count * depth * 10,
-            transcendentals=0,
+        compiler_params=pltpu.CompilerParams(
+            collective_id=collective_id, has_side_effects=True, vmem_limit_bytes=48 * 2**20
         ),
-    )(rows, weight)
-    return [out.reshape((KVH * parts,) + out.shape[2:]) for out in outs]
-
-
-def whole_image(visual, weight, parts):
-    pieces, squares = project(visual, weight, parts, False)
-    pieces, squares = exchange((pieces, squares), VIS, False, 3)
-    total = jnp.sum(pieces.astype(F32), axis=0)
-    inverse = lax.rsqrt(jnp.sum(squares[:, 0, :], axis=0) / D + EPS)
-    share = (total * inverse[:, None]).astype(BF16)
-    (whole,) = exchange((share,), ("ctx",) + SUB, True, 4)
-    return whole.reshape(-1, 2 * HD)
+    )(
+        visual, kv_gain.reshape(1, -1), token_dest, token_row, resp_len, text_kv, w_kv, queries,
+        resp_kv,
+    )
 
 
 def per_device(
@@ -1085,69 +1152,16 @@
     resp_kv,
     resp_len,
 ):
-    parts = lax.axis_size("vh") * lax.axis_size("core")
-    vis_count = lax.axis_size("vk") * parts
-    ctx_count = lax.axis_size("ctx")
-    vis_index = flat_index(VIS, tuple(lax.axis_size(name) for name in VIS))
-    shard_rows = prompt_text.shape[0]
-
     qkv, gathered, chain_last, text_mine, text_sq = front(
         patches, vis_gain, w_qkv, prompt_text, kv_gain, w_kv, 0
     )
     visual, text_kv = middle(
         qkv, gathered, w_out, merge_gain, w_merge, chain_last, text_mine, text_sq, 1
     )
-    weight = (w_kv.astype(F32) * kv_gain[:, None]).astype(BF16)
-
-    image_kv = whole_image(visual, weight, parts)
-
-    flat = (token_dest * shard_rows + token_row).reshape(-1)
-    positions = jnp.arange(ctx_count * shard_rows, dtype=jnp.int32)
-    taken = jnp.any(positions[:, None] == flat[None, :], axis=1)
-
-    width = KVH * HD
-    group = QH // KVH
-    mine = QH // vis_count
-    resp_rows = queries.shape[0]
-    scale = 1.0 / math.sqrt(HD)
-    query = lax.dynamic_slice_in_dim(queries, vis_index * mine * HD, mine * HD, 1)
-    query = query.reshape(resp_rows, mine, HD).transpose(1, 0, 2).reshape(mine * resp_rows, HD)
-    kv_head = (vis_index * mine) // group
-    own_keys = lax.dynamic_slice_in_dim(resp_kv, kv_head * HD, HD, 1)
-    own_values = lax.dynamic_slice_in_dim(resp_kv, width + kv_head * HD, HD, 1)
-    early_keys = jnp.concatenate([text_kv[:, :HD], own_keys], axis=0)
-    early_values = jnp.concatenate([text_kv[:, HD:], own_values], axis=0)
-    query_positions = jnp.arange(resp_rows, dtype=jnp.int32)
-    causal = query_positions[None, :] <= query_positions[:, None]
-    visible = jnp.concatenate(
-        [jnp.broadcast_to(~taken[None, :], (resp_rows, taken.shape[0])), causal], axis=1
+    return tail(
+        visual, kv_gain, token_dest, token_row, resp_len, text_kv, w_kv, queries, resp_kv,
+        prompt_text.shape[0], 2
     )
-    visible = jnp.broadcast_to(visible[None], (mine,) + visible.shape).reshape(
-        mine * resp_rows, -1
-    )
-
-    def scores_of(keys):
-        return jnp.einsum("qd,kd->qk", query, keys, preferred_element_type=F32) * scale
-
-    scores = jnp.where(visible, scores_of(early_keys), -1e30)
-    early_high = jnp.max(scores, axis=1, keepdims=True)
-    expo = jnp.where(visible, jnp.exp(scores - early_high), 0.0)
-    early_sum = jnp.sum(expo, axis=1, keepdims=True)
-    early_mix = jnp.dot(expo.astype(BF16), early_values, preferred_element_type=F32)
-
-    late_scores = scores_of(image_kv[:, :HD])
-    high = jnp.maximum(early_high, jnp.max(late_scores, axis=1, keepdims=True))
-    late = jnp.exp(late_scores - high)
-    fade = jnp.exp(early_high - high)
-    summed = early_sum * fade + jnp.sum(late, axis=1, keepdims=True)
-    mix = early_mix * fade + jnp.dot(
-        late.astype(BF16), image_kv[:, HD:], preferred_element_type=F32
-    )
-    live = jnp.tile(query_positions < resp_len[0], mine)[:, None]
-    result = jnp.where(live, mix / summed, 0.0).astype(BF16)
-    result = result.reshape(mine, resp_rows, HD).transpose(1, 0, 2)
-    whole = line_gather(result.reshape(resp_rows, mine * HD), 2, 5)
-    return whole.transpose(1, 0, 2).reshape(resp_rows, QH * HD)
 
 
 def solution(mesh):

time: 168 us -> 130 us (0.77)
  Pallas kernels: 139 us -> 124 us
  other arithmetic: 10.9 us -> 0 us
  local copies, waits for them, and re-layouts: 11.5 us -> 5.4 us
  matrix products: 5.5 us -> 0 us
    pallas_call x4 -> x1, Pallas kernels: 49.6 us -> 35.1 us  [tail(): pl.pallas_call(functools.partial(tail_kernel, sizes, ctxs, mine, shard_ro...]
    reduce_sum x4 -> x0, other arithmetic: 6.32 us -> none  [the longest x1 3.88 us: per_device(): early_sum = jnp.sum(expo, axis=1, keepdims=True)]
    dot_general x4 -> x0, matrix products: 5.5 us -> none  [the longest x2 3.65 us: scores_of(): jnp.einsum('qd,kd->qk', query, keys, preferred_element_type=F32) * scale]
    convert_element_type x2 -> x0, other arithmetic: 2.45 us -> none  [the longest x1 1.72 us: per_device(): weight = (w_kv.astype(F32) * kv_gain[:, None]).astype(BF16)]
    reduce_or x1 -> x0, other arithmetic: 1.97 us -> none  [per_device(): taken = jnp.any(positions[:, None] == flat[None, :], axis=1)]
    slice x1 -> x0, local copies, waits for them, and re-layouts: 1.88 us -> none  [per_device(): early_values = jnp.concatenate([text_kv[:, HD:], own_values], axis=0)]
    transpose x2 -> x0, local copies, waits for them, and re-layouts: 1.75 us -> none  [the longest x1 1.62 us: per_device(): return whole.transpose(1, 0, 2).reshape(resp_rows, QH * HD)]
    unnamed x28 -> x24, local copies, waits for them, and re-layouts: 4.93 us -> 5.39 us
where the time goes in v2:
time: 130 us
  Pallas kernels  124 us (95%)
  local copies, waits for them, and re-layouts  5.4 us (4%)
    pallas_call x1, Pallas kernels, middle(): pl.pallas_call(functools.partial(middle_kernel, sizes, ctxs), out_shape=[...  57.2 us
    pallas_call x1, Pallas kernels, tail(): pl.pallas_call(functools.partial(tail_kernel, sizes, ctxs, mine, shard_ro...  35.1 us
    pallas_call x1, Pallas kernels, front(): pl.pallas_call(functools.partial(front_kernel, sizes), out_shape=[jax.Sha...  31.8 us
    unnamed x24, local copies, waits for them, and re-layouts  5.39 us

profile of v2, /device:TPU:0, one launch (start us, length us, event | category | flops | bytes accessed | tf_op | source)
XLA Modules:
  0.0 130.3 jit_solution(6159968093490923539)
XLA Ops:
  0.0 0.0 copy-start.6
  0.0 0.0 copy-start.9
  0.0 0.0 copy-start.4
  0.0 1.6 %copy.15.refs_3_ = bf16[1280,480]{1,0:T(8,128)(2,1)S(1)} copy(bf16[1280,480]{0,1:T(8,128)(2,1)} %param.16) | data formatting | bytes 2457600 | tf_op args[2]
  1.6 0.0 copy-done.9
  1.7 0.0 copy-done.6
  1.7 0.0 copy-done.4
  1.7 0.0 copy-start.10
  1.7 0.0 copy-start.3
  1.7 31.8 %shard_map.136 = (bf16[1024,768]{1,0:T(8,128)(2,1)S(1)}, bf16[8,128,1280]{2,1,0:T(8,128)(2,1)}, bf16[2,528,256]{2,1,0:T(8,128)(2,1)S(1)}, f32[512,256]{1,0:T(8,128)S(1)}, f32[8,256]{1,0:T(8,128)S(1)}) custom-call(bf16[128,1280]{1,0:T(8,128)(2,1)S(1)} %copy-done.4, f32[1,1280]{1,0:T(1,128)S(1)} %reshape.13.refs_1_, f32[1,1024]{1,0:T(1,128)S(1)} %bitcast.2, ...), custom_call_target="tpu_custom_call" | custom-call | tf_op jit(solution)/shard_map/pallas_call | solution.py:324
  33.6 0.0 copy-start.1
  33.6 1.2 copy-done.1
  34.7 0.0 copy-done.10
  34.7 0.0 copy-done.3
  34.7 0.0 copy-start.2
  34.8 0.0 copy-start.5
  34.8 0.0 copy-start.7
  34.8 0.0 copy-start.8
  34.8 57.2 %shard_map.137 = (bf16[256,1024]{1,0:T(8,128)(2,1)S(1)}, bf16[4096,256]{1,0:T(8,128)(2,1)}) custom-call(bf16[1024,768]{1,0:T(8,128)(2,1)} %copy-done.1, bf16[1024,1280]{1,0:T(8,128)(2,1)} %bitcast.4, bf16[160,1280]{1,0:T(8,128)(2,1)S(1)} %copy-done.3, f32[1,1280]{1,0:T(1,128)S(1)} %reshape.16.refs_3_, bf16[2,528,256]{2,1,0:T(8,128)(2,1)S(1)} %get-tuple-element.14.refs_4_, ...), custom_call_target="tpu_custom_call" | custom-call | tf_op jit(solution)/shard_map/pallas_call | solution.py:747
  92.6 0.0 copy-done.2
  92.6 0.0 copy-done.5
  92.6 0.0 copy-done.7
  92.6 0.0 copy-done.8
  92.7 0.0 copy-start
  92.7 1.6 %copy-done = bf16[4096,256]{1,0:T(8,128)(2,1)S(1)} copy-done((bf16[4096,256]{1,0:T(8,128)(2,1)S(1)}, bf16[4096,256]{1,0:T(8,128)(2,1)}, u32[]{:S(2)}) %copy-start) | copy-done | bytes 2097176
  94.2 35.1 %shard_map.138 = bf16[128,4096]{1,0:T(8,128)(2,1)S(1)} custom-call(bf16[256,1024]{1,0:T(8,128)(2,1)S(1)} %get-tuple-element.17.refs_0_, f32[1,1024]{1,0:T(1,128)S(1)} %bitcast.3, s32[4,256]{1,0:T(4,128)S(1)} %copy-done.7, s32[4,256]{1,0:T(4,128)S(1)} %copy-done.8, s32[1]{0:T(128)S(6)} %copy.17.refs_4_, bf16[4096,256]{1,0:T(8,128)(2,1)S(1)} %copy-done, ...), custom_call_target="tpu_custom_call" | custom-call | tf_op jit(solution)/shard_map/pallas_call | solution.py:1096
  129.3 1.0 copy.18
  (2 shorter events, 0.0 us)
Async XLA Ops:
  0.0 1.7 %copy-start.6 = (f32[1024]{0:T(1024)S(1)}, f32[1024]{0:T(1024)}, u32[]{:S(2)}) copy-start(f32[1024]{0:T(1024)} %param.23) | copy-start | bytes 12292
  0.0 1.6 %copy-start.9 = (f32[1280]{0:T(1024)S(1)}, f32[1280]{0:T(1024)}, u32[]{:S(2)}) copy-start(f32[1280]{0:T(1024)} %param.15) | copy-start | bytes 15364
  0.0 1.7 %copy-start.4 = (bf16[128,1280]{1,0:T(8,128)(2,1)S(1)}, bf16[128,1280]{1,0:T(8,128)(2,1)}, u32[]{:S(2)}) copy-start(bf16[128,1280]{1,0:T(8,128)(2,1)} %refs_0_.1) | copy-start | bytes 983044
  1.7 33.0 %copy-start.10 = (f32[1280]{0:T(1024)S(1)}, f32[1280]{0:T(1024)}, u32[]{:S(2)}) copy-start(f32[1280]{0:T(1024)} %param.18) | copy-start | bytes 15364
  1.7 33.0 %copy-start.3 = (bf16[160,1280]{1,0:T(8,128)(2,1)S(1)}, bf16[160,1280]{1,0:T(8,128)(2,1)}, u32[]{:S(2)}) copy-start(bf16[160,1280]{1,0:T(8,128)(2,1)} %refs_2_.2) | copy-start | bytes 1228804
  33.6 1.2 copy-start.1
  34.7 57.9 %copy-start.2 = (bf16[128,4096]{1,0:T(8,128)(2,1)S(1)}, bf16[128,4096]{1,0:T(8,128)(2,1)}, u32[]{:S(2)}) copy-start(bf16[128,4096]{1,0:T(8,128)(2,1)} %refs_7_.3) | copy-start | bytes 3145732
  34.8 57.9 %copy-start.5 = (bf16[128,1024]{1,0:T(8,128)(2,1)S(1)}, bf16[128,1024]{1,0:T(8,128)(2,1)}, u32[]{:S(2)}) copy-start(bf16[128,1024]{1,0:T(8,128)(2,1)} %refs_8_.1) | copy-start | bytes 786436
  34.8 57.9 %copy-start.7 = (s32[4,256]{1,0:T(4,128)S(1)}, s32[4,256]{1,0:T(4,128)}, u32[]{:S(2)}) copy-start(s32[4,256]{1,0:T(4,128)} %refs_2_.3) | copy-start | bytes 12292
  34.8 57.9 %copy-start.8 = (s32[4,256]{1,0:T(4,128)S(1)}, s32[4,256]{1,0:T(4,128)}, u32[]{:S(2)}) copy-start(s32[4,256]{1,0:T(4,128)} %refs_3_.2) | copy-start | bytes 12292
  92.7 1.6 %copy-start = (bf16[4096,256]{1,0:T(8,128)(2,1)S(1)}, bf16[4096,256]{1,0:T(8,128)(2,1)}, u32[]{:S(2)}) copy-start(bf16[4096,256]{1,0:T(8,128)(2,1)} %get-tuple-element.18.refs_5_) | copy-start | bytes 6291460

commit v3 on v2

--- a/solution.py
+++ b/solution.py
@@ -22,6 +22,7 @@
 MESH = pl.DeviceIdType.MESH
 VMEM = pl.BlockSpec(memory_space=pltpu.VMEM)
 ANY = pl.BlockSpec(memory_space=pl.ANY)
+HBM = pl.BlockSpec(memory_space=pltpu.MemorySpace.HBM)
 F32 = jnp.float32
 BF16 = jnp.bfloat16
 PIECES = 2
@@ -41,7 +42,7 @@
     (
         patches_ref, gain_ref, tgain_ref, wqkv_hbm, text_hbm, wkv_hbm,
         qkv_ref, held, chain_last, mine_ref, mine_sq,
-        wqkv, wpad, text, wkv, normed, own, own_sq, pair_out, pair_in, chain_out, chain_in,
+        wpad, text, wkv, normed, own, own_sq, pair_out, pair_in, chain_out, chain_in,
         load_sem, send_sem, recv_sem, near_send, near_recv, pair_sem, chain_send, chain_recv,
     ) = refs
     chips, vh = sizes[0] * sizes[1], sizes[1]
@@ -70,7 +71,12 @@
     loads = [
         pltpu.make_async_copy(text_hbm, text, load_sem.at[0]),
         pltpu.make_async_copy(wkv_hbm, wkv, load_sem.at[1]),
-        pltpu.make_async_copy(wqkv_hbm, wqkv, load_sem.at[2]),
+    ] + [
+        pltpu.make_async_copy(
+            wqkv_hbm.at[pl.ds(part * VHD, VHD)], wpad.at[pl.ds(part * 128, VHD)],
+            load_sem.at[2 + part],
+        )
+        for part in range(wqkv_hbm.shape[0] // VHD)
     ]
     for load in loads:
         load.start()
@@ -130,7 +136,7 @@
             @pl.when(has(direction))
             def _():
                 pass_on(direction, 0, piece).start()
-    mine = pltpu.make_async_copy(patches_ref, held.at[chip * 2 + core], load_sem.at[3])
+    mine = pltpu.make_async_copy(patches_ref, held.at[chip * 2 + core], load_sem.at[len(loads)])
     mine.start()
     for piece in range(PIECES):
         give(chip, piece, 0).start()
@@ -188,10 +194,9 @@
     for v in range(vh):
         text_rows(v, core, write_own)
 
-    loads[2].wait()
-    wpad[...] = jnp.zeros_like(wpad)
-    for part in range(wqkv.shape[1] // VHD):
-        wpad[:, part * 128 : part * 128 + VHD] = wqkv[:, part * VHD : (part + 1) * VHD]
+    for part, load in enumerate(loads[2:]):
+        wpad[part * 128 + VHD : (part + 1) * 128, :] = jnp.zeros((128 - VHD, wpad.shape[1]), BF16)
+        load.wait()
 
     def project(origin):
         def norm_rows(i, carry):
@@ -204,8 +209,8 @@
 
         lax.fori_loop(0, 2 * count // LNROWS, norm_rows, 0)
         first = pl.multiple_of(origin * 2 * count, 2 * count)
-        qkv_ref[pl.ds(first, 2 * count), :] = jnp.dot(
-            normed[...], wpad[...], preferred_element_type=F32
+        qkv_ref[pl.ds(first, 2 * count), :] = lax.dot_general(
+            normed[...], wpad[...], (((1,), (1,)), ((), ())), preferred_element_type=F32
         ).astype(BF16)
 
     def project_hop(hop):
@@ -309,6 +314,10 @@
             @pl.when(chip < d - 1 if direction == 0 else chip > d + 1)
             def _():
                 link(direction, d).wait_send()
+
+
+def in_hbm(array):
+    return pltpu.with_memory_space_constraint(array, pltpu.MemorySpace.HBM)
 
 
 def front(patches, vis_gain, w_qkv, text, kv_gain, w_kv, collective_id):
@@ -330,11 +339,10 @@
             jax.ShapeDtypeStruct((each, 2 * HD), F32),
             jax.ShapeDtypeStruct((8, SUBROWS), F32),
         ],
-        in_specs=[VMEM] * 3 + [ANY] * 3,
+        in_specs=[VMEM] * 3 + [HBM] * 3,
         out_specs=[VMEM] * 5,
         scratch_shapes=[
-            pltpu.VMEM(w_qkv.shape, BF16),
-            pltpu.VMEM((width, heads3 * 128), BF16),
+            pltpu.VMEM((heads3 * 128, width), BF16),
             pltpu.VMEM(text.shape, BF16),
             pltpu.VMEM(w_kv.shape, BF16),
             pltpu.VMEM((2 * count, width), BF16),
@@ -344,7 +352,7 @@
             pltpu.VMEM((chips,) + block, BF16),
             pltpu.VMEM((2, chips) + block, BF16),
             pltpu.VMEM((2, chips) + block, BF16),
-            DMA((4,)),
+            DMA((3 + heads3,)),
             DMA((2, chips, PIECES)),
             DMA((2, chips, PIECES)),
             DMA((chips, PIECES)),
@@ -354,9 +362,9 @@
             DMA((2, chips)),
         ],
         compiler_params=pltpu.CompilerParams(
-            collective_id=collective_id, has_side_effects=True, vmem_limit_bytes=48 * 2**20
+            collective_id=collective_id, has_side_effects=True, vmem_limit_bytes=40 * 2**20
         ),
-    )(patches, vis_gain.reshape(1, -1), kv_gain.reshape(1, -1), w_qkv, text, w_kv)
+    )(patches, vis_gain.reshape(1, -1), kv_gain.reshape(1, -1), *map(in_hbm, (w_qkv.T, text, w_kv)))
 
 
 def spread_of(rows, width, places):
@@ -372,12 +380,12 @@
 
 def middle_kernel(sizes, ctxs, *refs):
     (
-        qkv_ref, patches_ref, wout_ref, gain_ref, chain_ref, mine_ref, sq_ref, wmerge_hbm,
-        visual_ref, text_ref,
-        held, wall, wmerge, mixed, merged, values, chain_in,
-        load_sem, send_sem, recv_sem, near_send, near_recv, chain_send, chain_recv,
+        qkv_ref, wout_ref, gain_ref, chain_ref, mine_ref, sq_ref, patches_hbm, wmerge_hbm,
+        visual_ref, share_ref,
+        patches, held, wall, wmerge, mixed, merged, token_sum, values, staged, chain_in,
+        load_sem, send_sem, recv_sem, near_send, near_recv, merge_send, merge_recv,
+        chain_send, chain_recv,
         line_send, line_recv, plane_send, plane_recv, pair_send, pair_recv,
-        text_send, text_recv, twin_send, twin_recv,
     ) = refs
     chips, vh = sizes[0] * sizes[1], sizes[1]
     core, ctx = lax.axis_index("core"), lax.axis_index("ctx")
@@ -388,7 +396,8 @@
     subs = each // SUBROWS
     deep, width = wout_ref.shape
     total = qkv_ref.shape[0]
-    blocks = total // LANES
+    half = total // 2
+    blocks = half // LANES
     heads = deep // VHD
     planes = ctxs * vh
     plane = ctx * vh + vh_index
@@ -412,6 +421,9 @@
         )
 
     twin = at(chip, 1 - core)
+    my_half = pl.ds(pl.multiple_of(core * half, LANES), half)
+    fetch = pltpu.make_async_copy(patches_hbm.at[my_half], patches, load_sem.at[2])
+    fetch.start()
     load = pltpu.make_async_copy(wmerge_hbm, wmerge, load_sem.at[0])
     load.start()
     my_rows = pl.ds(pl.multiple_of(me * deep, 16), deep)
@@ -436,11 +448,6 @@
             chain_send.at[direction], chain_recv.at[direction], at(neighbour(direction), core),
         )
 
-    for direction in range(2):
-        @pl.when(has(direction))
-        def _():
-            last_link(direction).start()
-
     down, across = spread_of(deep, width, ctxs)
     used, high, wide = down * across, deep // down, width // across
 
@@ -476,9 +483,12 @@
             line_part(k).start()
     own_to_twin().start()
 
-    def slot(origin, which, piece):
-        first = pl.multiple_of((origin * 2 + which) * deep, 16)
-        return held.at[pl.ds(first, deep), pl.ds(pl.multiple_of(piece * LANES, LANES), LANES)]
+    def lanes_of(piece):
+        return pl.ds(pl.multiple_of(piece * LANES, LANES), LANES)
+
+    def slot(origin, piece):
+        first = pl.multiple_of(origin * 2 * deep, 16)
+        return held.at[pl.ds(first, 2 * deep), lanes_of(piece)]
 
     def origin_of(direction, hop):
         return chip - hop if direction == 0 else chip + hop
@@ -487,35 +497,40 @@
         return chip >= hop if direction == 0 else chip + hop < chips
 
     def pass_on(direction, hop, piece):
-        block = slot(origin_of(direction, hop), core, piece)
+        block = slot(origin_of(direction, hop), piece)
         return remote(
             block, block, send_sem.at[direction, hop, piece], recv_sem.at[direction, hop, piece],
             at(neighbour(direction), core),
         )
 
     def arrival(direction, hop, piece):
-        block = slot(origin_of(direction, hop), core, piece)
+        block = slot(origin_of(direction, hop), piece)
         return remote(
             block, block, send_sem.at[direction, hop - 1, piece],
             recv_sem.at[direction, hop - 1, piece], twin,
         )
 
-    def give(origin, piece, which):
-        block = slot(origin, which, piece)
-        return remote(
-            block, block, near_send.at[origin, piece], near_recv.at[origin, piece], twin
-        )
+    def give(piece):
+        return remote(
+            staged.at[:, lanes_of(piece)], held.at[my_rows, lanes_of(piece)],
+            near_send.at[piece], near_recv.at[piece], twin,
+        )
+
+    def taken(piece):
+        first = pl.multiple_of((chip * 2 + 1 - core) * deep, 16)
+        block = held.at[pl.ds(first, deep), lanes_of(piece)]
+        return remote(block, block, near_send.at[piece], near_recv.at[piece], twin)
 
     scale = 1.0 / math.sqrt(VHD)
     for h in range(heads):
         first = (h * 3 + 2) * 128
         values[h] = jnp.transpose(qkv_ref[:, first : first + 128].astype(F32)).astype(BF16)
 
-    def attend(b, carry):
-        lanes = pl.ds(pl.multiple_of(b * LANES, LANES), LANES)
+    def attend(piece, side, put):
+        places = pl.ds(pl.multiple_of(side * half + piece * LANES, LANES), LANES)
         for h in range(heads):
             first = h * 3 * 128
-            query = qkv_ref[lanes, first : first + 128]
+            query = qkv_ref[places, first : first + 128]
             keys = qkv_ref[:, first + 128 : first + 256]
             scores = lax.dot_general(
                 keys, query, (((1,), (1,)), ((), ())), preferred_element_type=F32
@@ -523,16 +538,31 @@
             expo = jnp.exp(scores - jnp.max(scores, axis=0, keepdims=True))
             summed = jnp.sum(expo, axis=0, keepdims=True)
             mix = jnp.dot(values[h], expo.astype(BF16), preferred_element_type=F32)
+            put(h, (mix[:VHD] / summed).astype(BF16))
+
+    def attend_far(piece, carry):
+        def put(h, value):
+            staged[h * VHD : (h + 1) * VHD, lanes_of(piece)] = value
+
+        attend(piece, 1 - core, put)
+        give(piece).start()
+        return carry
+
+    def attend_near(piece, carry):
+        def put(h, value):
             rows = pl.ds(pl.multiple_of(me * deep + h * VHD, 16), VHD)
-            held[rows, lanes] = (mix[:VHD] / summed).astype(BF16)
+            held[rows, lanes_of(piece)] = value
+
+        attend(piece, core, put)
+        taken(piece).wait_recv()
         for direction in range(2):
             @pl.when(has(direction))
             def _():
-                pass_on(direction, 0, b).start()
-        give(chip, b, core).start()
+                pass_on(direction, 0, piece).start()
         return carry
 
-    lax.fori_loop(0, blocks, attend, 0)
+    lax.fori_loop(0, blocks, attend_far, 0)
+    lax.fori_loop(0, blocks, attend_near, 0)
 
     def relay(hop):
         def body(piece, carry):
@@ -544,27 +574,9 @@
                         @pl.when(has(direction))
                         def _():
                             pass_on(direction, hop, piece).start()
-                    give(origin_of(direction, hop), piece, core).start()
             return carry
 
         lax.fori_loop(0, blocks, body, 0)
-
-    def text_slot(place, which):
-        return text_ref.at[pl.ds(pl.multiple_of((place * 2 + which) * each, 16), each)]
-
-    def text_link(j):
-        block = text_slot(plane, core)
-        return remote(
-            block, block, text_send.at[j], text_recv.at[j], beside((plane + j) % planes)
-        )
-
-    def text_from(j):
-        block = text_slot((plane - j) % planes, core)
-        return remote(block, block, text_send.at[j], text_recv.at[j], twin)
-
-    def text_twin(j, which):
-        block = text_slot((plane - j) % planes, which)
-        return remote(block, block, twin_send.at[j], twin_recv.at[j], twin)
 
     def untail(block):
         block = block.astype(F32)
@@ -593,21 +605,11 @@
         inverse = lax.rsqrt(squares[...] / D + EPS)
         for s in range(subs):
             factor = jnp.transpose(jnp.broadcast_to(inverse[s : s + 1], (128, SUBROWS)))
-            place = pl.multiple_of((plane * 2 + core) * each + s * SUBROWS, 16)
             for side in range(2):
                 lanes = slice(side * HD, (side + 1) * HD)
-                value = mine_sum[s * SUBROWS : (s + 1) * SUBROWS, lanes] * factor
-                text_ref[pl.ds(place, SUBROWS), lanes] = value.astype(BF16)
-
-    mine_sum = squares = None
-    pl.run_scoped(
-        finish_text, pltpu.VMEM((each, 2 * HD), F32), pltpu.VMEM((8, SUBROWS), F32)
-    )
-    for j in range(1, planes):
-        text_link(j).start()
-    text_twin(0, core).start()
-
-    relay(1)
+                rows = slice(s * SUBROWS, (s + 1) * SUBROWS)
+                share_ref[rows, lanes] = (mine_sum[rows, lanes] * factor).astype(BF16)
+
     for k in range(1, chips):
         @pl.when(ctx < used)
         def _():
@@ -615,6 +617,8 @@
             for j in range(1, ctxs):
                 from_line(k, j).start()
             to_twin(k, 0, core).start()
+    relay(1)
+    mine_sum = squares = None
 
     def add_chip(origin, fresh):
         rows = pl.ds(pl.multiple_of(origin * 2 * deep, 16), 2 * deep)
@@ -626,7 +630,7 @@
                 preferred_element_type=F32,
             )
             if fresh:
-                product += patches_ref[places, :].astype(F32)
+                product += patches[places, :].astype(F32)
             for c in range(width // 128):
                 lanes = product[:, c * 128 : (c + 1) * 128]
                 mixed[c, places, :] = lanes if fresh else mixed[c, places, :] + lanes
@@ -638,19 +642,22 @@
         for direction in range(2 if hop else 1):
             @pl.when(exists(direction, hop))
             def _():
-                origin = origin_of(direction, hop)
-                for piece in range(blocks):
-                    give(origin, piece, 1 - core).wait_recv()
-                add_chip(origin, hop == 0)
+                add_chip(origin_of(direction, hop), hop == 0)
 
     keep.wait()
+    fetch.wait()
     own_to_twin().wait_recv()
     add_hop(0)
+    def last_sends():
+        for direction in range(2):
+            @pl.when(has(direction))
+            def _():
+                last_link(direction).start()
+
     if chips > 2:
         relay(2)
-    for j in range(1, planes):
-        text_from(j).wait_recv()
-        text_twin(j, core).start()
+    if chips < 5:
+        last_sends()
     for k in range(1, chips):
         for j in range(1, ctxs):
             @pl.when((ctx - j) % ctxs < used)
@@ -667,40 +674,52 @@
                 to_twin(k, j, 1 - core).wait_recv()
     add_hop(1)
     for hop in range(3, chips):
+        add_hop(hop - 1)
         relay(hop)
-        add_hop(hop - 1)
+        if hop == chips - 2:
+            last_sends()
     if chips > 2:
         add_hop(chips - 1)
 
-    load.wait()
-    tokens = total // 4
+    tokens = half // 4
+    my_tokens = pl.ds(pl.multiple_of(core * tokens, LNROWS), tokens)
+
+    def merge_link(r, which):
+        block = merged.at[r, pl.ds(pl.multiple_of(which * tokens, LNROWS), tokens)]
+        return remote(block, block, merge_send.at[r], merge_recv.at[r], twin)
+
     for r in range(4):
         def norm_rows(i, carry):
             every = pl.ds(i * 4 * LNROWS + r, LNROWS, stride=4)
             rows = jnp.concatenate([mixed[c, every, :] for c in range(width // 128)], axis=1)
-            place = pl.ds(pl.multiple_of(i * LNROWS, LNROWS), LNROWS)
+            place = pl.ds(pl.multiple_of(core * tokens + i * LNROWS, LNROWS), LNROWS)
             merged[r, place, :] = layer_norm(rows, gain_ref[...]).astype(BF16)
             return carry
 
         lax.fori_loop(0, tokens // LNROWS, norm_rows, 0)
-
-    def column(c, carry):
-        lanes = pl.ds(pl.multiple_of(c * LANES, LANES), LANES)
-        value = jnp.dot(merged[0], wmerge[:width, lanes], preferred_element_type=F32)
-        for r in range(1, 4):
-            value += jnp.dot(
+        merge_link(r, core).start()
+    load.wait()
+    for r in range(4):
+        merge_link(r, 1 - core).wait_recv()
+
+        def column(c, carry):
+            lanes = pl.ds(pl.multiple_of(c * LANES, LANES), LANES)
+            value = jnp.dot(
                 merged[r], wmerge[r * width : (r + 1) * width, lanes], preferred_element_type=F32
             )
-        visual_ref[:, lanes] = value.astype(BF16)
-        return carry
-
-    lax.fori_loop(0, visual_ref.shape[1] // LANES, column, 0)
-
-    for j in range(planes):
-        text_twin(j, 1 - core).wait_recv()
-        text_twin(j, core).wait_send()
-        if j:
-            text_link(j).wait_send()
+            if r:
+                value += token_sum[:, lanes]
+            if r < 3:
+                token_sum[:, lanes] = value
+            else:
+                visual_ref[:, lanes] = value.astype(BF16)
+            return carry
+
+        lax.fori_loop(0, visual_ref.shape[1] // LANES, column, 0)
+
+    pl.run_scoped(
+        finish_text, pltpu.VMEM((each, 2 * HD), F32), pltpu.VMEM((8, SUBROWS), F32)
+    )
     own_to_twin().wait_send()
     for k in range(1, chips):
         @pl.when(ctx < used)
@@ -717,18 +736,16 @@
         def _():
             last_link(direction).wait_send()
 
+    for r in range(4):
+        merge_link(r, core).wait_send()
+
     def drain(piece, carry):
-        give(chip, piece, core).wait_send()
+        give(piece).wait_send()
         for direction in range(2):
-            for hop in range(chips):
-                if hop < chips - 1:
-                    @pl.when(jnp.logical_and(exists(direction, hop), has(direction)))
-                    def _():
-                        pass_on(direction, hop, piece).wait_send()
-                if hop > 0:
-                    @pl.when(exists(direction, hop))
-                    def _():
-                        give(origin_of(direction, hop), piece, core).wait_send()
+            for hop in range(chips - 1):
+                @pl.when(jnp.logical_and(exists(direction, hop), has(direction)))
+                def _():
+                    pass_on(direction, hop, piece).wait_send()
         return carry
 
     lax.fori_loop(0, blocks, drain, 0)
@@ -740,7 +757,8 @@
     chips, planes = sizes[0] * sizes[1], ctxs * sizes[1]
     total, width = qkv.shape[0], w_out.shape[1]
     each = mine.shape[0]
-    blocks = total // LANES
+    half = total // 2
+    blocks = half // LANES
     heads = w_out.shape[0] // VHD
     tokens = total // 4
     DMA = pltpu.SemaphoreType.DMA
@@ -748,23 +766,28 @@
         functools.partial(middle_kernel, sizes, ctxs),
         out_shape=[
             jax.ShapeDtypeStruct((tokens, w_merge.shape[1]), BF16),
-            jax.ShapeDtypeStruct((planes * 2 * each, 2 * HD), BF16),
+            jax.ShapeDtypeStruct((each, 2 * HD), BF16),
         ],
-        in_specs=[VMEM] * 7 + [ANY],
+        in_specs=[VMEM] * 6 + [ANY] * 2,
         out_specs=[VMEM] * 2,
         scratch_shapes=[
-            pltpu.VMEM((VD, total), BF16),
+            pltpu.VMEM((half, width), BF16),
+            pltpu.VMEM((VD, half), BF16),
             pltpu.VMEM((VD, width), BF16),
             pltpu.VMEM(w_merge.shape, BF16),
-            pltpu.VMEM((width // 128, total, 128), F32),
+            pltpu.VMEM((width // 128, half, 128), F32),
             pltpu.VMEM((4, tokens, width), BF16),
+            pltpu.VMEM((tokens, w_merge.shape[1]), F32),
             pltpu.VMEM((heads, 128, total), BF16),
+            pltpu.VMEM((w_out.shape[0], half), BF16),
             pltpu.VMEM(chain_last.shape, BF16),
-            DMA((2,)),
+            DMA((3,)),
             DMA((2, chips, blocks)),
             DMA((2, chips, blocks)),
-            DMA((chips, blocks)),
-            DMA((chips, blocks)),
+            DMA((blocks,)),
+            DMA((blocks,)),
+            DMA((4,)),
+            DMA((4,)),
             DMA((2,)),
             DMA((2,)),
             DMA((chips,)),
@@ -773,28 +796,24 @@
             DMA((chips, ctxs)),
             DMA((chips, ctxs)),
             DMA((chips, ctxs)),
-            DMA((planes,)),
-            DMA((planes,)),
-            DMA((planes,)),
-            DMA((planes,)),
         ],
         compiler_params=pltpu.CompilerParams(
-            collective_id=collective_id, has_side_effects=True, vmem_limit_bytes=52 * 2**20
+            collective_id=collective_id, has_side_effects=True, vmem_limit_bytes=40 * 2**20
         ),
     )(
-        qkv, gathered.reshape(total, width), w_out, merge_gain.reshape(1, -1), chain_last, mine,
-        mine_sq, w_merge,
+        qkv, w_out, merge_gain.reshape(1, -1), chain_last, mine, mine_sq,
+        gathered.reshape(total, width), w_merge,
     )
 
 
 def tail_kernel(sizes, ctxs, mine, shard_rows, *refs):
     (
-        visual_ref, tgain_ref, dest_ref, row_ref, len_ref, text_ref, wkv_hbm, query_hbm, own_hbm,
+        visual_ref, tgain_ref, dest_ref, row_ref, len_ref, share_ref, wkv_hbm, query_hbm, own_hbm,
         out_ref,
-        wkv, query_in, query, own_kv, bias, image, own, own_sq, pair_out, pair_in, line_out, line_in,
+        wkv, query_in, query, own_kv, bias, text, image, own, own_sq, pair_out, pair_in, line_out, line_in,
         high, summed, mix,
         load_sem, swap_sem, line_send, line_recv, plane_send, plane_recv, twin_send, twin_recv,
-        send_sem, recv_sem, near_send, near_recv,
+        text_send, text_recv, pass_send, pass_recv, send_sem, recv_sem, near_send, near_recv,
     ) = refs
     chips, vh = sizes[0] * sizes[1], sizes[1]
     core, ctx = lax.axis_index("core"), lax.axis_index("ctx")
@@ -851,6 +870,32 @@
             barrier, inc=1, device_id=beside((plane + j) % planes), device_id_type=MESH
         )
     pl.semaphore_wait(barrier, chips + planes - 1)
+
+    rows_text = share_ref.shape[0]
+
+    def text_slot(place, which):
+        return text.at[pl.ds(pl.multiple_of((place * 2 + which) * rows_text, 16), rows_text)]
+
+    def text_link(j):
+        return remote(
+            share_ref, text_slot(plane, core), text_send.at[j], text_recv.at[j],
+            beside((plane + j) % planes),
+        )
+
+    def text_from(j):
+        block = text_slot((plane - j) % planes, core)
+        return remote(block, block, text_send.at[j], text_recv.at[j], twin)
+
+    def text_twin(j, which):
+        block = text_slot((plane - j) % planes, which)
+        return remote(block, block, pass_send.at[j], pass_recv.at[j], twin)
+
+    def text_own():
+        return remote(share_ref, text_slot(plane, core), pass_send.at[0], pass_recv.at[0], twin)
+
+    for j in range(1, planes):
+        text_link(j).start()
+    text_own().start()
 
     def token_rows(v, which, write):
         first = pl.multiple_of((v * 2 + which) * each, each)
@@ -947,15 +992,17 @@
         place = lax.broadcasted_iota(jnp.int32, scores.shape, 1) % resp
         return jnp.where(key <= place, scores, -1e30)
 
-    def text_chunk(i, carry):
-        rows = pl.ds(pl.multiple_of(i * KEYS, KEYS), KEYS)
-        attend(text_ref[rows, :HD], text_ref[rows, HD:], lambda scores: scores + bias[rows, 0:1])
-        return carry
-
-    chunks = text_ref.shape[0] // KEYS
-    early = chunks * 3 // 4
+    def text_rows(place, which):
+        first = (place * 2 + which) * rows_text
+        rows = pl.ds(pl.multiple_of(first, 128), rows_text)
+        attend(text[rows, :HD], text[rows, HD:], lambda scores: scores + bias[rows, 0:1])
+
     attend(own_kv[0], own_kv[1], causal)
-    lax.fori_loop(0, early, text_chunk, 0)
+    first_row = pl.multiple_of((plane * 2 + core) * rows_text, 128)
+    text[pl.ds(first_row, rows_text), :] = share_ref[...]
+    text_rows(plane, core)
+    text_twin(0, 1 - core).wait_recv()
+    text_rows(plane, 1 - core)
 
     def slot(place, which):
         return image.at[pl.ds(pl.multiple_of((place * 2 + which) * each, 16), each)]
@@ -990,10 +1037,24 @@
     for j in range(1, planes):
         plane_link(j).start()
     twin_link(0, core).start()
-    lax.fori_loop(early, chunks, text_chunk, 0)
+    for j in range(1, planes):
+        text_from(j).wait_recv()
+        text_twin(j, core).start()
+
+    def text_near(j, carry):
+        text_rows((plane - j) % planes, core)
+        return carry
+
+    def text_far(j, carry):
+        text_twin(j, 1 - core).wait_recv()
+        text_rows((plane - j) % planes, 1 - core)
+        return carry
+
+    lax.fori_loop(1, planes, text_near, 0)
     for j in range(1, planes):
         plane_from(j).wait_recv()
         twin_link(j, core).start()
+    lax.fori_loop(1, planes, text_far, 0)
     for j in range(planes):
         twin_link(j, 1 - core).wait_recv()
 
@@ -1064,10 +1125,13 @@
     swap.wait_send()
     for k in range(1, chips):
         line_link(k).wait_send()
+    text_own().wait_send()
     for j in range(planes):
         twin_link(j, core).wait_send()
         if j:
             plane_link(j).wait_send()
+            text_link(j).wait_send()
+            text_twin(j, core).wait_send()
     for piece in range(2):
         for origin in range(chips):
             give(origin, piece, 1 - core).wait_recv()
@@ -1084,7 +1148,7 @@
                         give(origin_of(direction, hop), piece, core).wait_send()
 
 
-def tail(visual, kv_gain, token_dest, token_row, resp_len, text_kv, w_kv, queries, resp_kv, shard_rows, collective_id):
+def tail(visual, kv_gain, token_dest, token_row, resp_len, text_share, w_kv, queries, resp_kv, shard_rows, collective_id):
     sizes = tuple(lax.axis_size(name) for name in VIS)
     ctxs = lax.axis_size("ctx")
     chips, planes = sizes[0] * sizes[1], ctxs * sizes[1]
@@ -1104,6 +1168,7 @@
             pltpu.VMEM((mine * resp, HD), BF16),
             pltpu.VMEM((2, resp, HD), BF16),
             pltpu.VMEM((ctxs * shard_rows, 128), F32),
+            pltpu.VMEM((planes * 2 * text_share.shape[0], 2 * HD), BF16),
             pltpu.VMEM((planes * 2 * each, 2 * HD), BF16),
             pltpu.VMEM((chips, each, 2 * HD), F32),
             pltpu.VMEM((sizes[1], 8, 2 * HD), F32),
@@ -1122,16 +1187,20 @@
             DMA((planes,)),
             DMA((planes,)),
             DMA((planes,)),
+            DMA((planes,)),
+            DMA((planes,)),
+            DMA((planes,)),
+            DMA((planes,)),
             DMA((2, chips, 2)),
             DMA((2, chips, 2)),
             DMA((chips, 2)),
             DMA((chips, 2)),
         ],
         compiler_params=pltpu.CompilerParams(
-            collective_id=collective_id, has_side_effects=True, vmem_limit_bytes=48 * 2**20
+            collective_id=collective_id, has_side_effects=True, vmem_limit_bytes=32 * 2**20
         ),
     )(
-        visual, kv_gain.reshape(1, -1), token_dest, token_row, resp_len, text_kv, w_kv, queries,
+        visual, kv_gain.reshape(1, -1), token_dest, token_row, resp_len, text_share, w_kv, queries,
         resp_kv,
     )
 
@@ -1155,11 +1224,11 @@
     qkv, gathered, chain_last, text_mine, text_sq = front(
         patches, vis_gain, w_qkv, prompt_text, kv_gain, w_kv, 0
     )
-    visual, text_kv = middle(
+    visual, text_share = middle(
         qkv, gathered, w_out, merge_gain, w_merge, chain_last, text_mine, text_sq, 1
     )
     return tail(
-        visual, kv_gain, token_dest, token_row, resp_len, text_kv, w_kv, queries, resp_kv,
+        visual, kv_gain, token_dest, token_row, resp_len, text_share, w_kv, queries, resp_kv,
         prompt_text.shape[0], 2
     )
 

time: 130 us -> 113 us (0.87)
  Pallas kernels: 124 us -> 109 us
  local copies, waits for them, and re-layouts: 5.4 us -> 3.38 us
    pallas_call x1, Pallas kernels: 57.2 us -> 43.3 us  [middle(): pl.pallas_call(functools.partial(middle_kernel, sizes, ctxs), out_shape=[...]
    unnamed x24 -> x19, local copies, waits for them, and re-layouts: 5.39 us -> 2.67 us
    pallas_call x1, Pallas kernels: 31.8 us -> 30.3 us  [front(): pl.pallas_call(functools.partial(front_kernel, sizes), out_shape=[jax.Sha...]
where the time goes in v3:
time: 113 us
  Pallas kernels  109 us (96%)
  local copies, waits for them, and re-layouts  3.38 us (3%)
    pallas_call x1, Pallas kernels, middle(): pl.pallas_call(functools.partial(middle_kernel, sizes, ctxs), out_shape=[...  43.3 us
    pallas_call x1, Pallas kernels, tail(): pl.pallas_call(functools.partial(tail_kernel, sizes, ctxs, mine, shard_ro...  35.2 us
    pallas_call x1, Pallas kernels, front(): pl.pallas_call(functools.partial(front_kernel, sizes), out_shape=[jax.Sha...  30.3 us
    unnamed x19, local copies, waits for them, and re-layouts  2.67 us

profile of v3, /device:TPU:0, one launch (start us, length us, event | category | flops | bytes accessed | tf_op | source)
XLA Modules:
  0.0 112.9 jit_solution(10786004484383213990)
XLA Ops:
  0.0 0.7 reshape.13.refs_1_
  0.7 0.0 copy-start.3
  0.7 1.0 copy-done.3
  1.7 0.0 copy-start.5
  1.7 0.7 copy-done.5
  2.4 0.0 copy-start.8
  2.4 0.0 copy-start.2
  2.4 30.3 %shard_map.136 = (bf16[1024,768]{1,0:T(8,128)(2,1)S(1)}, bf16[8,128,1280]{2,1,0:T(8,128)(2,1)S(1)}, bf16[2,528,256]{2,1,0:T(8,128)(2,1)S(1)}, f32[512,256]{1,0:T(8,128)S(1)}, f32[8,256]{1,0:T(8,128)S(1)}) custom-call(bf16[128,1280]{1,0:T(8,128)(2,1)S(1)} %copy-done.3, f32[1,1280]{1,0:T(1,128)S(1)} %reshape.13.refs_1_, f32[1,1024]{1,0:T(1,128)S(1)} %bitcast.4, ...), custom_call_target="tpu_custom_call" | custom-call | tf_op jit(solution)/shard_map/pallas_call | solution.py:333
  32.7 0.0 copy-done.8
  32.7 0.0 copy-done.2
  32.7 0.0 copy-start
  32.7 0.0 copy-start.1
  32.7 0.0 copy-start.4
  32.7 0.0 copy-start.6
  32.8 0.0 copy-start.7
  32.8 43.3 %shard_map.137 = (bf16[256,1024]{1,0:T(8,128)(2,1)S(1)}, bf16[512,256]{1,0:T(8,128)(2,1)S(1)}) custom-call(bf16[1024,768]{1,0:T(8,128)(2,1)S(1)} %get-tuple-element.12.refs_0_, bf16[160,1280]{1,0:T(8,128)(2,1)S(1)} %copy-done.2, f32[1,1280]{1,0:T(1,128)S(1)} %reshape.15.refs_2_, bf16[2,528,256]{2,1,0:T(8,128)(2,1)S(1)} %get-tuple-element.13.refs_3_, ...), custom_call_target="tpu_custom_call" | custom-call | tf_op jit(solution)/shard_map/pallas_call | solution.py:765
  76.8 0.0 copy-done
  76.8 0.0 copy-done.1
  76.8 0.0 copy-done.4
  76.8 0.0 copy-done.6
  76.8 0.0 copy-done.7
  76.8 35.2 %shard_map.138 = bf16[128,4096]{1,0:T(8,128)(2,1)S(1)} custom-call(bf16[256,1024]{1,0:T(8,128)(2,1)S(1)} %get-tuple-element.17.refs_0_, f32[1,1024]{1,0:T(1,128)S(1)} %bitcast.5, s32[4,256]{1,0:T(4,128)S(1)} %copy-done.6, s32[4,256]{1,0:T(4,128)S(1)} %copy-done.7, s32[1]{0:T(128)S(6)} %copy.16.refs_4_, bf16[512,256]{1,0:T(8,128)(2,1)S(1)} %get-tuple-element.18.refs_5_, ...), custom_call_target="tpu_custom_call" | custom-call | tf_op jit(solution)/shard_map/pallas_call | solution.py:1160
  112.0 1.0 copy.17
  (1 shorter events, 0.0 us)
Async XLA Ops:
  0.7 1.0 copy-start.3
  1.7 0.7 copy-start.5
  2.4 30.3 %copy-start.8 = (f32[1280]{0:T(1024)S(1)}, f32[1280]{0:T(1024)}, u32[]{:S(2)}) copy-start(f32[1280]{0:T(1024)} %param.18) | copy-start | bytes 15364
  2.4 30.3 %copy-start.2 = (bf16[160,1280]{1,0:T(8,128)(2,1)S(1)}, bf16[160,1280]{1,0:T(8,128)(2,1)}, u32[]{:S(2)}) copy-start(bf16[160,1280]{1,0:T(8,128)(2,1)} %refs_1_.1) | copy-start | bytes 1228804
  32.7 44.1 %copy-start = (bf16[1024,1024]{1,0:T(8,128)(2,1)S(1)}, bf16[1024,1024]{1,0:T(8,128)(2,1)}, u32[]{:S(2)}) copy-start(bf16[1024,1024]{1,0:T(8,128)(2,1)} %refs_6_.1) | copy-start | bytes 6291460
  32.7 44.1 %copy-start.1 = (bf16[128,4096]{1,0:T(8,128)(2,1)S(1)}, bf16[128,4096]{1,0:T(8,128)(2,1)}, u32[]{:S(2)}) copy-start(bf16[128,4096]{1,0:T(8,128)(2,1)} %refs_7_.3) | copy-start | bytes 3145732
  32.7 44.1 %copy-start.4 = (bf16[128,1024]{1,0:T(8,128)(2,1)S(1)}, bf16[128,1024]{1,0:T(8,128)(2,1)}, u32[]{:S(2)}) copy-start(bf16[128,1024]{1,0:T(8,128)(2,1)} %refs_8_.1) | copy-start | bytes 786436
  32.7 44.1 %copy-start.6 = (s32[4,256]{1,0:T(4,128)S(1)}, s32[4,256]{1,0:T(4,128)}, u32[]{:S(2)}) copy-start(s32[4,256]{1,0:T(4,128)} %refs_2_.1) | copy-start | bytes 12292
  32.8 44.1 %copy-start.7 = (s32[4,256]{1,0:T(4,128)S(1)}, s32[4,256]{1,0:T(4,128)}, u32[]{:S(2)}) copy-start(s32[4,256]{1,0:T(4,128)} %refs_3_.1) | copy-start | bytes 12292

commit v4 on v3

--- a/solution.py
+++ b/solution.py
@@ -22,14 +22,13 @@
 MESH = pl.DeviceIdType.MESH
 VMEM = pl.BlockSpec(memory_space=pltpu.VMEM)
 ANY = pl.BlockSpec(memory_space=pl.ANY)
-HBM = pl.BlockSpec(memory_space=pltpu.MemorySpace.HBM)
 F32 = jnp.float32
 BF16 = jnp.bfloat16
 PIECES = 2
 SUBROWS = 256
 LNROWS = 64
 LANES = 256
-KEYS = 512
+KEYS = 1024
 
 
 def layer_norm(values, gain):
@@ -40,7 +39,7 @@
 
 def front_kernel(sizes, *refs):
     (
-        patches_ref, gain_ref, tgain_ref, wqkv_hbm, text_hbm, wkv_hbm,
+        patches_ref, gain_ref, tgain_ref, wqkv_hbm, text_hbm, wkv_hbm, greet,
         qkv_ref, held, chain_last, mine_ref, mine_sq,
         wpad, text, wkv, normed, own, own_sq, pair_out, pair_in, chain_out, chain_in,
         load_sem, send_sem, recv_sem, near_send, near_recv, pair_sem, chain_send, chain_recv,
@@ -81,18 +80,11 @@
     for load in loads:
         load.start()
 
-    barrier = pltpu.get_barrier_semaphore()
-    pl.semaphore_signal(barrier, inc=1, device_id=at(chip, 1 - core), device_id_type=MESH)
-    for direction in range(2):
-        @pl.when(has(direction))
-        def _():
-            pl.semaphore_signal(
-                barrier, inc=1, device_id=at(neighbour(direction), core), device_id_type=MESH
-            )
-    pl.semaphore_wait(barrier, 1 + jnp.where(has(0), 1, 0) + jnp.where(has(1), 1, 0))
+    greet()
 
     def slot(origin, which, piece):
-        return held.at[origin * 2 + which, pl.ds(piece * half, half)]
+        first = pl.multiple_of((origin * 2 + which) * count + piece * half, 16)
+        return held.at[pl.ds(first, half)]
 
     def source(origin, piece, hop):
         return patches_ref.at[pl.ds(piece * half, half)] if hop == 0 else slot(origin, core, piece)
@@ -136,7 +128,8 @@
             @pl.when(has(direction))
             def _():
                 pass_on(direction, 0, piece).start()
-    mine = pltpu.make_async_copy(patches_ref, held.at[chip * 2 + core], load_sem.at[len(loads)])
+    my_rows = pl.ds(pl.multiple_of((chip * 2 + core) * count, 16), count)
+    mine = pltpu.make_async_copy(patches_ref, held.at[my_rows], load_sem.at[len(loads)])
     mine.start()
     for piece in range(PIECES):
         give(chip, piece, 0).start()
@@ -200,9 +193,8 @@
 
     def project(origin):
         def norm_rows(i, carry):
-            which = i // (count // LNROWS)
-            begin = pl.multiple_of((i % (count // LNROWS)) * LNROWS, LNROWS)
-            floats = held[origin * 2 + which, pl.ds(begin, LNROWS), :].astype(F32)
+            begin = pl.multiple_of(origin * 2 * count + i * LNROWS, LNROWS)
+            floats = held[pl.ds(begin, LNROWS), :].astype(F32)
             place = pl.multiple_of(i * LNROWS, LNROWS)
             normed[pl.ds(place, LNROWS), :] = layer_norm(floats, gain_ref[...]).astype(BF16)
             return carry
@@ -296,75 +288,27 @@
     chain(chips - 1)
     project_hop(chips - 1)
 
-    swap.wait_send()
-    for piece in range(PIECES):
-        give(chip, piece, 0).wait_send()
+    def drain():
+        swap.wait_send()
+        for piece in range(PIECES):
+            give(chip, piece, 0).wait_send()
+            for direction in range(2):
+                for hop in range(chips):
+                    if hop < chips - 1:
+                        @pl.when(jnp.logical_and(exists(direction, hop), has(direction)))
+                        def _():
+                            pass_on(direction, hop, piece).wait_send()
+                    if hop > 0:
+                        @pl.when(exists(direction, hop))
+                        def _():
+                            give(origin_of(direction, hop), piece, hop).wait_send()
         for direction in range(2):
-            for hop in range(chips):
-                if hop < chips - 1:
-                    @pl.when(jnp.logical_and(exists(direction, hop), has(direction)))
-                    def _():
-                        pass_on(direction, hop, piece).wait_send()
-                if hop > 0:
-                    @pl.when(exists(direction, hop))
-                    def _():
-                        give(origin_of(direction, hop), piece, hop).wait_send()
-    for direction in range(2):
-        for d in range(chips):
-            @pl.when(chip < d - 1 if direction == 0 else chip > d + 1)
-            def _():
-                link(direction, d).wait_send()
-
-
-def in_hbm(array):
-    return pltpu.with_memory_space_constraint(array, pltpu.MemorySpace.HBM)
-
-
-def front(patches, vis_gain, w_qkv, text, kv_gain, w_kv, collective_id):
-    sizes = tuple(lax.axis_size(name) for name in VIS)
-    chips = sizes[0] * sizes[1]
-    parts = sizes[1] * 2
-    count, width = patches.shape
-    rows, features = text.shape
-    each = rows // parts
-    heads3 = w_qkv.shape[1] // VHD
-    block = (each + 16, 2 * HD)
-    DMA = pltpu.SemaphoreType.DMA
-    return pl.pallas_call(
-        functools.partial(front_kernel, sizes),
-        out_shape=[
-            jax.ShapeDtypeStruct((2 * chips * count, heads3 * 128), BF16),
-            jax.ShapeDtypeStruct((2 * chips, count, width), BF16),
-            jax.ShapeDtypeStruct((2,) + block, BF16),
-            jax.ShapeDtypeStruct((each, 2 * HD), F32),
-            jax.ShapeDtypeStruct((8, SUBROWS), F32),
-        ],
-        in_specs=[VMEM] * 3 + [HBM] * 3,
-        out_specs=[VMEM] * 5,
-        scratch_shapes=[
-            pltpu.VMEM((heads3 * 128, width), BF16),
-            pltpu.VMEM(text.shape, BF16),
-            pltpu.VMEM(w_kv.shape, BF16),
-            pltpu.VMEM((2 * count, width), BF16),
-            pltpu.VMEM((chips,) + (each, 2 * HD), F32),
-            pltpu.VMEM((sizes[1], 8, SUBROWS), F32),
-            pltpu.VMEM((chips,) + block, BF16),
-            pltpu.VMEM((chips,) + block, BF16),
-            pltpu.VMEM((2, chips) + block, BF16),
-            pltpu.VMEM((2, chips) + block, BF16),
-            DMA((3 + heads3,)),
-            DMA((2, chips, PIECES)),
-            DMA((2, chips, PIECES)),
-            DMA((chips, PIECES)),
-            DMA((chips, PIECES)),
-            DMA((2,)),
-            DMA((2, chips)),
-            DMA((2, chips)),
-        ],
-        compiler_params=pltpu.CompilerParams(
-            collective_id=collective_id, has_side_effects=True, vmem_limit_bytes=40 * 2**20
-        ),
-    )(patches, vis_gain.reshape(1, -1), kv_gain.reshape(1, -1), *map(in_hbm, (w_qkv.T, text, w_kv)))
+            for d in range(chips):
+                @pl.when(chip < d - 1 if direction == 0 else chip > d + 1)
+                def _():
+                    link(direction, d).wait_send()
+
+    return drain
 
 
 def spread_of(rows, width, places):
@@ -380,9 +324,9 @@
 
 def middle_kernel(sizes, ctxs, *refs):
     (
-        qkv_ref, wout_ref, gain_ref, chain_ref, mine_ref, sq_ref, patches_hbm, wmerge_hbm,
+        qkv_ref, wout_ref, gain_ref, chain_ref, mine_ref, sq_ref, patches, wmerge_hbm,
         visual_ref, share_ref,
-        patches, held, wall, wmerge, mixed, merged, token_sum, values, staged, chain_in,
+        held, wall, wmerge, mixed, merged, token_sum, values, staged, chain_in,
         load_sem, send_sem, recv_sem, near_send, near_recv, merge_send, merge_recv,
         chain_send, chain_recv,
         line_send, line_recv, plane_send, plane_recv, pair_send, pair_recv,
@@ -421,26 +365,11 @@
         )
 
     twin = at(chip, 1 - core)
-    my_half = pl.ds(pl.multiple_of(core * half, LANES), half)
-    fetch = pltpu.make_async_copy(patches_hbm.at[my_half], patches, load_sem.at[2])
-    fetch.start()
     load = pltpu.make_async_copy(wmerge_hbm, wmerge, load_sem.at[0])
     load.start()
     my_rows = pl.ds(pl.multiple_of(me * deep, 16), deep)
     keep = pltpu.make_async_copy(wout_ref, wall.at[my_rows], load_sem.at[1])
     keep.start()
-
-    barrier = pltpu.get_barrier_semaphore()
-    pl.semaphore_signal(barrier, inc=1, device_id=twin, device_id_type=MESH)
-    for k in range(1, chips):
-        pl.semaphore_signal(
-            barrier, inc=1, device_id=at((chip + k) % chips, core), device_id_type=MESH
-        )
-    for j in range(1, planes):
-        pl.semaphore_signal(
-            barrier, inc=1, device_id=beside((plane + j) % planes), device_id_type=MESH
-        )
-    pl.semaphore_wait(barrier, chips + planes - 1)
 
     def last_link(direction):
         return remote(
@@ -587,28 +516,24 @@
 
         def body(i, carry):
             rows = pl.ds(pl.multiple_of(i * 128, 128), 128)
-            mine_sum[rows, :] += chain_in[direction, rows, :].astype(F32)
+            mine_ref[rows, :] += chain_in[direction, rows, :].astype(F32)
             return carry
 
         lax.fori_loop(0, each // 128, body, 0)
-        squares[...] += untail(chain_in[direction, each:, :])
-
-    def finish_text(sum_ref, square_ref):
-        nonlocal mine_sum, squares
-        mine_sum, squares = sum_ref, square_ref
-        mine_sum[...] = mine_ref[...]
-        squares[...] = sq_ref[...]
+        sq_ref[...] += untail(chain_in[direction, each:, :])
+
+    def finish_text():
         for direction in range(2):
             @pl.when(has(1 - direction))
             def _():
                 gain_from(direction)
-        inverse = lax.rsqrt(squares[...] / D + EPS)
+        inverse = lax.rsqrt(sq_ref[...] / D + EPS)
         for s in range(subs):
             factor = jnp.transpose(jnp.broadcast_to(inverse[s : s + 1], (128, SUBROWS)))
             for side in range(2):
                 lanes = slice(side * HD, (side + 1) * HD)
                 rows = slice(s * SUBROWS, (s + 1) * SUBROWS)
-                share_ref[rows, lanes] = (mine_sum[rows, lanes] * factor).astype(BF16)
+                share_ref[rows, lanes] = (mine_ref[rows, lanes] * factor).astype(BF16)
 
     for k in range(1, chips):
         @pl.when(ctx < used)
@@ -618,8 +543,6 @@
                 from_line(k, j).start()
             to_twin(k, 0, core).start()
     relay(1)
-    mine_sum = squares = None
-
     def add_chip(origin, fresh):
         rows = pl.ds(pl.multiple_of(origin * 2 * deep, 16), 2 * deep)
 
@@ -630,7 +553,8 @@
                 preferred_element_type=F32,
             )
             if fresh:
-                product += patches[places, :].astype(F32)
+                mine_in = pl.ds(pl.multiple_of(core * half + i * LANES, LANES), LANES)
+                product += patches[mine_in, :].astype(F32)
             for c in range(width // 128):
                 lanes = product[:, c * 128 : (c + 1) * 128]
                 mixed[c, places, :] = lanes if fresh else mixed[c, places, :] + lanes
@@ -645,7 +569,6 @@
                 add_chip(origin_of(direction, hop), hop == 0)
 
     keep.wait()
-    fetch.wait()
     own_to_twin().wait_recv()
     add_hop(0)
     def last_sends():
@@ -717,100 +640,46 @@
 
         lax.fori_loop(0, visual_ref.shape[1] // LANES, column, 0)
 
-    pl.run_scoped(
-        finish_text, pltpu.VMEM((each, 2 * HD), F32), pltpu.VMEM((8, SUBROWS), F32)
-    )
-    own_to_twin().wait_send()
-    for k in range(1, chips):
-        @pl.when(ctx < used)
-        def _():
-            line_part(k).wait_send()
-            for j in range(1, ctxs):
-                from_line(k, j).wait_send()
-        for j in range(ctxs):
-            @pl.when((ctx - j) % ctxs < used)
+    finish_text()
+    def drain():
+        own_to_twin().wait_send()
+        for k in range(1, chips):
+            @pl.when(ctx < used)
             def _():
-                to_twin(k, j, core).wait_send()
-    for direction in range(2):
-        @pl.when(has(direction))
-        def _():
-            last_link(direction).wait_send()
-
-    for r in range(4):
-        merge_link(r, core).wait_send()
-
-    def drain(piece, carry):
-        give(piece).wait_send()
+                line_part(k).wait_send()
+                for j in range(1, ctxs):
+                    from_line(k, j).wait_send()
+            for j in range(ctxs):
+                @pl.when((ctx - j) % ctxs < used)
+                def _():
+                    to_twin(k, j, core).wait_send()
         for direction in range(2):
-            for hop in range(chips - 1):
-                @pl.when(jnp.logical_and(exists(direction, hop), has(direction)))
-                def _():
-                    pass_on(direction, hop, piece).wait_send()
-        return carry
-
-    lax.fori_loop(0, blocks, drain, 0)
-
-
-def middle(qkv, gathered, w_out, merge_gain, w_merge, chain_last, mine, mine_sq, collective_id):
-    sizes = tuple(lax.axis_size(name) for name in VIS)
-    ctxs = lax.axis_size("ctx")
-    chips, planes = sizes[0] * sizes[1], ctxs * sizes[1]
-    total, width = qkv.shape[0], w_out.shape[1]
-    each = mine.shape[0]
-    half = total // 2
-    blocks = half // LANES
-    heads = w_out.shape[0] // VHD
-    tokens = total // 4
-    DMA = pltpu.SemaphoreType.DMA
-    return pl.pallas_call(
-        functools.partial(middle_kernel, sizes, ctxs),
-        out_shape=[
-            jax.ShapeDtypeStruct((tokens, w_merge.shape[1]), BF16),
-            jax.ShapeDtypeStruct((each, 2 * HD), BF16),
-        ],
-        in_specs=[VMEM] * 6 + [ANY] * 2,
-        out_specs=[VMEM] * 2,
-        scratch_shapes=[
-            pltpu.VMEM((half, width), BF16),
-            pltpu.VMEM((VD, half), BF16),
-            pltpu.VMEM((VD, width), BF16),
-            pltpu.VMEM(w_merge.shape, BF16),
-            pltpu.VMEM((width // 128, half, 128), F32),
-            pltpu.VMEM((4, tokens, width), BF16),
-            pltpu.VMEM((tokens, w_merge.shape[1]), F32),
-            pltpu.VMEM((heads, 128, total), BF16),
-            pltpu.VMEM((w_out.shape[0], half), BF16),
-            pltpu.VMEM(chain_last.shape, BF16),
-            DMA((3,)),
-            DMA((2, chips, blocks)),
-            DMA((2, chips, blocks)),
-            DMA((blocks,)),
-            DMA((blocks,)),
-            DMA((4,)),
-            DMA((4,)),
-            DMA((2,)),
-            DMA((2,)),
-            DMA((chips,)),
-            DMA((chips,)),
-            DMA((chips, ctxs)),
-            DMA((chips, ctxs)),
-            DMA((chips, ctxs)),
-            DMA((chips, ctxs)),
-        ],
-        compiler_params=pltpu.CompilerParams(
-            collective_id=collective_id, has_side_effects=True, vmem_limit_bytes=40 * 2**20
-        ),
-    )(
-        qkv, w_out, merge_gain.reshape(1, -1), chain_last, mine, mine_sq,
-        gathered.reshape(total, width), w_merge,
-    )
+            @pl.when(has(direction))
+            def _():
+                last_link(direction).wait_send()
+
+        for r in range(4):
+            merge_link(r, core).wait_send()
+
+        def drain_line(piece, carry):
+            give(piece).wait_send()
+            for direction in range(2):
+                for hop in range(chips - 1):
+                    @pl.when(jnp.logical_and(exists(direction, hop), has(direction)))
+                    def _():
+                        pass_on(direction, hop, piece).wait_send()
+            return carry
+
+        lax.fori_loop(0, blocks, drain_line, 0)
+
+    return drain
 
 
 def tail_kernel(sizes, ctxs, mine, shard_rows, *refs):
     (
-        visual_ref, tgain_ref, dest_ref, row_ref, len_ref, share_ref, wkv_hbm, query_hbm, own_hbm,
+        visual_ref, tgain_ref, dest_ref, row_ref, len_ref, share_ref, wkv, query_hbm, own_hbm,
         out_ref,
-        wkv, query_in, query, own_kv, bias, text, image, own, own_sq, pair_out, pair_in, line_out, line_in,
+        query_in, query, own_kv, bias, text, image, own, own_sq, pair_out, pair_in, line_out, line_in,
         high, summed, mix,
         load_sem, swap_sem, line_send, line_recv, plane_send, plane_recv, twin_send, twin_recv,
         text_send, text_recv, pass_send, pass_recv, send_sem, recv_sem, near_send, near_recv,
@@ -849,7 +718,6 @@
     lane = pl.multiple_of(me * mine * HD, HD)
     head = pl.multiple_of(((me * mine) // group) * HD, HD)
     loads = [
-        pltpu.make_async_copy(wkv_hbm, wkv, load_sem.at[0]),
         pltpu.make_async_copy(query_hbm.at[:, pl.ds(lane, mine * HD)], query_in, load_sem.at[1]),
         pltpu.make_async_copy(own_hbm.at[:, pl.ds(head, HD)], own_kv.at[0], load_sem.at[2]),
         pltpu.make_async_copy(
@@ -858,18 +726,6 @@
     ]
     for load in loads:
         load.start()
-
-    barrier = pltpu.get_barrier_semaphore()
-    pl.semaphore_signal(barrier, inc=1, device_id=twin, device_id_type=MESH)
-    for k in range(1, chips):
-        pl.semaphore_signal(
-            barrier, inc=1, device_id=at((chip + k) % chips, core), device_id_type=MESH
-        )
-    for j in range(1, planes):
-        pl.semaphore_signal(
-            barrier, inc=1, device_id=beside((plane + j) % planes), device_id_type=MESH
-        )
-    pl.semaphore_wait(barrier, chips + planes - 1)
 
     rows_text = share_ref.shape[0]
 
@@ -925,7 +781,6 @@
         own[d, :, side * HD : (side + 1) * HD] = value
 
     own_sq[...] = jnp.zeros_like(own_sq)
-    loads[0].wait()
     for v in range(vh):
         token_rows(v, 1 - core, write_pair)
         for h in range(KVH):
@@ -934,7 +789,7 @@
     swap.start()
     for v in range(vh):
         token_rows(v, core, write_own)
-    for load in loads[1:]:
+    for load in loads:
         load.wait()
     for j in range(mine):
         query[j * resp : (j + 1) * resp, :] = query_in[:, j * HD : (j + 1) * HD]
@@ -952,8 +807,7 @@
         line_out[d, each:, :] = split(own_sq[d % vh] + joined(pair_in[d, each:, :]))
         line_link(k).start()
 
-    groups = bias.shape[0] // 128
-    padded = -(-groups // 128) * 128
+    padded = bias.shape[1]
     count = jnp.zeros((128, padded), F32)
     for i in range(dest_ref.shape[0]):
         flat = dest_ref[i : i + 1, :] * shard_rows + row_ref[i : i + 1, :]
@@ -963,26 +817,24 @@
             jnp.where(low, 1.0, 0.0).astype(BF16), jnp.where(upper, 1.0, 0.0).astype(BF16),
             (((1,), (1,)), ((), ())), preferred_element_type=F32,
         )
-    hidden = jnp.where(count > 0.5, -1e30, 0.0)
-    for g in range(groups):
-        bias[g * 128 : (g + 1) * 128, :] = jnp.broadcast_to(hidden[:, g : g + 1], (128, 128))
+    bias[...] = count.astype(BF16)
 
     high[...] = jnp.full_like(high, -1e30)
     summed[...] = jnp.zeros_like(summed)
     mix[...] = jnp.zeros_like(mix)
     scale = 1.0 / math.sqrt(HD)
 
-    def attend(keys, values, mask):
+    def attend(keys, values, mask, lanes=slice(None)):
         scores = lax.dot_general(
-            keys, query[...], (((1,), (1,)), ((), ())), preferred_element_type=F32
+            keys, query[lanes, :], (((1,), (1,)), ((), ())), preferred_element_type=F32
         ) * scale
         scores = mask(scores)
-        top = jnp.maximum(high[...], jnp.max(scores, axis=0, keepdims=True))
-        fade = jnp.exp(high[...] - top)
+        top = jnp.maximum(high[:, lanes], jnp.max(scores, axis=0, keepdims=True))
+        fade = jnp.exp(high[:, lanes] - top)
         expo = jnp.exp(scores - top)
-        high[...] = top
-        summed[...] = summed[...] * fade + jnp.sum(expo, axis=0, keepdims=True)
-        mix[...] = mix[...] * fade + jnp.dot(
+        high[:, lanes] = top
+        summed[:, lanes] = summed[:, lanes] * fade + jnp.sum(expo, axis=0, keepdims=True)
+        mix[:, lanes] = mix[:, lanes] * fade + jnp.dot(
             jnp.transpose(values.astype(F32)).astype(BF16), expo.astype(BF16),
             preferred_element_type=F32,
         )
@@ -995,7 +847,19 @@
     def text_rows(place, which):
         first = (place * 2 + which) * rows_text
         rows = pl.ds(pl.multiple_of(first, 128), rows_text)
-        attend(text[rows, :HD], text[rows, HD:], lambda scores: scores + bias[rows, 0:1])
+
+        def mask(scores):
+            upper = lax.broadcasted_iota(jnp.int32, (padded, scores.shape[1]), 0)
+            taken = [
+                jnp.dot(
+                    bias[...], jnp.where(upper == first // 128 + i, 1.0, 0.0).astype(BF16),
+                    preferred_element_type=F32,
+                )
+                for i in range(rows_text // 128)
+            ]
+            return jnp.where(jnp.concatenate(taken, axis=0) > 0.5, -1e30, scores)
+
+        attend(text[rows, :HD], text[rows, HD:], mask)
 
     attend(own_kv[0], own_kv[1], causal)
     first_row = pl.multiple_of((plane * 2 + core) * rows_text, 128)
@@ -1058,18 +922,9 @@
     for j in range(planes):
         twin_link(j, 1 - core).wait_recv()
 
-    def image_chunk(i, carry):
-        rows = pl.ds(pl.multiple_of(i * KEYS, KEYS), KEYS)
-        attend(image[rows, :HD], image[rows, HD:], lambda scores: scores)
-        return carry
-
-    lax.fori_loop(0, image.shape[0] // KEYS, image_chunk, 0)
-
-    piece_width = mine * HD // 2
-
     def result_slot(origin, which, piece):
-        first = ((origin * 2 + which) * 2 + piece) * piece_width
-        return out_ref.at[:, pl.ds(pl.multiple_of(first, 128), piece_width)]
+        first = ((origin * 2 + which) * mine + piece) * HD
+        return out_ref.at[:, pl.ds(pl.multiple_of(first, HD), HD)]
 
     def origin_of(direction, hop):
         return chip - hop if direction == 0 else chip + hop
@@ -1098,20 +953,26 @@
         )
 
     live = lax.broadcasted_iota(jnp.int32, (resp, HD), 0) < len_ref[0]
-    for piece in range(2):
-        for j in range(piece * mine // 2, (piece + 1) * mine // 2):
-            lanes = slice(j * resp, (j + 1) * resp)
-            value = jnp.transpose(mix[:, lanes] / summed[:, lanes])
-            out_ref[:, pl.ds(pl.multiple_of(lane + j * HD, HD), HD)] = jnp.where(
-                live, value, 0.0
-            ).astype(BF16)
+    for piece in range(mine):
+        lanes = slice(piece * resp, (piece + 1) * resp)
+
+        def image_chunk(i, carry):
+            rows = pl.ds(pl.multiple_of(i * KEYS, KEYS), KEYS)
+            attend(image[rows, :HD], image[rows, HD:], lambda scores: scores, lanes)
+            return carry
+
+        lax.fori_loop(0, image.shape[0] // KEYS, image_chunk, 0)
+        value = jnp.transpose(mix[:, lanes] / summed[:, lanes])
+        out_ref[:, pl.ds(pl.multiple_of(lane + piece * HD, HD), HD)] = jnp.where(
+            live, value, 0.0
+        ).astype(BF16)
         for direction in range(2):
             @pl.when(has(direction))
             def _():
                 pass_on(direction, 0, piece).start()
         give(chip, piece, core).start()
     for hop in range(1, chips):
-        for piece in range(2):
+        for piece in range(mine):
             for direction in range(2):
                 @pl.when(exists(direction, hop))
                 def _():
@@ -1132,7 +993,7 @@
             plane_link(j).wait_send()
             text_link(j).wait_send()
             text_twin(j, core).wait_send()
-    for piece in range(2):
+    for piece in range(mine):
         for origin in range(chips):
             give(origin, piece, 1 - core).wait_recv()
         give(chip, piece, core).wait_send()
@@ -1148,61 +1009,56 @@
                         give(origin_of(direction, hop), piece, core).wait_send()
 
 
-def tail(visual, kv_gain, token_dest, token_row, resp_len, text_share, w_kv, queries, resp_kv, shard_rows, collective_id):
-    sizes = tuple(lax.axis_size(name) for name in VIS)
-    ctxs = lax.axis_size("ctx")
-    chips, planes = sizes[0] * sizes[1], ctxs * sizes[1]
-    each = visual.shape[0] // (2 * sizes[1])
-    mine = QH // (2 * chips)
-    resp = queries.shape[0]
-    block = (chips, each + 16, 2 * HD)
-    DMA = pltpu.SemaphoreType.DMA
-    return pl.pallas_call(
-        functools.partial(tail_kernel, sizes, ctxs, mine, shard_rows),
-        out_shape=jax.ShapeDtypeStruct((resp, QH * HD), BF16),
-        in_specs=[VMEM] * 4 + [pl.BlockSpec(memory_space=pltpu.SMEM), VMEM] + [ANY] * 3,
-        out_specs=VMEM,
-        scratch_shapes=[
-            pltpu.VMEM(w_kv.shape, BF16),
-            pltpu.VMEM((resp, mine * HD), BF16),
-            pltpu.VMEM((mine * resp, HD), BF16),
-            pltpu.VMEM((2, resp, HD), BF16),
-            pltpu.VMEM((ctxs * shard_rows, 128), F32),
-            pltpu.VMEM((planes * 2 * text_share.shape[0], 2 * HD), BF16),
-            pltpu.VMEM((planes * 2 * each, 2 * HD), BF16),
-            pltpu.VMEM((chips, each, 2 * HD), F32),
-            pltpu.VMEM((sizes[1], 8, 2 * HD), F32),
-            pltpu.VMEM(block, BF16),
-            pltpu.VMEM(block, BF16),
-            pltpu.VMEM(block, BF16),
-            pltpu.VMEM(block, BF16),
-            pltpu.VMEM((1, mine * resp), F32),
-            pltpu.VMEM((1, mine * resp), F32),
-            pltpu.VMEM((HD, mine * resp), F32),
-            DMA((4,)),
-            DMA((2,)),
-            DMA((chips,)),
-            DMA((chips,)),
-            DMA((planes,)),
-            DMA((planes,)),
-            DMA((planes,)),
-            DMA((planes,)),
-            DMA((planes,)),
-            DMA((planes,)),
-            DMA((planes,)),
-            DMA((planes,)),
-            DMA((2, chips, 2)),
-            DMA((2, chips, 2)),
-            DMA((chips, 2)),
-            DMA((chips, 2)),
-        ],
-        compiler_params=pltpu.CompilerParams(
-            collective_id=collective_id, has_side_effects=True, vmem_limit_bytes=32 * 2**20
+def in_hbm(array):
+    return pltpu.with_memory_space_constraint(array, pltpu.MemorySpace.HBM)
+
+
+def whole_kernel(sizes, ctxs, mine, shard_rows, groups, *refs):
+    (
+        vis_gain, tgain, merge_gain, dest, row, length,
+        patches, w_out, w_qkv, text, w_kv, w_merge, queries, resp_kv, out,
+    ) = refs[:15]
+    scratch = refs[15:]
+    first, second = groups
+    front_refs, middle_refs = scratch[:first], scratch[first : first + second]
+    tail_refs = scratch[first + second :]
+    chips, vh = sizes[0] * sizes[1], sizes[1]
+    core, ctx = lax.axis_index("core"), lax.axis_index("ctx")
+    chip = lax.axis_index("vk") * vh + lax.axis_index("vh")
+    planes = ctxs * vh
+    plane = ctx * vh + lax.axis_index("vh")
+
+    def greet():
+        barrier = pltpu.get_barrier_semaphore()
+        pl.semaphore_signal(barrier, inc=1, device_id={"core": 1 - core}, device_id_type=MESH)
+        for k in range(1, chips):
+            other = (chip + k) % chips
+            pl.semaphore_signal(
+                barrier, inc=1, device_id={"vk": other // vh, "vh": other % vh}, device_id_type=MESH
+            )
+        for j in range(1, planes):
+            other = (plane + j) % planes
+            pl.semaphore_signal(
+                barrier, inc=1, device_id={"ctx": other // vh, "vh": other % vh}, device_id_type=MESH
+            )
+        pl.semaphore_wait(barrier, chips + planes - 1)
+
+    qkv, held, chain_last, sums, squares = front_refs[:5]
+    wkv = front_refs[7]
+    visual, share = middle_refs[:2]
+    drains = [
+        front_kernel(sizes, patches, vis_gain, tgain, w_qkv, text, w_kv, greet, *front_refs),
+        middle_kernel(
+            sizes, ctxs, qkv, w_out, merge_gain, chain_last, sums, squares, held, w_merge,
+            *middle_refs
         ),
-    )(
-        visual, kv_gain.reshape(1, -1), token_dest, token_row, resp_len, text_share, w_kv, queries,
-        resp_kv,
+    ]
+    tail_kernel(
+        sizes, ctxs, mine, shard_rows, visual, tgain, dest, row, length, share, wkv, queries,
+        resp_kv, out, *tail_refs
     )
+    for drain in drains:
+        drain()
 
 
 def per_device(
@@ -1221,15 +1077,127 @@
     resp_kv,
     resp_len,
 ):
-    qkv, gathered, chain_last, text_mine, text_sq = front(
-        patches, vis_gain, w_qkv, prompt_text, kv_gain, w_kv, 0
+    sizes = tuple(lax.axis_size(name) for name in VIS)
+    ctxs = lax.axis_size("ctx")
+    chips, planes, parts = sizes[0] * sizes[1], ctxs * sizes[1], sizes[1] * 2
+    count, width = patches.shape
+    shard_rows = prompt_text.shape[0]
+    each = shard_rows // parts
+    heads3 = w_qkv.shape[1] // VHD
+    total = 2 * chips * count
+    half = total // 2
+    blocks = half // LANES
+    tokens = total // 4
+    token_part = tokens // parts
+    mine = QH // (2 * chips)
+    resp = queries.shape[0]
+    DMA, V = pltpu.SemaphoreType.DMA, pltpu.VMEM
+    text_block = (each + 16, 2 * HD)
+    image_block = (chips, token_part + 16, 2 * HD)
+    front_scratch = [
+        V((total, heads3 * 128), BF16),
+        V((total, width), BF16),
+        V((2,) + text_block, BF16),
+        V((each, 2 * HD), F32),
+        V((8, SUBROWS), F32),
+        V((heads3 * 128, width), BF16),
+        V(prompt_text.shape, BF16),
+        V(w_kv.shape, BF16),
+        V((2 * count, width), BF16),
+        V((chips, each, 2 * HD), F32),
+        V((sizes[1], 8, SUBROWS), F32),
+        V((chips,) + text_block, BF16),
+        V((chips,) + text_block, BF16),
+        V((2, chips) + text_block, BF16),
+        V((2, chips) + text_block, BF16),
+        DMA((3 + heads3,)),
+        DMA((2, chips, PIECES)),
+        DMA((2, chips, PIECES)),
+        DMA((chips, PIECES)),
+        DMA((chips, PIECES)),
+        DMA((2,)),
+        DMA((2, chips)),
+        DMA((2, chips)),
+    ]
+    middle_scratch = [
+        V((tokens, w_merge.shape[1]), BF16),
+        V((each, 2 * HD), BF16),
+        V((VD, half), BF16),
+        V((VD, width), BF16),
+        V(w_merge.shape, BF16),
+        V((width // 128, half, 128), F32),
+        V((4, tokens, width), BF16),
+        V((tokens, w_merge.shape[1]), F32),
+        V((w_out.shape[0] // VHD, 128, total), BF16),
+        V((w_out.shape[0], half), BF16),
+        V((2,) + text_block, BF16),
+        DMA((2,)),
+        DMA((2, chips, blocks)),
+        DMA((2, chips, blocks)),
+        DMA((blocks,)),
+        DMA((blocks,)),
+        DMA((4,)),
+        DMA((4,)),
+        DMA((2,)),
+        DMA((2,)),
+        DMA((chips,)),
+        DMA((chips,)),
+        DMA((chips, ctxs)),
+        DMA((chips, ctxs)),
+        DMA((chips, ctxs)),
+        DMA((chips, ctxs)),
+    ]
+    tail_scratch = [
+        V((resp, mine * HD), BF16),
+        V((mine * resp, HD), BF16),
+        V((2, resp, HD), BF16),
+        V((128, -(-ctxs * shard_rows // 16384) * 128), BF16),
+        V((planes * 2 * each, 2 * HD), BF16),
+        V((planes * 2 * token_part, 2 * HD), BF16),
+        V((chips, token_part, 2 * HD), F32),
+        V((sizes[1], 8, 2 * HD), F32),
+        V(image_block, BF16),
+        V(image_block, BF16),
+        V(image_block, BF16),
+        V(image_block, BF16),
+        V((1, mine * resp), F32),
+        V((1, mine * resp), F32),
+        V((HD, mine * resp), F32),
+        DMA((4,)),
+        DMA((2,)),
+        DMA((chips,)),
+        DMA((chips,)),
+        DMA((planes,)),
+        DMA((planes,)),
+        DMA((planes,)),
+        DMA((planes,)),
+        DMA((planes,)),
+        DMA((planes,)),
+        DMA((planes,)),
+        DMA((planes,)),
+        DMA((2, chips, mine)),
+        DMA((2, chips, mine)),
+        DMA((chips, mine)),
+        DMA((chips, mine)),
+    ]
+    room = sum(
+        math.prod(item.shape) * item.dtype.itemsize
+        for item in front_scratch + middle_scratch + tail_scratch
+        if item.memory_space == pltpu.MemorySpace.VMEM
     )
-    visual, text_share = middle(
-        qkv, gathered, w_out, merge_gain, w_merge, chain_last, text_mine, text_sq, 1
-    )
-    return tail(
-        visual, kv_gain, token_dest, token_row, resp_len, text_share, w_kv, queries, resp_kv,
-        prompt_text.shape[0], 2
+    groups = (len(front_scratch), len(middle_scratch))
+    return pl.pallas_call(
+        functools.partial(whole_kernel, sizes, ctxs, mine, shard_rows, groups),
+        out_shape=jax.ShapeDtypeStruct((resp, QH * HD), BF16),
+        in_specs=[VMEM] * 5 + [pl.BlockSpec(memory_space=pltpu.SMEM)] + [ANY] * 8,
+        out_specs=VMEM,
+        scratch_shapes=front_scratch + middle_scratch + tail_scratch,
+        compiler_params=pltpu.CompilerParams(
+            collective_id=0, has_side_effects=True, vmem_limit_bytes=min(67_000_000, room + 6 * 2**20)
+        ),
+    )(
+        vis_gain, kv_gain.reshape(1, -1), merge_gain, token_dest, token_row, resp_len,
+        *map(in_hbm, (patches, w_out, w_qkv.T, prompt_text, w_kv, w_merge, queries, resp_kv)),
     )
 
 

time: 113 us -> 109 us (0.965)
  Pallas kernels: 109 us -> 103 us
    pallas_call x3 -> x1, Pallas kernels: 109 us -> 103 us  [per_device(): pl.pallas_call(functools.partial(whole_kernel, sizes, ctxs, mine, shard_r...]
    unnamed x19 -> x11, local copies, waits for them, and re-layouts: 2.67 us -> 4.42 us
where the time goes in v4:
time: 109 us; the launch traced here: 108 us
  Pallas kernels  103 us (94%)
  local copies, waits for them, and re-layouts  4.42 us (4%)
    pallas_call x1, Pallas kernels, per_device(): pl.pallas_call(functools.partial(whole_kernel, sizes, ctxs, mine, shard_r...  103 us
    unnamed x11, local copies, waits for them, and re-layouts  4.42 us

profile of v4, /device:TPU:0, one launch (start us, length us, event | category | flops | bytes accessed | tf_op | source)
XLA Modules:
  0.0 108.2 jit_solution(1608791895386951725)
XLA Ops:
  0.7 0.0 copy-start
  0.7 0.7 copy-done
  1.4 0.0 copy-start.1
  1.4 0.7 copy-done.1
  2.0 0.0 copy-start.2
  2.0 0.7 copy-done.2
  2.7 0.0 copy-start.3
  2.7 0.7 copy-done.3
  3.4 0.0 copy-start.4
  3.4 0.7 copy-done.4
  4.1 103.1 %shard_map.136 = bf16[128,4096]{1,0:T(8,128)(2,1)S(1)} custom-call(f32[1280]{0:T(1024)S(1)} %copy-done, f32[1,1024]{1,0:T(1,128)S(1)} %bitcast.2, f32[1280]{0:T(1024)S(1)} %copy-done.1, s32[4,256]{1,0:T(4,128)S(1)} %copy-done.3, s32[4,256]{1,0:T(4,128)S(1)} %copy-done.4, s32[1]{0:T(128)S(6)} %copy.16.refs_5_, bf16[128,1280]{1,0:T(8,128)(2,1)} %refs_6_.1, ...), custom_call_target="tpu_custom_call" | custom-call | tf_op jit(solution)/shard_map/pallas_call | solution.py:1189
  107.2 1.0 copy.17
Async XLA Ops:
  0.7 0.7 copy-start
  1.4 0.7 copy-start.1
  2.0 0.7 copy-start.2
  2.7 0.7 copy-start.3
  3.4 0.7 copy-start.4

commit v5 on v4

--- a/solution.py
+++ b/solution.py
@@ -39,7 +39,7 @@
 
 def front_kernel(sizes, *refs):
     (
-        patches_ref, gain_ref, tgain_ref, wqkv_hbm, text_hbm, wkv_hbm, greet,
+        patches_ref, gain_ref, tgain_ref, wqkv_hbm, text_hbm, wkv_hbm, greet, settle,
         qkv_ref, held, chain_last, mine_ref, mine_sq,
         wpad, text, wkv, normed, own, own_sq, pair_out, pair_in, chain_out, chain_in,
         load_sem, send_sem, recv_sem, near_send, near_recv, pair_sem, chain_send, chain_recv,
@@ -176,6 +176,7 @@
         own[d, s * SUBROWS : (s + 1) * SUBROWS, side * HD : (side + 1) * HD] = value
 
     own_sq[...] = jnp.zeros_like(own_sq)
+    settle()
     loads[0].wait()
     loads[1].wait()
     for v in range(vh):
@@ -1015,11 +1016,21 @@
 
 def whole_kernel(sizes, ctxs, mine, shard_rows, groups, *refs):
     (
-        vis_gain, tgain, merge_gain, dest, row, length,
+        length, vis_gain_hbm, tgain_hbm, merge_gain_hbm, dest_hbm, row_hbm,
         patches, w_out, w_qkv, text, w_kv, w_merge, queries, resp_kv, out,
     ) = refs[:15]
-    scratch = refs[15:]
+    vis_gain, tgain, merge_gain, dest, row, small_sem = refs[15:21]
+    scratch = refs[21:]
     first, second = groups
+    smalls = [
+        pltpu.make_async_copy(source, target, small_sem.at[i])
+        for i, (source, target) in enumerate(
+            [
+                (tgain_hbm, tgain), (vis_gain_hbm, vis_gain), (merge_gain_hbm, merge_gain),
+                (dest_hbm, dest), (row_hbm, row),
+            ]
+        )
+    ]
     front_refs, middle_refs = scratch[:first], scratch[first : first + second]
     tail_refs = scratch[first + second :]
     chips, vh = sizes[0] * sizes[1], sizes[1]
@@ -1041,13 +1052,19 @@
             pl.semaphore_signal(
                 barrier, inc=1, device_id={"ctx": other // vh, "vh": other % vh}, device_id_type=MESH
             )
+        for small in smalls:
+            small.start()
         pl.semaphore_wait(barrier, chips + planes - 1)
+
+    def settle():
+        for small in smalls:
+            small.wait()
 
     qkv, held, chain_last, sums, squares = front_refs[:5]
     wkv = front_refs[7]
     visual, share = middle_refs[:2]
     drains = [
-        front_kernel(sizes, patches, vis_gain, tgain, w_qkv, text, w_kv, greet, *front_refs),
+        front_kernel(sizes, patches, vis_gain, tgain, w_qkv, text, w_kv, greet, settle, *front_refs),
         middle_kernel(
             sizes, ctxs, qkv, w_out, merge_gain, chain_last, sums, squares, held, w_merge,
             *middle_refs
@@ -1180,6 +1197,8 @@
         DMA((chips, mine)),
         DMA((chips, mine)),
     ]
+    smalls = (vis_gain, kv_gain.reshape(1, -1), merge_gain, token_dest, token_row)
+    small_scratch = [V(item.shape, item.dtype) for item in smalls] + [DMA((len(smalls),))]
     room = sum(
         math.prod(item.shape) * item.dtype.itemsize
         for item in front_scratch + middle_scratch + tail_scratch
@@ -1189,14 +1208,15 @@
     return pl.pallas_call(
         functools.partial(whole_kernel, sizes, ctxs, mine, shard_rows, groups),
         out_shape=jax.ShapeDtypeStruct((resp, QH * HD), BF16),
-        in_specs=[VMEM] * 5 + [pl.BlockSpec(memory_space=pltpu.SMEM)] + [ANY] * 8,
+        in_specs=[pl.BlockSpec(memory_space=pltpu.SMEM)] + [ANY] * 13,
         out_specs=VMEM,
-        scratch_shapes=front_scratch + middle_scratch + tail_scratch,
+        scratch_shapes=small_scratch + front_scratch + middle_scratch + tail_scratch,
         compiler_params=pltpu.CompilerParams(
             collective_id=0, has_side_effects=True, vmem_limit_bytes=min(67_000_000, room + 6 * 2**20)
         ),
     )(
-        vis_gain, kv_gain.reshape(1, -1), merge_gain, token_dest, token_row, resp_len,
+        resp_len,
+        *map(in_hbm, smalls),
         *map(in_hbm, (patches, w_out, w_qkv.T, prompt_text, w_kv, w_merge, queries, resp_kv)),
     )
 

time: 109 us -> 105 us (0.963)
  local copies, waits for them, and re-layouts: 4.42 us -> 0.97 us
    unnamed x11 -> x1, local copies, waits for them, and re-layouts: 4.42 us -> 0.97 us
where the time goes in v5:
time: 105 us
  Pallas kernels  103 us (98%)
    pallas_call x1, Pallas kernels, per_device(): pl.pallas_call(functools.partial(whole_kernel, sizes, ctxs, mine, shard_r...  103 us

profile of v5, /device:TPU:0, one launch (start us, length us, event | category | flops | bytes accessed | tf_op | source)
XLA Modules:
  0.0 104.8 jit_solution(3351495601075370059)
XLA Ops:
  0.7 103.1 %shard_map.136 = bf16[128,4096]{1,0:T(8,128)(2,1)S(1)} custom-call(s32[1]{0:T(128)S(6)} %copy.16.refs_0_, f32[1280]{0:T(1024)} %refs_1_.1, f32[1,1024]{1,0:T(1,128)} %bitcast.3, f32[1280]{0:T(1024)} %refs_3_.1, s32[4,256]{1,0:T(4,128)} %refs_4_.1, s32[4,256]{1,0:T(4,128)} %refs_5_.1, bf16[128,1280]{1,0:T(8,128)(2,1)} %refs_6_.1, bf16[160,1280]{1,0:T(8,128)(2,1)} %refs_7_.1, ...), custom_call_target="tpu_custom_call" | custom-call | tf_op jit(solution)/shard_map/pallas_call | solution.py:1208
  103.8 1.0 copy.17
